TPU v7x, 32 devices: a whole 2x2x4 slice. The times are simulated.
32 devices in a mesh: rows: 8 (over z, y), cols: 4 (over x, core).
Axes of the slice: x: 2, y: 2, z: 4, core: 2. Of those that a mesh axis runs over, the one named last changes fastest.
Arguments:
- basis_cols: bfloat16 [32768, 1024], P('rows', 'cols'), may hold values from -6 to 6, as said below
- snapshots: bfloat16 [256, 32768], P(None, 'rows'), may hold values from -600 to 600
Outputs:
- coefficients: float32 [1024, 256], P('cols')
- factor: float32 [256, 256], replicated
- directions: bfloat16 [256, 32768], P(None, ('rows', 'cols'))
Inputs may be any that keep to these rules, and one draw needn't show every extreme that they name: `basis_cols`: normal entries.
All inputs are finite; a program needn't handle non-finite values.
Results may differ from a plain program's by a relative error of at most 0.0056.
Values may be sent and summed in bfloat16 or wider, within the bound.
No kernel may reach another device: no remote copies, remote signals or barrier semaphores. Data moves between devices by JAX's collectives and lax.ppermute only.
A program may use at most 64 MiB of HBM per device.

v0:
```python
import functools
import math

import jax
import jax.numpy as jnp
from jax import lax
from jax.experimental import pallas as pl
from jax.experimental.pallas import tpu as pltpu
from jax.sharding import PartitionSpec as P


RANK = 1024
LANES = 128
BLOCK = 32
SUB = 8


def swap(value, masks):
    count = lax.axis_size("rows") * lax.axis_size("cols")
    return lax.ppermute(value, ("rows", "cols"), [(i, i ^ masks[i % 2]) for i in range(count)])


def bits(count, step=1):
    found = []
    while count > 1:
        found.append(step)
        step, count = 2 * step, count // 2
    return found


def wide_split(value):
    high = value.astype(jnp.bfloat16)
    return high, (value - high.astype(jnp.float32)).astype(jnp.bfloat16)


def nt_dot(left, right):
    return lax.dot_general(left, right, (((1,), (1,)), ((), ())), preferred_element_type=jnp.float32)


def tn_dot(left, right):
    return lax.dot_general(left, right, (((0,), (0,)), ((), ())), preferred_element_type=jnp.float32)


def project_kernel(place_ref, basis_ref, snaps_ref, keep_ref, send_ref, *refs):
    count = (len(refs) - 2) // 2
    slab_refs, part_refs, basis_sem, snaps_sem = refs[:count], refs[count : 2 * count], refs[-2], refs[-1]
    points = slab_refs[0].shape[0]
    copies = []
    for offset in range(count):
        start = pl.multiple_of((place_ref[0] ^ offset) * points, points)
        span = pl.ds(start, points)
        copies.append(
            (
                pltpu.make_async_copy(basis_ref.at[span, :], slab_refs[offset], basis_sem.at[offset]),
                pltpu.make_async_copy(snaps_ref.at[:, span], part_refs[offset], snaps_sem.at[offset]),
            )
        )
    for pair in copies:
        for copy in pair:
            copy.start()
    total = None
    for offset in range(count):
        for copy in copies[offset]:
            copy.wait()
        value = jnp.dot(part_refs[offset][...], slab_refs[offset][...], preferred_element_type=jnp.float32)
        total = value if total is None else total + value
    half = total.shape[0] // 2
    odd = place_ref[1] == 1
    first, second = total[:half, :], total[half:, :]
    keep_ref[...] = jnp.where(odd, second, first)
    send_ref[...] = jnp.where(odd, first, second)


def recon_kernel(place_ref, *refs):
    count = (len(refs) - 1) // 2
    points = refs[count].shape[0]
    chunk = 256
    for start in range(0, points, chunk):
        cols = slice(start, start + chunk)
        recon = nt_dot(refs[0][...], refs[count][cols, :])
        for low_ref, basis_ref in zip(refs[1:count], refs[count + 1 : -1]):
            recon += nt_dot(low_ref[...], basis_ref[cols, :])
        refs[-1][:, cols] = recon


def packed_rows(tiles):
    return tiles // 2 * (LANES + 2 * SUB) + tiles * (tiles - 1) // 2 * LANES


def pack_layout(tiles):
    at, pairs, blocks = 0, [], []
    for first in range(0, tiles, 2):
        pairs.append((first, at, at + LANES))
        at += LANES + 2 * SUB
    for row in range(tiles):
        for col in range(row + 1, tiles):
            blocks.append((row, col, at))
            at += LANES
    return pairs, blocks


def square_iota(dim):
    return lax.broadcasted_iota(jnp.int32, (LANES, LANES), dim)


def residual_kernel(total_points, place_ref, *refs):
    count = (len(refs) - 7) // 2
    low_refs, basis_refs = refs[:count], refs[count : 2 * count]
    begun_ref, snaps_ref, high_ref, rest_ref, keep_ref, send_ref, pack_ref = refs[2 * count :]
    snaps, points = snaps_ref.shape
    chunk = 256
    for start in range(0, points, chunk):
        cols = slice(start, start + chunk)
        recon = begun_ref[:, cols]
        for low_ref, basis_ref in zip(low_refs, basis_refs):
            recon += nt_dot(low_ref[...], basis_ref[cols, :])
        residual = snaps_ref[:, cols].astype(jnp.float32) - recon * (1.0 / math.sqrt(RANK))
        high, rest = wide_split(residual)
        high_ref[:, cols] = high
        rest_ref[:, cols] = rest
    scale = 1.0 / total_points

    def block(row, col):
        rows, cols = pl.ds(row * LANES, LANES), pl.ds(col * LANES, LANES)
        value = nt_dot(high_ref[rows, :], high_ref[cols, :])
        value += nt_dot(high_ref[rows, :], rest_ref[cols, :]) + nt_dot(rest_ref[rows, :], high_ref[cols, :])
        return value * scale

    pairs, blocks = pack_layout(snaps // LANES)
    down, across = square_iota(0), square_iota(1)
    for first, at, line in pairs:
        upper, lower = block(first, first), block(first + 1, first + 1)
        pack_ref[pl.ds(at, LANES), :] = jnp.where(down <= across, upper, lower)
        diagonal = jnp.sum(jnp.where(down == across, lower, 0.0), axis=0, keepdims=True)
        pack_ref[pl.ds(line, 2 * SUB), :] = jnp.broadcast_to(diagonal, (2 * SUB, LANES))
    for row, col, at in blocks:
        pack_ref[pl.ds(at, LANES), :] = block(row, col)
    half = pack_ref.shape[0] // 2
    odd = place_ref[0] % 2 == 1
    first, second = pack_ref[pl.ds(0, half), :], pack_ref[pl.ds(half, half), :]
    keep_ref[...] = jnp.where(odd, second, first)
    send_ref[...] = jnp.where(odd, first, second)


def row_of(tile, index):
    return jnp.broadcast_to(tile[index : index + 1, :], tile.shape)


def eliminate(panel, offset):
    groups = BLOCK // SUB
    sub_iota = lax.broadcasted_iota(jnp.int32, (SUB, LANES), 0)
    columns = [
        [jnp.broadcast_to(panel[0][g][:, offset + j : offset + j + 1], (SUB, LANES)) for g in range(groups)]
        for j in range(BLOCK)
    ]
    scales = [jnp.zeros((SUB, LANES), jnp.float32) for _ in range(groups)]
    for p in range(BLOCK):
        home, line = divmod(p, SUB)
        pivot = row_of(columns[p][home], line)
        inverse = 1.0 / pivot
        scales[home] = jnp.where(sub_iota == line, lax.rsqrt(pivot), scales[home])
        factors = {}
        for g in range(home, groups):
            value = columns[p][g] * inverse
            if g == home:
                if line == SUB - 1:
                    continue
                value = jnp.where(sub_iota > line, value, 0.0)
            factors[g] = value
        for lanes in columns[p + 1 :] + panel:
            lead = row_of(lanes[home], line)
            for g, value in factors.items():
                lanes[g] = lanes[g] - value * lead
    return [[tile * scale for tile, scale in zip(lanes, scales)] for lanes in panel]


def three_way(value):
    first = value.astype(jnp.bfloat16)
    value = value - first.astype(jnp.float32)
    second = value.astype(jnp.bfloat16)
    third = (value - second.astype(jnp.float32)).astype(jnp.bfloat16)
    return first, second, third


def factor_kernel(place_ref, mine_ref, other_ref, high_ref, rest_ref, factor_ref, out_ref, a_ref, w_ref, pack_ref):
    size = factor_ref.shape[0]
    tiles = size // LANES
    half = mine_ref.shape[0]
    odd = place_ref[0] % 2 == 1
    pack_ref[pl.ds(0, half), :] = jnp.where(odd, other_ref[...], mine_ref[...])
    pack_ref[pl.ds(half, half), :] = jnp.where(odd, mine_ref[...], other_ref[...])
    pairs, blocks = pack_layout(tiles)
    down, across = square_iota(0), square_iota(1)

    def square(tile):
        return pl.ds(tile * LANES, LANES), pl.ds(tile * LANES, LANES)

    for first, at, line in pairs:
        folded = pack_ref[pl.ds(at, LANES), :]
        turned = folded.T
        a_ref[square(first)] = jnp.where(down <= across, folded, turned)
        diagonal = jnp.broadcast_to(pack_ref[pl.ds(line, 1), :], (LANES, LANES))
        value = jnp.where(down > across, folded, turned)
        a_ref[square(first + 1)] = jnp.where(down == across, diagonal, value)
    for row, col, at in blocks:
        a_ref[pl.ds(row * LANES, LANES), pl.ds(col * LANES, LANES)] = pack_ref[pl.ds(at, LANES), :]
    rows_iota = lax.broadcasted_iota(jnp.int32, (size, size), 0)
    cols_iota = lax.broadcasted_iota(jnp.int32, (size, size), 1)
    w_ref[...] = jnp.where(rows_iota == cols_iota, 1.0, 0.0)

    for base in range(0, size, BLOCK):
        tile, offset = divmod(base, LANES)
        a_tiles, w_tiles = range(tile, tiles), range(tile + 1)
        places = [(a_ref, t) for t in a_tiles] + [(w_ref, t) for t in w_tiles]
        panel = [
            [ref[pl.ds(base + g, SUB), pl.ds(t * LANES, LANES)] for g in range(0, BLOCK, SUB)] for ref, t in places
        ]
        panel = [jnp.concatenate(lanes, axis=0) for lanes in eliminate(panel, offset)]
        for (ref, t), value in zip(places, panel):
            ref[pl.ds(base, BLOCK), pl.ds(t * LANES, LANES)] = value
        after = base + BLOCK
        if after == size:
            break
        parts = [three_way(value) for value in panel]
        left = [jnp.concatenate([a, a, b, a, c, b], axis=0) for a, b, c in parts[: len(a_tiles)]]
        right = [jnp.concatenate([a, b, a, c, a, b], axis=0) for a, b, c in parts]
        for row_tile in a_tiles:
            skip = after - row_tile * LANES if after > row_tile * LANES else 0
            if skip == LANES:
                continue
            rows = pl.ds(row_tile * LANES + skip, LANES - skip)
            for (ref, t), value in zip(places, right):
                if ref is a_ref and t < row_tile:
                    continue
                update = tn_dot(left[row_tile - tile], value)
                lanes = pl.ds(t * LANES, LANES)
                ref[rows, lanes] = ref[rows, lanes] - update[skip:, :]

    lower = rows_iota[:LANES, :LANES] >= cols_iota[:LANES, :LANES]
    for row in range(tiles):
        for col in range(tiles):
            into = (pl.ds(row * LANES, LANES), pl.ds(col * LANES, LANES))
            if row < col:
                factor_ref[into] = jnp.zeros((LANES, LANES), jnp.float32)
                continue
            block = a_ref[pl.ds(col * LANES, LANES), pl.ds(row * LANES, LANES)].T
            factor_ref[into] = jnp.where(lower, block, 0.0) if row == col else block
    chunk = 256
    for row in range(tiles):
        depth = (row + 1) * LANES
        rows = pl.ds(row * LANES, LANES)
        high, rest = wide_split(w_ref[rows, pl.ds(0, depth)])
        for start in range(0, out_ref.shape[1], chunk):
            cols = pl.ds(start, chunk)
            right_high, right_rest = high_ref[pl.ds(0, depth), cols], rest_ref[pl.ds(0, depth), cols]
            value = jnp.dot(high, right_high, preferred_element_type=jnp.float32)
            value += jnp.dot(high, right_rest, preferred_element_type=jnp.float32)
            value += jnp.dot(rest, right_high, preferred_element_type=jnp.float32)
            out_ref[rows, cols] = value.astype(jnp.bfloat16)


def call(kernel, outs, scratch, flops, grant, whole=0):
    vmem = pl.BlockSpec(memory_space=pltpu.VMEM)
    smem = pl.BlockSpec(memory_space=pltpu.SMEM)
    anywhere = pl.BlockSpec(memory_space=pl.ANY)

    def run(scalar, *args):
        size = sum(math.prod(x.shape) * x.dtype.itemsize for x in (*args, *outs))
        return pl.pallas_call(
            kernel,
            out_shape=outs,
            in_specs=[smem] + [anywhere] * whole + [vmem] * (len(args) - whole),
            out_specs=[vmem] * len(outs),
            scratch_shapes=scratch,
            compiler_params=pltpu.CompilerParams(vmem_limit_bytes=grant << 20),
            cost_estimate=pl.CostEstimate(flops=flops, bytes_accessed=size, transcendentals=0),
        )(scalar, *args)

    return run


def shape(dtype, *dims):
    return jax.ShapeDtypeStruct(dims, dtype)


def compute(basis_cols, snapshots):
    snaps, row_points = snapshots.shape
    modes = basis_cols.shape[1]
    row_index, column_index = lax.axis_index("rows"), lax.axis_index("cols")
    row_count, columns = lax.axis_size("rows"), lax.axis_size("cols")
    total_points = row_points * row_count
    points = row_points // columns
    half = snaps // 2
    bf16, f32 = jnp.bfloat16, jnp.float32

    row_bits = bits(row_count, columns)
    sum_steps = list(zip(row_bits, row_bits[1:] + row_bits[:1]))
    flat = row_index * columns + column_index
    odd = (flat // jnp.where(column_index % 2 == 0, sum_steps[0][0], sum_steps[0][1])) % 2
    place = jnp.stack([column_index, odd]).astype(jnp.int32)

    kept, sent, *slabs = call(
        project_kernel,
        (shape(f32, half, modes),) * 2 + (shape(bf16, points, modes),) * columns + (shape(bf16, snaps, points),),
        [pltpu.VMEM((snaps, points), bf16)] * (columns - 1)
        + [pltpu.SemaphoreType.DMA((columns,)), pltpu.SemaphoreType.DMA((columns,))],
        2 * snaps * row_points * modes,
        16,
        2,
    )(place, basis_cols, snapshots)
    own_snaps = slabs.pop()
    for offset in reversed(range(1, columns)):
        slabs[offset] = swap(slabs[offset], (offset, offset))

    arrived = swap(sent, sum_steps[0])
    kept = kept + arrived
    for step in sum_steps[1:]:
        kept = kept + swap(kept, step)
    low = (kept * (math.sqrt(RANK) / total_points)).astype(bf16)
    other = swap(low, sum_steps[0])
    low = jnp.where(odd == 1, jnp.concatenate([other, low], 0), jnp.concatenate([low, other], 0))
    coefficients = low.astype(f32).T
    lows = {0: low}
    near = swap(low, (1, 1))
    for offset in reversed(bits(columns // 2, 2)):
        lows.update({key ^ offset: swap(value, (offset, offset)) for key, value in list(lows.items())})
    lows.update({key ^ 1: near if key == 0 else swap(value, (1, 1)) for key, value in list(lows.items())})

    (begun,) = call(recon_kernel, (shape(f32, snaps, points),), [], 4 * snaps * points * modes, 8)(
        place, lows[0], lows[1], slabs[0], slabs[1]
    )
    packed = packed_rows(snaps // LANES)
    part = shape(f32, packed // 2, LANES)
    wide = shape(bf16, snaps, points)
    high, rest, keep, send = call(
        functools.partial(residual_kernel, total_points),
        (wide, wide, part, part),
        [pltpu.VMEM((packed, LANES), f32)],
        2 * snaps * points * (modes * (columns - 2) + 3 * snaps),
        16,
    )(place, *[lows[offset] for offset in range(2, columns)], *slabs[2:], begun, own_snaps)
    keep = keep + swap(send, (1, 1))
    rest_bits = bits(columns // 2, 2) + row_bits
    first_order = rest_bits[-1:] + rest_bits[:-1]
    second_order = list(first_order)
    for at in range(0, len(first_order) - 1, 2):
        second_order[at : at + 2] = reversed(first_order[at : at + 2])
    for step in zip(first_order, second_order):
        keep = keep + swap(keep, step)
    rest_of_gram = swap(keep, (1, 1))
    factor, directions = call(
        factor_kernel,
        (shape(f32, snaps, snaps), wide),
        [pltpu.VMEM((snaps, snaps), f32)] * 2 + [pltpu.VMEM((packed, LANES), f32)],
        6 * snaps * snaps * points,
        16,
    )(place, keep, rest_of_gram, high, rest)
    return (coefficients, factor, directions)


def solution(mesh):
    placed = (P("rows", "cols"), P(None, "rows"))
    return jax.shard_map(
        compute,
        mesh=mesh,
        in_specs=placed,
        out_specs=(P("cols", None), P(), P(None, ("rows", "cols"))),
        check_vma=False,
    )
```

profile of v0, /device:TPU:0, one launch (start us, length us, event | category | flops | bytes accessed | tf_op | source)
XLA Modules:
  0.0 85.6 jit_solution(13291868685594382755)
XLA Ops:
  0.7 0.1 pad_add_fusion.place_ref
  0.8 1.6 %copy-done = bf16[4096,256]{1,0:T(8,128)(2,1)S(1)} copy-done((bf16[4096,256]{1,0:T(8,128)(2,1)S(1)}, bf16[4096,256]{1,0:T(8,128)(2,1)}, u32[]{:S(2)}) %copy-start) | copy-done | bytes 2097176
  2.4 1.6 %copy-done.1 = bf16[256,4096]{1,0:T(8,128)(2,1)S(1)} copy-done((bf16[256,4096]{1,0:T(8,128)(2,1)S(1)}, bf16[256,4096]{1,0:T(8,128)(2,1)}, u32[]{:S(2)}) %copy-start.1) | copy-done | bytes 2097176
  3.9 3.0 %shard_map.49 = (f32[128,256]{1,0:T(8,128)S(1)}, f32[128,256]{1,0:T(8,128)S(1)}, bf16[1024,256]{1,0:T(8,128)(2,1)S(1)}, bf16[1024,256]{1,0:T(8,128)(2,1)}, bf16[...) custom-call(s32[2]{0:T(128)S(1)} %pad_add_fusion.place_ref, ...), custom_call_target="tpu_custom_call" | custom-call | flops 536870912 | bytes 7077888 | tf_op jit(solution)/shard_map/pallas_call | solution.py:269
  7.0 3.1 %collective-permute-start = (f32[128,256]{1,0:T(8,128)S(1)}, f32[128,256]{1,0:T(8,128)S(1)}, u32[]{:S(2)}, u32[]{:S(2)}) collective-permute-start(f32[128,256]{1,0:T(8,128)S(1)} %get-tuple-element.17), channel_id=1, source_target_pairs={{0,4},{1,9},{2,6},{3,11},{4,0},{5,13},{6,2},{7,15},{8,12},{9,1},{1... | collective-permute-start | bytes 393224 | tf_op jit(solution)/shard_map/ppermute | solution.py:20
  10.0 2.9 %collective-permute-done = f32[128,256]{1,0:T(8,128)S(1)} collective-permute-done((f32[128,256]{1,0:T(8,128)S(1)}, f32[128,256]{1,0:T(8,128)S(1)}, u32[]{:S(2)}, u32[]{:S(2)}) %collective-permute-start) | collective-permute-done | bytes 131104 | tf_op jit(solution)/shard_map/ppermute | solution.py:20
  13.0 2.1 %collective-permute-start.1 = (f32[128,256]{1,0:T(8,128)S(1)}, f32[128,256]{1,0:T(8,128)S(1)}, u32[]{:S(2)}, u32[]{:S(2)}) collective-permute-start(f32[128,256]{1,0:T(8,128)S(1)} %add.38), channel_id=1, source_target_pairs={{0,8},{1,17},{2,10},{3,19},{4,12},{5,21},{6,14},{7,23},{8,0},{9,25... | collective-permute-start | bytes 393224 | tf_op jit(solution)/shard_map/ppermute | solution.py:20
  15.1 3.4 %collective-permute-done.1 = f32[128,256]{1,0:T(8,128)S(1)} collective-permute-done((f32[128,256]{1,0:T(8,128)S(1)}, f32[128,256]{1,0:T(8,128)S(1)}, u32[]{:S(2)}, u32[]{:S(2)}) %collective-permute-start.1) | collective-permute-done | bytes 131104 | tf_op jit(solution)/shard_map/ppermute | solution.py:20
  18.6 3.0 %collective-permute-start.2 = (f32[128,256]{1,0:T(8,128)S(1)}, f32[128,256]{1,0:T(8,128)S(1)}, u32[]{:S(2)}, u32[]{:S(2)}) collective-permute-start(f32[128,256]{1,0:T(8,128)S(1)} %add.39), channel_id=1, source_target_pairs={{0,16},{1,5},{2,18},{3,7},{4,20},{5,1},{6,22},{7,3},{8,24},{9,13},... | collective-permute-start | bytes 393224 | tf_op jit(solution)/shard_map/ppermute | solution.py:20
  21.6 1.5 %collective-permute-start.6 = (bf16[1024,256]{1,0:T(8,128)(2,1)}, bf16[1024,256]{1,0:T(8,128)(2,1)S(1)}, u32[]{:S(2)}, u32[]{:S(2)}) collective-permute-start(bf16[1024,256]{1,0:T(8,128)(2,1)} %get-tuple-element.18), channel_id=1, source_target_pairs={{0,2},{1,3},{2,0},{3,1},{4,6},{5,7},{6,4},{7,5},{8,10},{9,11},{10,... | collective-permute-start | bytes 1572872 | tf_op jit(solution)/shard_map/ppermute | solution.py:20
  23.1 0.4 collective-permute-start.7
  23.4 1.1 %collective-permute-done.2 = f32[128,256]{1,0:T(8,128)S(1)} collective-permute-done((f32[128,256]{1,0:T(8,128)S(1)}, f32[128,256]{1,0:T(8,128)S(1)}, u32[]{:S(2)}, u32[]{:S(2)}) %collective-permute-start.2) | collective-permute-done | bytes 131104 | tf_op jit(solution)/shard_map/ppermute | solution.py:20
  24.6 1.6 %collective-permute-start.3 = (bf16[128,256]{1,0:T(8,128)(2,1)S(1)}, bf16[128,256]{1,0:T(8,128)(2,1)S(1)}, u32[]{:S(2)}, u32[]{:S(2)}) collective-permute-start(bf16[128,256]{1,0:T(8,128)(2,1)S(1)} %multiply_convert_fusion), channel_id=1, source_target_pairs={{0,4},{1,9},{2,6},{3,11},{4,0},{5,13},{6,2},{7,15},{8,12},{9,1},{1... | collective-permute-start | bytes 196616 | tf_op jit(solution)/shard_map/ppermute | solution.py:20
  26.1 2.7 %collective-permute-done.3 = bf16[128,256]{1,0:T(8,128)(2,1)S(1)} collective-permute-done((bf16[128,256]{1,0:T(8,128)(2,1)S(1)}, bf16[128,256]{1,0:T(8,128)(2,1)S(1)}, u32[]{:S(2)}, u32[]{:S(2)}) %collective-permute-start.3) | collective-permute-done | bytes 65568 | tf_op jit(solution)/shard_map/ppermute | solution.py:20
  28.9 1.6 %collective-permute-start.4 = (bf16[256,256]{1,0:T(8,128)(2,1)S(1)}, bf16[256,256]{1,0:T(8,128)(2,1)S(1)}, u32[]{:S(2)}, u32[]{:S(2)}) collective-permute-start(bf16[256,256]{1,0:T(8,128)(2,1)S(1)} %get-tuple-element.33.refs_0_), channel_id=1, source_target_pairs={{0,2},{1,3},{2,0},{3,1},{4,6},{5,7},{6,4},{7,5},{8,10},{9,11},{10,... | collective-permute-start | bytes 393224 | tf_op jit(solution)/shard_map/ppermute | solution.py:20
  30.5 19.7 %collective-permute-done.4.refs_0_ = bf16[256,256]{1,0:T(8,128)(2,1)S(1)} collective-permute-done((bf16[256,256]{1,0:T(8,128)(2,1)S(1)}, bf16[256,256]{1,0:T(8,128)(2,1)S(1)}, u32[]{:S(2)}, u32[]{:S(2)}) %collective-permute-start.4) | collective-permute-done | bytes 131104 | tf_op jit(solution)/shard_map/ppermute | solution.py:20
  50.2 1.0 %shard_map.50.refs_4_ = f32[256,1024]{1,0:T(8,128)S(1)} custom-call(s32[2]{0:T(128)S(1)} %pad_add_fusion.place_ref, bf16[256,256]{1,0:T(8,128)(2,1)S(1)} %get-tuple-element.33.refs_0_, bf16[256,256]{1,0:T(8,128)(2,1)S(1)} %collective-permute-done.8.refs_1_, bf16[1024,256]{1,0:T(8,128)(2,1)S(1)} %get-tuple-element.20.refs_2_, ...), custom_call_target="tpu_custom_call" | custom-call | flops 268435456 | bytes 2359296 | tf_op jit(solution)/shard_map/pallas_call | solution.py:269
  51.2 0.3 collective-permute-done.5.refs_1_
  51.5 2.1 %shard_map.51 = (bf16[256,1024]{1,0:T(8,128)(2,1)S(1)}, bf16[256,1024]{1,0:T(8,128)(2,1)S(1)}, f32[136,128]{1,0:T(8,128)S(1)}, f32[136,128]{1,0:T(8,128)S(1)}) custom-call(s32[2]{0:T(128)S(1)} %pad_add_fusion.place_ref, bf16[256,256]{1,0:T(8,128)(2,1)S(1)} %collective-permute-done.4.refs_0_, bf16[256,256]{1,0:T(8,128)(2,1)S(1)} %collective-permute-done.5.refs_1_, ...), custom_call_target="tpu_custom_call" | custom-call | flops 671088640 | bytes 4071424 | tf_op jit(solution)/shard_map/pallas_call | solution.py:269
  53.6 0.3 collective-permute-start.10
  53.9 1.0 %collective-permute-done.10 = f32[136,128]{1,0:T(8,128)S(1)} collective-permute-done((f32[136,128]{1,0:T(8,128)S(1)}, f32[136,128]{1,0:T(8,128)S(1)}, u32[]{:S(2)}, u32[]{:S(2)}) %collective-permute-start.10) | collective-permute-done | bytes 69664 | tf_op jit(solution)/shard_map/ppermute | solution.py:20
  55.0 0.1 collective-permute-start.11
  55.1 5.1 %collective-permute-done.11 = f32[136,128]{1,0:T(8,128)S(1)} collective-permute-done((f32[136,128]{1,0:T(8,128)S(1)}, f32[136,128]{1,0:T(8,128)S(1)}, u32[]{:S(2)}, u32[]{:S(2)}) %collective-permute-start.11) | collective-permute-done | bytes 69664 | tf_op jit(solution)/shard_map/ppermute | solution.py:20
  60.2 1.6 %collective-permute-start.12 = (f32[136,128]{1,0:T(8,128)S(1)}, f32[136,128]{1,0:T(8,128)S(1)}, u32[]{:S(2)}, u32[]{:S(2)}) collective-permute-start(f32[136,128]{1,0:T(8,128)S(1)} %add.42), channel_id=1, source_target_pairs={{0,2},{1,17},{2,0},{3,19},{4,6},{5,21},{6,4},{7,23},{8,10},{9,25},... | collective-permute-start | bytes 208904 | tf_op jit(solution)/shard_map/ppermute | solution.py:20
  61.8 2.8 %collective-permute-done.12 = f32[136,128]{1,0:T(8,128)S(1)} collective-permute-done((f32[136,128]{1,0:T(8,128)S(1)}, f32[136,128]{1,0:T(8,128)S(1)}, u32[]{:S(2)}, u32[]{:S(2)}) %collective-permute-start.12) | collective-permute-done | bytes 69664 | tf_op jit(solution)/shard_map/ppermute | solution.py:20
  64.6 1.6 %collective-permute-start.13 = (f32[136,128]{1,0:T(8,128)S(1)}, f32[136,128]{1,0:T(8,128)S(1)}, u32[]{:S(2)}, u32[]{:S(2)}) collective-permute-start(f32[136,128]{1,0:T(8,128)S(1)} %add.43), channel_id=1, source_target_pairs={{0,4},{1,9},{2,6},{3,11},{4,0},{5,13},{6,2},{7,15},{8,12},{9,1},{1... | collective-permute-start | bytes 208904 | tf_op jit(solution)/shard_map/ppermute | solution.py:20
  66.2 2.8 %collective-permute-done.13 = f32[136,128]{1,0:T(8,128)S(1)} collective-permute-done((f32[136,128]{1,0:T(8,128)S(1)}, f32[136,128]{1,0:T(8,128)S(1)}, u32[]{:S(2)}, u32[]{:S(2)}) %collective-permute-start.13) | collective-permute-done | bytes 69664 | tf_op jit(solution)/shard_map/ppermute | solution.py:20
  69.0 3.1 %collective-permute-start.14 = (f32[136,128]{1,0:T(8,128)S(1)}, f32[136,128]{1,0:T(8,128)S(1)}, u32[]{:S(2)}, u32[]{:S(2)}) collective-permute-start(f32[136,128]{1,0:T(8,128)S(1)} %add.44), channel_id=1, source_target_pairs={{0,8},{1,5},{2,10},{3,7},{4,12},{5,1},{6,14},{7,3},{8,0},{9,13},{1... | collective-permute-start | bytes 208904 | tf_op jit(solution)/shard_map/ppermute | solution.py:20
  72.2 2.3 %collective-permute-done.14 = f32[136,128]{1,0:T(8,128)S(1)} collective-permute-done((f32[136,128]{1,0:T(8,128)S(1)}, f32[136,128]{1,0:T(8,128)S(1)}, u32[]{:S(2)}, u32[]{:S(2)}) %collective-permute-start.14) | collective-permute-done | bytes 69664 | tf_op jit(solution)/shard_map/ppermute | solution.py:20
  74.5 0.8 copy.5
  75.4 0.4 collective-permute-done.15.other_ref
  75.8 9.8 %shard_map.52 = (f32[256,256]{1,0:T(8,128)}, bf16[256,1024]{1,0:T(8,128)(2,1)}) custom-call(s32[2]{0:T(128)S(1)} %pad_add_fusion.place_ref, f32[136,128]{1,0:T(8,128)S(1)} %add.45.mine_ref, f32[136,128]{1,0:T(8,128)S(1)} %collective-permute-done.15.other_ref, bf16[256,1024]{1,0:T(8,128)(2,1)S(1)} %get-tuple-element.25.high_ref, ...), custom_call_target="tpu_custom_call" | custom-call | flops 402653184 | bytes 1974272 | tf_op jit(solution)/shard_map/pallas_call | solution.py:269
  (19 shorter events, 0.2 us)
Async XLA Ops:
  0.8 1.6 %copy-start = (bf16[4096,256]{1,0:T(8,128)(2,1)S(1)}, bf16[4096,256]{1,0:T(8,128)(2,1)}, u32[]{:S(2)}) copy-start(bf16[4096,256]{1,0:T(8,128)(2,1)} %basis_ref.1) | copy-start | bytes 6291460
  2.4 1.6 %copy-start.1 = (bf16[256,4096]{1,0:T(8,128)(2,1)S(1)}, bf16[256,4096]{1,0:T(8,128)(2,1)}, u32[]{:S(2)}) copy-start(bf16[256,4096]{1,0:T(8,128)(2,1)} %snaps_ref.1) | copy-start | bytes 6291460
  7.0 6.0 %collective-permute-start = (f32[128,256]{1,0:T(8,128)S(1)}, f32[128,256]{1,0:T(8,128)S(1)}, u32[]{:S(2)}, u32[]{:S(2)}) collective-permute-start(f32[128,256]{1,0:T(8,128)S(1)} %get-tuple-element.17), channel_id=1, source_target_pairs={{0,4},{1,9},{2,6},{3,11},{4,0},{5,13},{6,2},{7,15},{8,12},{9,1},{1... | collective-permute-start | bytes 393224 | tf_op jit(solution)/shard_map/ppermute | solution.py:20
  13.0 5.6 %collective-permute-start.1 = (f32[128,256]{1,0:T(8,128)S(1)}, f32[128,256]{1,0:T(8,128)S(1)}, u32[]{:S(2)}, u32[]{:S(2)}) collective-permute-start(f32[128,256]{1,0:T(8,128)S(1)} %add.38), channel_id=1, source_target_pairs={{0,8},{1,17},{2,10},{3,19},{4,12},{5,21},{6,14},{7,23},{8,0},{9,25... | collective-permute-start | bytes 393224 | tf_op jit(solution)/shard_map/ppermute | solution.py:20
  18.6 6.0 %collective-permute-start.2 = (f32[128,256]{1,0:T(8,128)S(1)}, f32[128,256]{1,0:T(8,128)S(1)}, u32[]{:S(2)}, u32[]{:S(2)}) collective-permute-start(f32[128,256]{1,0:T(8,128)S(1)} %add.39), channel_id=1, source_target_pairs={{0,16},{1,5},{2,18},{3,7},{4,20},{5,1},{6,22},{7,3},{8,24},{9,13},... | collective-permute-start | bytes 393224 | tf_op jit(solution)/shard_map/ppermute | solution.py:20
  21.6 28.6 %collective-permute-start.9 = (bf16[1024,256]{1,0:T(8,128)(2,1)}, bf16[1024,256]{1,0:T(8,128)(2,1)S(1)}, u32[]{:S(2)}, u32[]{:S(2)}) collective-permute-start(bf16[1024,256]{1,0:T(8,128)(2,1)} %get-tuple-element.21), channel_id=1, source_target_pairs={{0,1},{1,0},{2,3},{3,2},{4,5},{5,4},{6,7},{7,6},{8,9},{9,8},{10,11... | collective-permute-start | bytes 1572872 | tf_op jit(solution)/shard_map/ppermute | solution.py:20
  21.6 29.6 %collective-permute-start.6 = (bf16[1024,256]{1,0:T(8,128)(2,1)}, bf16[1024,256]{1,0:T(8,128)(2,1)S(1)}, u32[]{:S(2)}, u32[]{:S(2)}) collective-permute-start(bf16[1024,256]{1,0:T(8,128)(2,1)} %get-tuple-element.18), channel_id=1, source_target_pairs={{0,2},{1,3},{2,0},{3,1},{4,6},{5,7},{6,4},{7,5},{8,10},{9,11},{10,... | collective-permute-start | bytes 1572872 | tf_op jit(solution)/shard_map/ppermute | solution.py:20
  23.1 28.1 %collective-permute-start.7 = (bf16[1024,256]{1,0:T(8,128)(2,1)S(1)}, bf16[1024,256]{1,0:T(8,128)(2,1)S(1)}, u32[]{:S(2)}, u32[]{:S(2)}) collective-permute-start(bf16[1024,256]{1,0:T(8,128)(2,1)S(1)} %get-tuple-element.19), channel_id=1, source_target_pairs={{0,3},{1,2},{2,1},{3,0},{4,7},{5,6},{6,5},{7,4},{8,11},{9,10},{10,... | collective-permute-start | bytes 1572872 | tf_op jit(solution)/shard_map/ppermute | solution.py:20
  24.6 4.3 %collective-permute-start.3 = (bf16[128,256]{1,0:T(8,128)(2,1)S(1)}, bf16[128,256]{1,0:T(8,128)(2,1)S(1)}, u32[]{:S(2)}, u32[]{:S(2)}) collective-permute-start(bf16[128,256]{1,0:T(8,128)(2,1)S(1)} %multiply_convert_fusion), channel_id=1, source_target_pairs={{0,4},{1,9},{2,6},{3,11},{4,0},{5,13},{6,2},{7,15},{8,12},{9,1},{1... | collective-permute-start | bytes 196616 | tf_op jit(solution)/shard_map/ppermute | solution.py:20
  28.9 21.3 %collective-permute-start.4 = (bf16[256,256]{1,0:T(8,128)(2,1)S(1)}, bf16[256,256]{1,0:T(8,128)(2,1)S(1)}, u32[]{:S(2)}, u32[]{:S(2)}) collective-permute-start(bf16[256,256]{1,0:T(8,128)(2,1)S(1)} %get-tuple-element.33.refs_0_), channel_id=1, source_target_pairs={{0,2},{1,3},{2,0},{3,1},{4,6},{5,7},{6,4},{7,5},{8,10},{9,11},{10,... | collective-permute-start | bytes 393224 | tf_op jit(solution)/shard_map/ppermute | solution.py:20
  30.5 19.7 %collective-permute-start.8 = (bf16[256,256]{1,0:T(8,128)(2,1)S(1)}, bf16[256,256]{1,0:T(8,128)(2,1)S(1)}, u32[]{:S(2)}, u32[]{:S(2)}) collective-permute-start(bf16[256,256]{1,0:T(8,128)(2,1)S(1)} %get-tuple-element.33.refs_0_), channel_id=1, source_target_pairs={{0,1},{1,0},{2,3},{3,2},{4,5},{5,4},{6,7},{7,6},{8,9},{9,8},{10,11... | collective-permute-start | bytes 393224 | tf_op jit(solution)/shard_map/ppermute | solution.py:20
  50.2 1.3 %collective-permute-start.5 = (bf16[256,256]{1,0:T(8,128)(2,1)S(1)}, bf16[256,256]{1,0:T(8,128)(2,1)S(1)}, u32[]{:S(2)}, u32[]{:S(2)}) collective-permute-start(bf16[256,256]{1,0:T(8,128)(2,1)S(1)} %collective-permute-done.4.refs_0_), channel_id=1, source_target_pairs={{0,1},{1,0},{2,3},{3,2},{4,5},{5,4},{6,7},{7,6},{8,9},{9,8},{10,11... | collective-permute-start | bytes 393224 | tf_op jit(solution)/shard_map/ppermute | solution.py:20
  53.6 1.3 %collective-permute-start.10 = (f32[136,128]{1,0:T(8,128)S(1)}, f32[136,128]{1,0:T(8,128)S(1)}, u32[]{:S(2)}, u32[]{:S(2)}) collective-permute-start(f32[136,128]{1,0:T(8,128)S(1)} %get-tuple-element.24), channel_id=1, source_target_pairs={{0,1},{1,0},{2,3},{3,2},{4,5},{5,4},{6,7},{7,6},{8,9},{9,8},{10,11... | collective-permute-start | bytes 208904 | tf_op jit(solution)/shard_map/ppermute | solution.py:20
  55.0 5.3 %collective-permute-start.11 = (f32[136,128]{1,0:T(8,128)S(1)}, f32[136,128]{1,0:T(8,128)S(1)}, u32[]{:S(2)}, u32[]{:S(2)}) collective-permute-start(f32[136,128]{1,0:T(8,128)S(1)} %add.41), channel_id=1, source_target_pairs={{0,16},{1,3},{2,18},{3,1},{4,20},{5,7},{6,22},{7,5},{8,24},{9,11},... | collective-permute-start | bytes 208904 | tf_op jit(solution)/shard_map/ppermute | solution.py:20
  60.2 4.4 %collective-permute-start.12 = (f32[136,128]{1,0:T(8,128)S(1)}, f32[136,128]{1,0:T(8,128)S(1)}, u32[]{:S(2)}, u32[]{:S(2)}) collective-permute-start(f32[136,128]{1,0:T(8,128)S(1)} %add.42), channel_id=1, source_target_pairs={{0,2},{1,17},{2,0},{3,19},{4,6},{5,21},{6,4},{7,23},{8,10},{9,25},... | collective-permute-start | bytes 208904 | tf_op jit(solution)/shard_map/ppermute | solution.py:20
  64.6 4.4 %collective-permute-start.13 = (f32[136,128]{1,0:T(8,128)S(1)}, f32[136,128]{1,0:T(8,128)S(1)}, u32[]{:S(2)}, u32[]{:S(2)}) collective-permute-start(f32[136,128]{1,0:T(8,128)S(1)} %add.43), channel_id=1, source_target_pairs={{0,4},{1,9},{2,6},{3,11},{4,0},{5,13},{6,2},{7,15},{8,12},{9,1},{1... | collective-permute-start | bytes 208904 | tf_op jit(solution)/shard_map/ppermute | solution.py:20
  69.0 5.4 %collective-permute-start.14 = (f32[136,128]{1,0:T(8,128)S(1)}, f32[136,128]{1,0:T(8,128)S(1)}, u32[]{:S(2)}, u32[]{:S(2)}) collective-permute-start(f32[136,128]{1,0:T(8,128)S(1)} %add.44), channel_id=1, source_target_pairs={{0,8},{1,5},{2,10},{3,7},{4,12},{5,1},{6,14},{7,3},{8,0},{9,13},{1... | collective-permute-start | bytes 208904 | tf_op jit(solution)/shard_map/ppermute | solution.py:20
  74.5 1.3 %collective-permute-start.15 = (f32[136,128]{1,0:T(8,128)S(1)}, f32[136,128]{1,0:T(8,128)S(1)}, u32[]{:S(2)}, u32[]{:S(2)}) collective-permute-start(f32[136,128]{1,0:T(8,128)S(1)} %add.45.mine_ref), channel_id=1, source_target_pairs={{0,1},{1,0},{2,3},{3,2},{4,5},{5,4},{6,7},{7,6},{8,9},{9,8},{10,11... | collective-permute-start | bytes 208904 | tf_op jit(solution)/shard_map/ppermute | solution.py:20
where the time goes:
time: 85.8 us; the launch traced here: 85.6 us
  waiting for transfers between devices  44.7 us (52%)
  starting transfers between devices  20 us (23%)
  Pallas kernels  15.9 us (19%)
  local copies, waits for them, and re-layouts  4.02 us (5%)
    ppermute x16, waiting for transfers between devices, swap(): lax.ppermute(value, ('rows', 'cols'), [(i, i ^ masks[i % 2]) for i in ran...  44.7 us
    ppermute x16, starting transfers between devices, swap(): lax.ppermute(value, ('rows', 'cols'), [(i, i ^ masks[i % 2]) for i in ran...  20 us
    pallas_call x4, Pallas kernels, run(): pl.pallas_call(kernel, out_shape=outs, in_specs=[smem] + [anywhere] * who...  15.9 us
    unnamed x5, local copies, waits for them, and re-layouts  4.02 us
  transfers between devices with their start and end apart: 16, of which 12 were waited for; matrix products, arithmetic and copies ran while one was open for 1% of the time, Pallas kernels for 1%

commit v1 on v0

--- a/solution.py
+++ b/solution.py
@@ -11,7 +11,8 @@
 
 RANK = 1024
 LANES = 128
-BLOCK = 32
+BLOCK = 64
+STEP = 16
 SUB = 8
 
 
@@ -41,27 +42,40 @@
     return lax.dot_general(left, right, (((0,), (0,)), ((), ())), preferred_element_type=jnp.float32)
 
 
-def project_kernel(place_ref, basis_ref, snaps_ref, keep_ref, send_ref, *refs):
-    count = (len(refs) - 2) // 2
-    slab_refs, part_refs, basis_sem, snaps_sem = refs[:count], refs[count : 2 * count], refs[-2], refs[-1]
-    points = slab_refs[0].shape[0]
+def slab_copies(place_ref, whole_ref, into_refs, sem_ref, first, by_rows):
     copies = []
-    for offset in range(count):
-        start = pl.multiple_of((place_ref[0] ^ offset) * points, points)
-        span = pl.ds(start, points)
-        copies.append(
-            (
-                pltpu.make_async_copy(basis_ref.at[span, :], slab_refs[offset], basis_sem.at[offset]),
-                pltpu.make_async_copy(snaps_ref.at[:, span], part_refs[offset], snaps_sem.at[offset]),
-            )
-        )
-    for pair in copies:
-        for copy in pair:
-            copy.start()
+    for index, into_ref in enumerate(into_refs):
+        size = into_ref.shape[0 if by_rows else 1]
+        start = pl.multiple_of((place_ref[0] ^ (first + index)) * size, size)
+        span = whole_ref.at[pl.ds(start, size), :] if by_rows else whole_ref.at[:, pl.ds(start, size)]
+        copies.append(pltpu.make_async_copy(span, into_ref, sem_ref.at[index]))
+    return copies
+
+
+def slab_kernel(place_ref, basis_ref, *refs):
+    copies = slab_copies(place_ref, basis_ref, refs[:-1], refs[-1], 2, True)
+    for copy in copies:
+        copy.start()
+    for copy in copies:
+        copy.wait()
+
+
+def project_kernel(place_ref, basis_ref, snaps_ref, *refs):
+    count = (len(refs) - 3) // 2
+    far_refs = refs[: count - 2]
+    keep_ref, send_ref, own_ref, near_ref = refs[count - 2 : count + 2]
+    part_refs, basis_sem, snaps_sem = refs[count + 2 : -2], refs[-2], refs[-1]
+    basis_copies = slab_copies(place_ref, basis_ref, (own_ref, near_ref), basis_sem, 0, True)
+    snaps_copies = slab_copies(place_ref, snaps_ref, part_refs, snaps_sem, 0, False)
+    for copy in snaps_copies[2:] + basis_copies + snaps_copies[:2]:
+        copy.start()
     total = None
-    for offset in range(count):
-        for copy in copies[offset]:
-            copy.wait()
+    order = list(range(2, count)) + [0, 1]
+    slab_refs = (own_ref, near_ref) + tuple(far_refs)
+    for offset in order:
+        snaps_copies[offset].wait()
+        if offset < 2:
+            basis_copies[offset].wait()
         value = jnp.dot(part_refs[offset][...], slab_refs[offset][...], preferred_element_type=jnp.float32)
         total = value if total is None else total + value
     half = total.shape[0] // 2
@@ -72,15 +86,12 @@
 
 
 def recon_kernel(place_ref, *refs):
-    count = (len(refs) - 1) // 2
-    points = refs[count].shape[0]
+    recon_ref, coefficients_ref = refs[-2:]
+    coefficients_ref[...] = refs[0][...].astype(jnp.float32).T
     chunk = 256
-    for start in range(0, points, chunk):
+    for start in range(0, recon_ref.shape[1], chunk):
         cols = slice(start, start + chunk)
-        recon = nt_dot(refs[0][...], refs[count][cols, :])
-        for low_ref, basis_ref in zip(refs[1:count], refs[count + 1 : -1]):
-            recon += nt_dot(low_ref[...], basis_ref[cols, :])
-        refs[-1][:, cols] = recon
+        recon_ref[:, cols] = nt_dot(refs[0][...], refs[2][cols, :]) + nt_dot(refs[1][...], refs[3][cols, :])
 
 
 def packed_rows(tiles):
@@ -149,37 +160,36 @@
 def eliminate(panel, offset):
     groups = BLOCK // SUB
     sub_iota = lax.broadcasted_iota(jnp.int32, (SUB, LANES), 0)
-    columns = [
-        [jnp.broadcast_to(panel[0][g][:, offset + j : offset + j + 1], (SUB, LANES)) for g in range(groups)]
-        for j in range(BLOCK)
-    ]
     scales = [jnp.zeros((SUB, LANES), jnp.float32) for _ in range(groups)]
-    for p in range(BLOCK):
-        home, line = divmod(p, SUB)
-        pivot = row_of(columns[p][home], line)
-        inverse = 1.0 / pivot
-        scales[home] = jnp.where(sub_iota == line, lax.rsqrt(pivot), scales[home])
-        factors = {}
-        for g in range(home, groups):
-            value = columns[p][g] * inverse
-            if g == home:
-                if line == SUB - 1:
-                    continue
-                value = jnp.where(sub_iota > line, value, 0.0)
-            factors[g] = value
-        for lanes in columns[p + 1 :] + panel:
-            lead = row_of(lanes[home], line)
-            for g, value in factors.items():
-                lanes[g] = lanes[g] - value * lead
+    for begin in range(0, BLOCK, STEP):
+        columns = [
+            [
+                jnp.broadcast_to(panel[0][g][:, offset + j : offset + j + 1], (SUB, LANES))
+                if g >= begin // SUB
+                else None
+                for g in range(groups)
+            ]
+            for j in range(begin, begin + STEP)
+        ]
+        for p in range(begin, begin + STEP):
+            home, line = divmod(p, SUB)
+            column = columns[p - begin]
+            pivot = row_of(column[home], line)
+            inverse = 1.0 / pivot
+            scales[home] = jnp.where(sub_iota == line, lax.rsqrt(pivot), scales[home])
+            factors = {}
+            for g in range(home, groups):
+                value = column[g] * inverse
+                if g == home:
+                    if line == SUB - 1:
+                        continue
+                    value = jnp.where(sub_iota > line, value, 0.0)
+                factors[g] = value
+            for lanes in columns[p - begin + 1 :] + panel:
+                lead = row_of(lanes[home], line)
+                for g, value in factors.items():
+                    lanes[g] = lanes[g] - value * lead
     return [[tile * scale for tile, scale in zip(lanes, scales)] for lanes in panel]
-
-
-def three_way(value):
-    first = value.astype(jnp.bfloat16)
-    value = value - first.astype(jnp.float32)
-    second = value.astype(jnp.bfloat16)
-    third = (value - second.astype(jnp.float32)).astype(jnp.bfloat16)
-    return first, second, third
 
 
 def factor_kernel(place_ref, mine_ref, other_ref, high_ref, rest_ref, factor_ref, out_ref, a_ref, w_ref, pack_ref):
@@ -221,9 +231,9 @@
         after = base + BLOCK
         if after == size:
             break
-        parts = [three_way(value) for value in panel]
-        left = [jnp.concatenate([a, a, b, a, c, b], axis=0) for a, b, c in parts[: len(a_tiles)]]
-        right = [jnp.concatenate([a, b, a, c, a, b], axis=0) for a, b, c in parts]
+        parts = [wide_split(value) for value in panel]
+        left = [jnp.concatenate([a, a, b], axis=0) for a, b in parts[: len(a_tiles)]]
+        right = [jnp.concatenate([a, b, a], axis=0) for a, b in parts]
         for row_tile in a_tiles:
             skip = after - row_tile * LANES if after > row_tile * LANES else 0
             if skip == LANES:
@@ -262,14 +272,15 @@
 def call(kernel, outs, scratch, flops, grant, whole=0):
     vmem = pl.BlockSpec(memory_space=pltpu.VMEM)
     smem = pl.BlockSpec(memory_space=pltpu.SMEM)
-    anywhere = pl.BlockSpec(memory_space=pl.ANY)
+    hbm = pl.BlockSpec(memory_space=pltpu.HBM)
 
     def run(scalar, *args):
         size = sum(math.prod(x.shape) * x.dtype.itemsize for x in (*args, *outs))
+        args = [pltpu.with_memory_space_constraint(x, pltpu.HBM) for x in args[:whole]] + list(args[whole:])
         return pl.pallas_call(
             kernel,
             out_shape=outs,
-            in_specs=[smem] + [anywhere] * whole + [vmem] * (len(args) - whole),
+            in_specs=[smem] + [hbm] * whole + [vmem] * (len(args) - whole),
             out_specs=[vmem] * len(outs),
             scratch_shapes=scratch,
             compiler_params=pltpu.CompilerParams(vmem_limit_bytes=grant << 20),
@@ -299,36 +310,35 @@
     odd = (flat // jnp.where(column_index % 2 == 0, sum_steps[0][0], sum_steps[0][1])) % 2
     place = jnp.stack([column_index, odd]).astype(jnp.int32)
 
-    kept, sent, *slabs = call(
+    slab = shape(bf16, points, modes)
+    semaphores = pltpu.SemaphoreType.DMA((columns,))
+    far_slabs = call(slab_kernel, (slab,) * (columns - 2), [semaphores], 0, 8, 1)(place, basis_cols)
+    arrived_slabs = [swap(far_slabs[at], (2 + at,) * 2) for at in range(columns - 2)]
+    part = shape(f32, half, modes)
+    kept, sent, own_slab, near_slab, own_snaps = call(
         project_kernel,
-        (shape(f32, half, modes),) * 2 + (shape(bf16, points, modes),) * columns + (shape(bf16, snaps, points),),
-        [pltpu.VMEM((snaps, points), bf16)] * (columns - 1)
-        + [pltpu.SemaphoreType.DMA((columns,)), pltpu.SemaphoreType.DMA((columns,))],
+        (part, part, slab, slab, shape(bf16, snaps, points)),
+        [pltpu.VMEM((snaps, points), bf16)] * (columns - 1) + [semaphores, semaphores],
         2 * snaps * row_points * modes,
-        16,
+        12,
         2,
-    )(place, basis_cols, snapshots)
-    own_snaps = slabs.pop()
-    for offset in reversed(range(1, columns)):
-        slabs[offset] = swap(slabs[offset], (offset, offset))
-
+    )(place, basis_cols, snapshots, *far_slabs)
     arrived = swap(sent, sum_steps[0])
+    near_slab = swap(near_slab, (1, 1))
     kept = kept + arrived
     for step in sum_steps[1:]:
         kept = kept + swap(kept, step)
     low = (kept * (math.sqrt(RANK) / total_points)).astype(bf16)
-    other = swap(low, sum_steps[0])
-    low = jnp.where(odd == 1, jnp.concatenate([other, low], 0), jnp.concatenate([low, other], 0))
-    coefficients = low.astype(f32).T
-    lows = {0: low}
-    near = swap(low, (1, 1))
-    for offset in reversed(bits(columns // 2, 2)):
-        lows.update({key ^ offset: swap(value, (offset, offset)) for key, value in list(lows.items())})
-    lows.update({key ^ 1: near if key == 0 else swap(value, (1, 1)) for key, value in list(lows.items())})
-
-    (begun,) = call(recon_kernel, (shape(f32, snaps, points),), [], 4 * snaps * points * modes, 8)(
-        place, lows[0], lows[1], slabs[0], slabs[1]
-    )
+    lows = {}
+    for offset in range(0, columns, 2):
+        own = swap(low, (offset, offset)) if offset else low
+        other = swap(low, tuple(mask ^ offset for mask in sum_steps[0]))
+        lows[offset] = jnp.concatenate([jnp.where(odd == 1, other, own), jnp.where(odd == 1, own, other)], 0)
+        lows[offset + 1] = swap(lows[offset], (1, 1))
+
+    begun, coefficients = call(
+        recon_kernel, (shape(f32, snaps, points), shape(f32, modes, snaps)), [], 4 * snaps * points * modes, 8
+    )(place, lows[0], lows[1], own_slab, near_slab)
     packed = packed_rows(snaps // LANES)
     part = shape(f32, packed // 2, LANES)
     wide = shape(bf16, snaps, points)
@@ -338,7 +348,7 @@
         [pltpu.VMEM((packed, LANES), f32)],
         2 * snaps * points * (modes * (columns - 2) + 3 * snaps),
         16,
-    )(place, *[lows[offset] for offset in range(2, columns)], *slabs[2:], begun, own_snaps)
+    )(place, *[lows[offset] for offset in range(2, columns)], *arrived_slabs, begun, own_snaps)
     keep = keep + swap(send, (1, 1))
     rest_bits = bits(columns // 2, 2) + row_bits
     first_order = rest_bits[-1:] + rest_bits[:-1]

time: 85.8 us -> 88.6 us (1.033)
  local copies, waits for them, and re-layouts: 4.02 us -> 0 us
  waiting for transfers between devices: 44.7 us -> 48 us
  Pallas kernels: 15.9 us -> 19.1 us
    unnamed x5 -> x0, local copies, waits for them, and re-layouts: 4.02 us -> none
    ppermute x16 -> x17, waiting for transfers between devices: 44.7 us -> 48 us  [swap(): lax.ppermute(value, ('rows', 'cols'), [(i, i ^ masks[i % 2]) for i in ran...]
    pallas_call x4 -> x5, Pallas kernels: 15.9 us -> 19.1 us  [run(): pl.pallas_call(kernel, out_shape=outs, in_specs=[smem] + [hbm] * whole +...]
    ppermute x16 -> x17, starting transfers between devices: 20 us -> 20.4 us  [swap(): lax.ppermute(value, ('rows', 'cols'), [(i, i ^ masks[i % 2]) for i in ran...]
  transfers between devices with their start and end apart: 16 -> 17, of which waited for: 12 -> 11; matrix products, arithmetic and copies ran while one was open for 1% -> 0% of each run, Pallas kernels for 1% -> 2%
where the time goes in v1:
time: 88.6 us; the launch traced here: 88.4 us
  waiting for transfers between devices  48 us (54%)
  starting transfers between devices  20.4 us (23%)
  Pallas kernels  19.1 us (22%)
    ppermute x17, waiting for transfers between devices, swap(): lax.ppermute(value, ('rows', 'cols'), [(i, i ^ masks[i % 2]) for i in ran...  48 us
    ppermute x17, starting transfers between devices, swap(): lax.ppermute(value, ('rows', 'cols'), [(i, i ^ masks[i % 2]) for i in ran...  20.4 us
    pallas_call x5, Pallas kernels, run(): pl.pallas_call(kernel, out_shape=outs, in_specs=[smem] + [hbm] * whole +...  19.1 us
  transfers between devices with their start and end apart: 17, of which 11 were waited for; matrix products, arithmetic and copies ran while one was open for 0% of the time, Pallas kernels for 2%

profile of v1, /device:TPU:0, one launch (start us, length us, event | category | flops | bytes accessed | tf_op | source)
XLA Modules:
  0.0 88.4 jit_solution(5115123881094840595)
XLA Ops:
  0.7 0.1 pad_add_fusion.place_ref
  0.8 2.6 %shard_map.49 = (bf16[1024,256]{1,0:T(8,128)(2,1)}, bf16[1024,256]{1,0:T(8,128)(2,1)S(1)}) custom-call(s32[2]{0:T(128)S(1)} %pad_add_fusion.place_ref, bf16[4096,256]{1,0:T(8,128)(2,1)} %basis_ref.3), custom_call_target="tpu_custom_call" | custom-call | bytes 3145728 | tf_op jit(solution)/shard_map/pallas_call | solution.py:280
  3.3 4.1 %shard_map.50 = (f32[128,256]{1,0:T(8,128)S(1)}, f32[128,256]{1,0:T(8,128)S(1)}, bf16[1024,256]{1,0:T(8,128)(2,1)S(1)}, bf16[1024,256]{1,0:T(8,128)(2,1)}, bf16[256,1024]{1,0:T(8,128)(2,1)S(1)}) custom-call(s32[2]{0:T(128)S(1)} %pad_add_fusion.place_ref, bf16[4096,256]{1,0:T(8,128)(2,1)} %basis_ref.3, bf16[256,4096]{1,0:T(8,128)(2,1)} %snaps_ref.1, ...), custom_call_target="tpu_custom_call" | custom-call | flops 536870912 | bytes 7077888 | tf_op jit(solution)/shard_map/pallas_call | solution.py:280
  7.5 3.1 %collective-permute-start = (f32[128,256]{1,0:T(8,128)S(1)}, f32[128,256]{1,0:T(8,128)S(1)}, u32[]{:S(2)}, u32[]{:S(2)}) collective-permute-start(f32[128,256]{1,0:T(8,128)S(1)} %get-tuple-element.21), channel_id=1, source_target_pairs={{0,4},{1,9},{2,6},{3,11},{4,0},{5,13},{6,2},{7,15},{8,12},{9,1},{1... | collective-permute-start | bytes 393224 | tf_op jit(solution)/shard_map/ppermute | solution.py:21
  10.5 2.9 %collective-permute-done = f32[128,256]{1,0:T(8,128)S(1)} collective-permute-done((f32[128,256]{1,0:T(8,128)S(1)}, f32[128,256]{1,0:T(8,128)S(1)}, u32[]{:S(2)}, u32[]{:S(2)}) %collective-permute-start) | collective-permute-done | bytes 131104 | tf_op jit(solution)/shard_map/ppermute | solution.py:21
  13.5 2.1 %collective-permute-start.1 = (f32[128,256]{1,0:T(8,128)S(1)}, f32[128,256]{1,0:T(8,128)S(1)}, u32[]{:S(2)}, u32[]{:S(2)}) collective-permute-start(f32[128,256]{1,0:T(8,128)S(1)} %add.38), channel_id=1, source_target_pairs={{0,8},{1,17},{2,10},{3,19},{4,12},{5,21},{6,14},{7,23},{8,0},{9,25... | collective-permute-start | bytes 393224 | tf_op jit(solution)/shard_map/ppermute | solution.py:21
  15.6 3.4 %collective-permute-done.1 = f32[128,256]{1,0:T(8,128)S(1)} collective-permute-done((f32[128,256]{1,0:T(8,128)S(1)}, f32[128,256]{1,0:T(8,128)S(1)}, u32[]{:S(2)}, u32[]{:S(2)}) %collective-permute-start.1) | collective-permute-done | bytes 131104 | tf_op jit(solution)/shard_map/ppermute | solution.py:21
  19.1 3.0 %collective-permute-start.2 = (f32[128,256]{1,0:T(8,128)S(1)}, f32[128,256]{1,0:T(8,128)S(1)}, u32[]{:S(2)}, u32[]{:S(2)}) collective-permute-start(f32[128,256]{1,0:T(8,128)S(1)} %add.39), channel_id=1, source_target_pairs={{0,16},{1,5},{2,18},{3,7},{4,20},{5,1},{6,22},{7,3},{8,24},{9,13},... | collective-permute-start | bytes 393224 | tf_op jit(solution)/shard_map/ppermute | solution.py:21
  22.1 2.9 %collective-permute-done.2 = f32[128,256]{1,0:T(8,128)S(1)} collective-permute-done((f32[128,256]{1,0:T(8,128)S(1)}, f32[128,256]{1,0:T(8,128)S(1)}, u32[]{:S(2)}, u32[]{:S(2)}) %collective-permute-start.2) | collective-permute-done | bytes 131104 | tf_op jit(solution)/shard_map/ppermute | solution.py:21
  25.1 1.6 %collective-permute-start.3 = (bf16[128,256]{1,0:T(8,128)(2,1)S(1)}, bf16[128,256]{1,0:T(8,128)(2,1)S(1)}, u32[]{:S(2)}, u32[]{:S(2)}) collective-permute-start(bf16[128,256]{1,0:T(8,128)(2,1)S(1)} %multiply_convert_fusion), channel_id=1, source_target_pairs={{0,4},{1,9},{2,6},{3,11},{4,0},{5,13},{6,2},{7,15},{8,12},{9,1},{1... | collective-permute-start | bytes 196616 | tf_op jit(solution)/shard_map/ppermute | solution.py:21
  26.7 1.5 %collective-permute-start.9 = (bf16[1024,256]{1,0:T(8,128)(2,1)}, bf16[1024,256]{1,0:T(8,128)(2,1)S(1)}, u32[]{:S(2)}, u32[]{:S(2)}) collective-permute-start(bf16[1024,256]{1,0:T(8,128)(2,1)} %get-tuple-element.18.refs_0_), channel_id=1, source_target_pairs={{0,2},{1,3},{2,0},{3,1},{4,6},{5,7},{6,4},{7,5},{8,10},{9,11},{10,... | collective-permute-start | bytes 1572872 | tf_op jit(solution)/shard_map/ppermute | solution.py:21
  28.1 0.7 collective-permute-start.5
  28.8 1.4 %collective-permute-start.6 = (bf16[128,256]{1,0:T(8,128)(2,1)S(1)}, bf16[128,256]{1,0:T(8,128)(2,1)S(1)}, u32[]{:S(2)}, u32[]{:S(2)}) collective-permute-start(bf16[128,256]{1,0:T(8,128)(2,1)S(1)} %multiply_convert_fusion), channel_id=1, source_target_pairs={{0,6},{1,11},{2,4},{3,9},{4,2},{5,15},{6,0},{7,13},{8,14},{9,3},{1... | collective-permute-start | bytes 196616 | tf_op jit(solution)/shard_map/ppermute | solution.py:21
  30.2 0.7 collective-permute-start.7
  30.9 21.3 %collective-permute-done.6 = bf16[128,256]{1,0:T(8,128)(2,1)S(1)} collective-permute-done((bf16[128,256]{1,0:T(8,128)(2,1)S(1)}, bf16[128,256]{1,0:T(8,128)(2,1)S(1)}, u32[]{:S(2)}, u32[]{:S(2)}) %collective-permute-start.6) | collective-permute-done | bytes 65568 | tf_op jit(solution)/shard_map/ppermute | solution.py:21
  52.2 0.6 collective-permute-start.8
  52.8 0.7 collective-permute-done.4.refs_1_
  53.5 1.6 %shard_map.51 = (f32[256,1024]{1,0:T(8,128)S(1)}, f32[256,256]{1,0:T(8,128)}) custom-call(s32[2]{0:T(128)S(1)} %pad_add_fusion.place_ref, bf16[256,256]{1,0:T(8,128)(2,1)S(1)} %pad_maximum_fusion.refs_0_, bf16[256,256]{1,0:T(8,128)(2,1)S(1)} %collective-permute-done.4.refs_1_, bf16[1024,256]{1,0:T(8,128)(2,1)S(1)} %get-tuple-element.22.refs_2_, ...), custom_call_target="tpu_custom_call" | custom-call | flops 268435456 | bytes 2621440 | tf_op jit(solution)/shard_map/pallas_call | solution.py:280
  55.2 2.1 %shard_map.52 = (bf16[256,1024]{1,0:T(8,128)(2,1)S(1)}, bf16[256,1024]{1,0:T(8,128)(2,1)S(1)}, f32[136,128]{1,0:T(8,128)S(1)}, f32[136,128]{1,0:T(8,128)S(1)}) custom-call(s32[2]{0:T(128)S(1)} %pad_add_fusion.place_ref, bf16[256,256]{1,0:T(8,128)(2,1)S(1)} %pad_maximum_fusion.1.refs_0_, bf16[256,256]{1,0:T(8,128)(2,1)S(1)} %collective-permute-done.8.refs_1_, ...), custom_call_target="tpu_custom_call" | custom-call | flops 671088640 | bytes 4071424 | tf_op jit(solution)/shard_map/pallas_call | solution.py:280
  57.3 0.2 collective-permute-start.11
  57.5 1.1 %collective-permute-done.11 = f32[136,128]{1,0:T(8,128)S(1)} collective-permute-done((f32[136,128]{1,0:T(8,128)S(1)}, f32[136,128]{1,0:T(8,128)S(1)}, u32[]{:S(2)}, u32[]{:S(2)}) %collective-permute-start.11) | collective-permute-done | bytes 69664 | tf_op jit(solution)/shard_map/ppermute | solution.py:21
  58.6 3.3 %collective-permute-start.12 = (f32[136,128]{1,0:T(8,128)S(1)}, f32[136,128]{1,0:T(8,128)S(1)}, u32[]{:S(2)}, u32[]{:S(2)}) collective-permute-start(f32[136,128]{1,0:T(8,128)S(1)} %add.41), channel_id=1, source_target_pairs={{0,16},{1,3},{2,18},{3,1},{4,20},{5,7},{6,22},{7,5},{8,24},{9,11},... | collective-permute-start | bytes 208904 | tf_op jit(solution)/shard_map/ppermute | solution.py:21
  61.9 3.0 %collective-permute-done.12 = f32[136,128]{1,0:T(8,128)S(1)} collective-permute-done((f32[136,128]{1,0:T(8,128)S(1)}, f32[136,128]{1,0:T(8,128)S(1)}, u32[]{:S(2)}, u32[]{:S(2)}) %collective-permute-start.12) | collective-permute-done | bytes 69664 | tf_op jit(solution)/shard_map/ppermute | solution.py:21
  64.9 1.6 %collective-permute-start.13 = (f32[136,128]{1,0:T(8,128)S(1)}, f32[136,128]{1,0:T(8,128)S(1)}, u32[]{:S(2)}, u32[]{:S(2)}) collective-permute-start(f32[136,128]{1,0:T(8,128)S(1)} %add.42), channel_id=1, source_target_pairs={{0,2},{1,17},{2,0},{3,19},{4,6},{5,21},{6,4},{7,23},{8,10},{9,25},... | collective-permute-start | bytes 208904 | tf_op jit(solution)/shard_map/ppermute | solution.py:21
  66.5 2.8 %collective-permute-done.13 = f32[136,128]{1,0:T(8,128)S(1)} collective-permute-done((f32[136,128]{1,0:T(8,128)S(1)}, f32[136,128]{1,0:T(8,128)S(1)}, u32[]{:S(2)}, u32[]{:S(2)}) %collective-permute-start.13) | collective-permute-done | bytes 69664 | tf_op jit(solution)/shard_map/ppermute | solution.py:21
  69.3 0.6 collective-permute-start.14
  69.9 4.2 %collective-permute-done.14 = f32[136,128]{1,0:T(8,128)S(1)} collective-permute-done((f32[136,128]{1,0:T(8,128)S(1)}, f32[136,128]{1,0:T(8,128)S(1)}, u32[]{:S(2)}, u32[]{:S(2)}) %collective-permute-start.14) | collective-permute-done | bytes 69664 | tf_op jit(solution)/shard_map/ppermute | solution.py:21
  74.1 0.1 collective-permute-start.15
  74.2 4.3 %collective-permute-done.15 = f32[136,128]{1,0:T(8,128)S(1)} collective-permute-done((f32[136,128]{1,0:T(8,128)S(1)}, f32[136,128]{1,0:T(8,128)S(1)}, u32[]{:S(2)}, u32[]{:S(2)}) %collective-permute-start.15) | collective-permute-done | bytes 69664 | tf_op jit(solution)/shard_map/ppermute | solution.py:21
  78.5 0.1 collective-permute-start.16
  78.5 1.2 %collective-permute-done.16.other_ref = f32[136,128]{1,0:T(8,128)S(1)} collective-permute-done((f32[136,128]{1,0:T(8,128)S(1)}, f32[136,128]{1,0:T(8,128)S(1)}, u32[]{:S(2)}, u32[]{:S(2)}) %collective-permute-start.16) | collective-permute-done | bytes 69664 | tf_op jit(solution)/shard_map/ppermute | solution.py:21
  79.8 8.6 %shard_map.53 = (f32[256,256]{1,0:T(8,128)}, bf16[256,1024]{1,0:T(8,128)(2,1)}) custom-call(s32[2]{0:T(128)S(1)} %pad_add_fusion.place_ref, f32[136,128]{1,0:T(8,128)S(1)} %add.45.mine_ref, f32[136,128]{1,0:T(8,128)S(1)} %collective-permute-done.16.other_ref, bf16[256,1024]{1,0:T(8,128)(2,1)S(1)} %get-tuple-element.29.high_ref, ...), custom_call_target="tpu_custom_call" | custom-call | flops 402653184 | bytes 1974272 | tf_op jit(solution)/shard_map/pallas_call | solution.py:280
  (20 shorter events, 0.2 us)
Async XLA Ops:
  7.5 6.0 %collective-permute-start = (f32[128,256]{1,0:T(8,128)S(1)}, f32[128,256]{1,0:T(8,128)S(1)}, u32[]{:S(2)}, u32[]{:S(2)}) collective-permute-start(f32[128,256]{1,0:T(8,128)S(1)} %get-tuple-element.21), channel_id=1, source_target_pairs={{0,4},{1,9},{2,6},{3,11},{4,0},{5,13},{6,2},{7,15},{8,12},{9,1},{1... | collective-permute-start | bytes 393224 | tf_op jit(solution)/shard_map/ppermute | solution.py:21
  13.5 5.6 %collective-permute-start.1 = (f32[128,256]{1,0:T(8,128)S(1)}, f32[128,256]{1,0:T(8,128)S(1)}, u32[]{:S(2)}, u32[]{:S(2)}) collective-permute-start(f32[128,256]{1,0:T(8,128)S(1)} %add.38), channel_id=1, source_target_pairs={{0,8},{1,17},{2,10},{3,19},{4,12},{5,21},{6,14},{7,23},{8,0},{9,25... | collective-permute-start | bytes 393224 | tf_op jit(solution)/shard_map/ppermute | solution.py:21
  19.1 6.0 %collective-permute-start.2 = (f32[128,256]{1,0:T(8,128)S(1)}, f32[128,256]{1,0:T(8,128)S(1)}, u32[]{:S(2)}, u32[]{:S(2)}) collective-permute-start(f32[128,256]{1,0:T(8,128)S(1)} %add.39), channel_id=1, source_target_pairs={{0,16},{1,5},{2,18},{3,7},{4,20},{5,1},{6,22},{7,3},{8,24},{9,13},... | collective-permute-start | bytes 393224 | tf_op jit(solution)/shard_map/ppermute | solution.py:21
  25.1 5.2 %collective-permute-start.3 = (bf16[128,256]{1,0:T(8,128)(2,1)S(1)}, bf16[128,256]{1,0:T(8,128)(2,1)S(1)}, u32[]{:S(2)}, u32[]{:S(2)}) collective-permute-start(bf16[128,256]{1,0:T(8,128)(2,1)S(1)} %multiply_convert_fusion), channel_id=1, source_target_pairs={{0,4},{1,9},{2,6},{3,11},{4,0},{5,13},{6,2},{7,15},{8,12},{9,1},{1... | collective-permute-start | bytes 196616 | tf_op jit(solution)/shard_map/ppermute | solution.py:21
  26.7 28.5 %collective-permute-start.9 = (bf16[1024,256]{1,0:T(8,128)(2,1)}, bf16[1024,256]{1,0:T(8,128)(2,1)S(1)}, u32[]{:S(2)}, u32[]{:S(2)}) collective-permute-start(bf16[1024,256]{1,0:T(8,128)(2,1)} %get-tuple-element.18.refs_0_), channel_id=1, source_target_pairs={{0,2},{1,3},{2,0},{3,1},{4,6},{5,7},{6,4},{7,5},{8,10},{9,11},{10,... | collective-permute-start | bytes 1572872 | tf_op jit(solution)/shard_map/ppermute | solution.py:21
  28.1 27.0 %collective-permute-start.10 = (bf16[1024,256]{1,0:T(8,128)(2,1)S(1)}, bf16[1024,256]{1,0:T(8,128)(2,1)S(1)}, u32[]{:S(2)}, u32[]{:S(2)}) collective-permute-start(bf16[1024,256]{1,0:T(8,128)(2,1)S(1)} %get-tuple-element.19.refs_1_), channel_id=1, source_target_pairs={{0,3},{1,2},{2,1},{3,0},{4,7},{5,6},{6,5},{7,4},{8,11},{9,10},{10,... | collective-permute-start | bytes 1572872 | tf_op jit(solution)/shard_map/ppermute | solution.py:21
  28.1 24.7 %collective-permute-start.5 = (bf16[1024,256]{1,0:T(8,128)(2,1)}, bf16[1024,256]{1,0:T(8,128)(2,1)S(1)}, u32[]{:S(2)}, u32[]{:S(2)}) collective-permute-start(bf16[1024,256]{1,0:T(8,128)(2,1)} %get-tuple-element.23), channel_id=1, source_target_pairs={{0,1},{1,0},{2,3},{3,2},{4,5},{5,4},{6,7},{7,6},{8,9},{9,8},{10,11... | collective-permute-start | bytes 1572872 | tf_op jit(solution)/shard_map/ppermute | solution.py:21
  28.8 23.4 %collective-permute-start.6 = (bf16[128,256]{1,0:T(8,128)(2,1)S(1)}, bf16[128,256]{1,0:T(8,128)(2,1)S(1)}, u32[]{:S(2)}, u32[]{:S(2)}) collective-permute-start(bf16[128,256]{1,0:T(8,128)(2,1)S(1)} %multiply_convert_fusion), channel_id=1, source_target_pairs={{0,6},{1,11},{2,4},{3,9},{4,2},{5,15},{6,0},{7,13},{8,14},{9,3},{1... | collective-permute-start | bytes 196616 | tf_op jit(solution)/shard_map/ppermute | solution.py:21
  30.2 22.0 %collective-permute-start.7 = (bf16[128,256]{1,0:T(8,128)(2,1)S(1)}, bf16[128,256]{1,0:T(8,128)(2,1)S(1)}, u32[]{:S(2)}, u32[]{:S(2)}) collective-permute-start(bf16[128,256]{1,0:T(8,128)(2,1)S(1)} %multiply_convert_fusion), channel_id=1, source_target_pairs={{0,2},{1,3},{2,0},{3,1},{4,6},{5,7},{6,4},{7,5},{8,10},{9,11},{10,... | collective-permute-start | bytes 196616 | tf_op jit(solution)/shard_map/ppermute | solution.py:21
  52.2 1.3 %collective-permute-start.4 = (bf16[256,256]{1,0:T(8,128)(2,1)S(1)}, bf16[256,256]{1,0:T(8,128)(2,1)S(1)}, u32[]{:S(2)}, u32[]{:S(2)}) collective-permute-start(bf16[256,256]{1,0:T(8,128)(2,1)S(1)} %pad_maximum_fusion.refs_0_), channel_id=1, source_target_pairs={{0,1},{1,0},{2,3},{3,2},{4,5},{5,4},{6,7},{7,6},{8,9},{9,8},{10,11... | collective-permute-start | bytes 393224 | tf_op jit(solution)/shard_map/ppermute | solution.py:21
  52.2 2.9 %collective-permute-start.8 = (bf16[256,256]{1,0:T(8,128)(2,1)S(1)}, bf16[256,256]{1,0:T(8,128)(2,1)S(1)}, u32[]{:S(2)}, u32[]{:S(2)}) collective-permute-start(bf16[256,256]{1,0:T(8,128)(2,1)S(1)} %pad_maximum_fusion.1.refs_0_), channel_id=1, source_target_pairs={{0,1},{1,0},{2,3},{3,2},{4,5},{5,4},{6,7},{7,6},{8,9},{9,8},{10,11... | collective-permute-start | bytes 393224 | tf_op jit(solution)/shard_map/ppermute | solution.py:21
  57.3 1.3 %collective-permute-start.11 = (f32[136,128]{1,0:T(8,128)S(1)}, f32[136,128]{1,0:T(8,128)S(1)}, u32[]{:S(2)}, u32[]{:S(2)}) collective-permute-start(f32[136,128]{1,0:T(8,128)S(1)} %get-tuple-element.28), channel_id=1, source_target_pairs={{0,1},{1,0},{2,3},{3,2},{4,5},{5,4},{6,7},{7,6},{8,9},{9,8},{10,11... | collective-permute-start | bytes 208904 | tf_op jit(solution)/shard_map/ppermute | solution.py:21
  58.6 6.3 %collective-permute-start.12 = (f32[136,128]{1,0:T(8,128)S(1)}, f32[136,128]{1,0:T(8,128)S(1)}, u32[]{:S(2)}, u32[]{:S(2)}) collective-permute-start(f32[136,128]{1,0:T(8,128)S(1)} %add.41), channel_id=1, source_target_pairs={{0,16},{1,3},{2,18},{3,1},{4,20},{5,7},{6,22},{7,5},{8,24},{9,11},... | collective-permute-start | bytes 208904 | tf_op jit(solution)/shard_map/ppermute | solution.py:21
  64.9 4.4 %collective-permute-start.13 = (f32[136,128]{1,0:T(8,128)S(1)}, f32[136,128]{1,0:T(8,128)S(1)}, u32[]{:S(2)}, u32[]{:S(2)}) collective-permute-start(f32[136,128]{1,0:T(8,128)S(1)} %add.42), channel_id=1, source_target_pairs={{0,2},{1,17},{2,0},{3,19},{4,6},{5,21},{6,4},{7,23},{8,10},{9,25},... | collective-permute-start | bytes 208904 | tf_op jit(solution)/shard_map/ppermute | solution.py:21
  69.3 4.8 %collective-permute-start.14 = (f32[136,128]{1,0:T(8,128)S(1)}, f32[136,128]{1,0:T(8,128)S(1)}, u32[]{:S(2)}, u32[]{:S(2)}) collective-permute-start(f32[136,128]{1,0:T(8,128)S(1)} %add.43), channel_id=1, source_target_pairs={{0,4},{1,9},{2,6},{3,11},{4,0},{5,13},{6,2},{7,15},{8,12},{9,1},{1... | collective-permute-start | bytes 208904 | tf_op jit(solution)/shard_map/ppermute | solution.py:21
  74.1 4.4 %collective-permute-start.15 = (f32[136,128]{1,0:T(8,128)S(1)}, f32[136,128]{1,0:T(8,128)S(1)}, u32[]{:S(2)}, u32[]{:S(2)}) collective-permute-start(f32[136,128]{1,0:T(8,128)S(1)} %add.44), channel_id=1, source_target_pairs={{0,8},{1,5},{2,10},{3,7},{4,12},{5,1},{6,14},{7,3},{8,0},{9,13},{1... | collective-permute-start | bytes 208904 | tf_op jit(solution)/shard_map/ppermute | solution.py:21
  78.5 1.3 %collective-permute-start.16 = (f32[136,128]{1,0:T(8,128)S(1)}, f32[136,128]{1,0:T(8,128)S(1)}, u32[]{:S(2)}, u32[]{:S(2)}) collective-permute-start(f32[136,128]{1,0:T(8,128)S(1)} %add.45.mine_ref), channel_id=1, source_target_pairs={{0,1},{1,0},{2,3},{3,2},{4,5},{5,4},{6,7},{7,6},{8,9},{9,8},{10,11... | collective-permute-start | bytes 208904 | tf_op jit(solution)/shard_map/ppermute | solution.py:21

commit v2 on v1

--- a/solution.py
+++ b/solution.py
@@ -29,6 +29,13 @@
     return found
 
 
+def exchange_rounds(masks):
+    rounds = [(masks[at], masks[at + 1] if at + 1 < len(masks) else 0) for at in range(0, len(masks), 2)]
+    paired = [pair for pair in rounds if pair[1]]
+    single = [pair for pair in rounds if not pair[1]]
+    return paired + single, paired[::-1] + single
+
+
 def wide_split(value):
     high = value.astype(jnp.bfloat16)
     return high, (value - high.astype(jnp.float32)).astype(jnp.bfloat16)
@@ -42,40 +49,27 @@
     return lax.dot_general(left, right, (((0,), (0,)), ((), ())), preferred_element_type=jnp.float32)
 
 
-def slab_copies(place_ref, whole_ref, into_refs, sem_ref, first, by_rows):
+def project_kernel(place_ref, basis_ref, snaps_ref, keep_ref, send_ref, *refs):
+    count = (len(refs) - 2) // 2
+    slab_refs, part_refs, basis_sem, snaps_sem = refs[:count], refs[count : 2 * count], refs[-2], refs[-1]
+    points = slab_refs[0].shape[0]
     copies = []
-    for index, into_ref in enumerate(into_refs):
-        size = into_ref.shape[0 if by_rows else 1]
-        start = pl.multiple_of((place_ref[0] ^ (first + index)) * size, size)
-        span = whole_ref.at[pl.ds(start, size), :] if by_rows else whole_ref.at[:, pl.ds(start, size)]
-        copies.append(pltpu.make_async_copy(span, into_ref, sem_ref.at[index]))
-    return copies
-
-
-def slab_kernel(place_ref, basis_ref, *refs):
-    copies = slab_copies(place_ref, basis_ref, refs[:-1], refs[-1], 2, True)
-    for copy in copies:
-        copy.start()
-    for copy in copies:
-        copy.wait()
-
-
-def project_kernel(place_ref, basis_ref, snaps_ref, *refs):
-    count = (len(refs) - 3) // 2
-    far_refs = refs[: count - 2]
-    keep_ref, send_ref, own_ref, near_ref = refs[count - 2 : count + 2]
-    part_refs, basis_sem, snaps_sem = refs[count + 2 : -2], refs[-2], refs[-1]
-    basis_copies = slab_copies(place_ref, basis_ref, (own_ref, near_ref), basis_sem, 0, True)
-    snaps_copies = slab_copies(place_ref, snaps_ref, part_refs, snaps_sem, 0, False)
-    for copy in snaps_copies[2:] + basis_copies + snaps_copies[:2]:
-        copy.start()
+    for offset in range(count):
+        start = pl.multiple_of((place_ref[0] ^ offset) * points, points)
+        span = pl.ds(start, points)
+        copies.append(
+            (
+                pltpu.make_async_copy(basis_ref.at[span, :], slab_refs[offset], basis_sem.at[offset]),
+                pltpu.make_async_copy(snaps_ref.at[:, span], part_refs[offset], snaps_sem.at[offset]),
+            )
+        )
+    for pair in copies:
+        for copy in pair:
+            copy.start()
     total = None
-    order = list(range(2, count)) + [0, 1]
-    slab_refs = (own_ref, near_ref) + tuple(far_refs)
-    for offset in order:
-        snaps_copies[offset].wait()
-        if offset < 2:
-            basis_copies[offset].wait()
+    for offset in range(count):
+        for copy in copies[offset]:
+            copy.wait()
         value = jnp.dot(part_refs[offset][...], slab_refs[offset][...], preferred_element_type=jnp.float32)
         total = value if total is None else total + value
     half = total.shape[0] // 2
@@ -310,30 +304,30 @@
     odd = (flat // jnp.where(column_index % 2 == 0, sum_steps[0][0], sum_steps[0][1])) % 2
     place = jnp.stack([column_index, odd]).astype(jnp.int32)
 
-    slab = shape(bf16, points, modes)
+    slab, part = shape(bf16, points, modes), shape(f32, half, modes)
     semaphores = pltpu.SemaphoreType.DMA((columns,))
-    far_slabs = call(slab_kernel, (slab,) * (columns - 2), [semaphores], 0, 8, 1)(place, basis_cols)
-    arrived_slabs = [swap(far_slabs[at], (2 + at,) * 2) for at in range(columns - 2)]
-    part = shape(f32, half, modes)
-    kept, sent, own_slab, near_slab, own_snaps = call(
+    kept, sent, *slabs, own_snaps = call(
         project_kernel,
-        (part, part, slab, slab, shape(bf16, snaps, points)),
+        (part, part) + (slab,) * columns + (shape(bf16, snaps, points),),
         [pltpu.VMEM((snaps, points), bf16)] * (columns - 1) + [semaphores, semaphores],
         2 * snaps * row_points * modes,
         12,
         2,
-    )(place, basis_cols, snapshots, *far_slabs)
+    )(place, basis_cols, snapshots)
+    arrived_slabs = [swap(slabs[offset], (offset,) * 2) for offset in range(2, columns)]
+    own_slab, near_slab = slabs[:2]
     arrived = swap(sent, sum_steps[0])
     near_slab = swap(near_slab, (1, 1))
     kept = kept + arrived
     for step in sum_steps[1:]:
         kept = kept + swap(kept, step)
     low = (kept * (math.sqrt(RANK) / total_points)).astype(bf16)
-    lows = {}
+    other = swap(low, sum_steps[0])
+    low = jnp.concatenate([jnp.where(odd == 1, other, low), jnp.where(odd == 1, low, other)], 0)
+    lows = {0: low}
+    for offset in range(2, columns, 2):
+        lows[offset] = swap(low, (offset, offset))
     for offset in range(0, columns, 2):
-        own = swap(low, (offset, offset)) if offset else low
-        other = swap(low, tuple(mask ^ offset for mask in sum_steps[0]))
-        lows[offset] = jnp.concatenate([jnp.where(odd == 1, other, own), jnp.where(odd == 1, own, other)], 0)
         lows[offset + 1] = swap(lows[offset], (1, 1))
 
     begun, coefficients = call(
@@ -350,13 +344,13 @@
         16,
     )(place, *[lows[offset] for offset in range(2, columns)], *arrived_slabs, begun, own_snaps)
     keep = keep + swap(send, (1, 1))
-    rest_bits = bits(columns // 2, 2) + row_bits
-    first_order = rest_bits[-1:] + rest_bits[:-1]
-    second_order = list(first_order)
-    for at in range(0, len(first_order) - 1, 2):
-        second_order[at : at + 2] = reversed(first_order[at : at + 2])
-    for step in zip(first_order, second_order):
-        keep = keep + swap(keep, step)
+    for masks in zip(*exchange_rounds(bits(columns // 2, 2) + row_bits)):
+        if masks[0][1] == 0:
+            keep = keep + swap(keep, [mask[0] for mask in masks])
+            continue
+        far = swap(keep, [mask[1] for mask in masks])
+        diagonal = swap(keep, [mask[0] ^ mask[1] for mask in masks])
+        keep = (keep + swap(keep, [mask[0] for mask in masks])) + (far + diagonal)
     rest_of_gram = swap(keep, (1, 1))
     factor, directions = call(
         factor_kernel,

time: 88.6 us -> 85.7 us (0.967)
  waiting for transfers between devices: 48 us -> 44.6 us
  starting transfers between devices: 20.4 us -> 23.4 us
  Pallas kernels: 19.1 us -> 16.6 us
    ppermute x17 -> x18, waiting for transfers between devices: 48 us -> 44.6 us  [swap(): lax.ppermute(value, ('rows', 'cols'), [(i, i ^ masks[i % 2]) for i in ran...]
    ppermute x17 -> x18, starting transfers between devices: 20.4 us -> 23.4 us  [swap(): lax.ppermute(value, ('rows', 'cols'), [(i, i ^ masks[i % 2]) for i in ran...]
    pallas_call x5 -> x4, Pallas kernels: 19.1 us -> 16.6 us  [run(): pl.pallas_call(kernel, out_shape=outs, in_specs=[smem] + [hbm] * whole +...]
  transfers between devices with their start and end apart: 17 -> 18, of which waited for: 11 -> 12; matrix products, arithmetic and copies ran while one was open for 0% -> 0% of each run, Pallas kernels for 2% -> 2%
where the time goes in v2:
time: 85.7 us; the launch traced here: 85.6 us
  waiting for transfers between devices  44.6 us (52%)
  starting transfers between devices  23.4 us (27%)
  Pallas kernels  16.6 us (19%)
    ppermute x18, waiting for transfers between devices, swap(): lax.ppermute(value, ('rows', 'cols'), [(i, i ^ masks[i % 2]) for i in ran...  44.6 us
    ppermute x18, starting transfers between devices, swap(): lax.ppermute(value, ('rows', 'cols'), [(i, i ^ masks[i % 2]) for i in ran...  23.4 us
    pallas_call x4, Pallas kernels, run(): pl.pallas_call(kernel, out_shape=outs, in_specs=[smem] + [hbm] * whole +...  16.6 us
  transfers between devices with their start and end apart: 18, of which 12 were waited for; matrix products, arithmetic and copies ran while one was open for 0% of the time, Pallas kernels for 2%

profile of v2, /device:TPU:0, one launch (start us, length us, event | category | flops | bytes accessed | tf_op | source)
XLA Modules:
  0.0 85.6 jit_solution(17361719123715742792)
XLA Ops:
  0.7 0.1 pad_add_fusion.place_ref
  0.8 4.3 %shard_map.49 = (f32[128,256]{1,0:T(8,128)S(1)}, f32[128,256]{1,0:T(8,128)S(1)}, bf16[1024,256]{1,0:T(8,128)(2,1)S(1)}, bf16[1024,256]{1,0:T(8,128)(2,1)}, bf16[...) custom-call(s32[2]{0:T(128)S(1)} %pad_add_fusion.place_ref, ...), custom_call_target="tpu_custom_call" | custom-call | flops 536870912 | bytes 7077888 | tf_op jit(solution)/shard_map/pallas_call | solution.py:274
  5.1 3.1 %collective-permute-start = (f32[128,256]{1,0:T(8,128)S(1)}, f32[128,256]{1,0:T(8,128)S(1)}, u32[]{:S(2)}, u32[]{:S(2)}) collective-permute-start(f32[128,256]{1,0:T(8,128)S(1)} %get-tuple-element.19), channel_id=1, source_target_pairs={{0,4},{1,9},{2,6},{3,11},{4,0},{5,13},{6,2},{7,15},{8,12},{9,1},{1... | collective-permute-start | bytes 393224 | tf_op jit(solution)/shard_map/ppermute | solution.py:21
  8.1 2.9 %collective-permute-done = f32[128,256]{1,0:T(8,128)S(1)} collective-permute-done((f32[128,256]{1,0:T(8,128)S(1)}, f32[128,256]{1,0:T(8,128)S(1)}, u32[]{:S(2)}, u32[]{:S(2)}) %collective-permute-start) | collective-permute-done | bytes 131104 | tf_op jit(solution)/shard_map/ppermute | solution.py:21
  11.1 2.1 %collective-permute-start.1 = (f32[128,256]{1,0:T(8,128)S(1)}, f32[128,256]{1,0:T(8,128)S(1)}, u32[]{:S(2)}, u32[]{:S(2)}) collective-permute-start(f32[128,256]{1,0:T(8,128)S(1)} %add.44), channel_id=1, source_target_pairs={{0,8},{1,17},{2,10},{3,19},{4,12},{5,21},{6,14},{7,23},{8,0},{9,25... | collective-permute-start | bytes 393224 | tf_op jit(solution)/shard_map/ppermute | solution.py:21
  13.2 3.4 %collective-permute-done.1 = f32[128,256]{1,0:T(8,128)S(1)} collective-permute-done((f32[128,256]{1,0:T(8,128)S(1)}, f32[128,256]{1,0:T(8,128)S(1)}, u32[]{:S(2)}, u32[]{:S(2)}) %collective-permute-start.1) | collective-permute-done | bytes 131104 | tf_op jit(solution)/shard_map/ppermute | solution.py:21
  16.7 3.0 %collective-permute-start.2 = (f32[128,256]{1,0:T(8,128)S(1)}, f32[128,256]{1,0:T(8,128)S(1)}, u32[]{:S(2)}, u32[]{:S(2)}) collective-permute-start(f32[128,256]{1,0:T(8,128)S(1)} %add.45), channel_id=1, source_target_pairs={{0,16},{1,5},{2,18},{3,7},{4,20},{5,1},{6,22},{7,3},{8,24},{9,13},... | collective-permute-start | bytes 393224 | tf_op jit(solution)/shard_map/ppermute | solution.py:21
  19.7 2.9 %collective-permute-done.2 = f32[128,256]{1,0:T(8,128)S(1)} collective-permute-done((f32[128,256]{1,0:T(8,128)S(1)}, f32[128,256]{1,0:T(8,128)S(1)}, u32[]{:S(2)}, u32[]{:S(2)}) %collective-permute-start.2) | collective-permute-done | bytes 131104 | tf_op jit(solution)/shard_map/ppermute | solution.py:21
  22.7 1.6 %collective-permute-start.3 = (bf16[128,256]{1,0:T(8,128)(2,1)S(1)}, bf16[128,256]{1,0:T(8,128)(2,1)S(1)}, u32[]{:S(2)}, u32[]{:S(2)}) collective-permute-start(bf16[128,256]{1,0:T(8,128)(2,1)S(1)} %multiply_convert_fusion), channel_id=1, source_target_pairs={{0,4},{1,9},{2,6},{3,11},{4,0},{5,13},{6,2},{7,15},{8,12},{9,1},{1... | collective-permute-start | bytes 196616 | tf_op jit(solution)/shard_map/ppermute | solution.py:21
  24.3 1.5 %collective-permute-start.8 = (bf16[1024,256]{1,0:T(8,128)(2,1)}, bf16[1024,256]{1,0:T(8,128)(2,1)S(1)}, u32[]{:S(2)}, u32[]{:S(2)}) collective-permute-start(bf16[1024,256]{1,0:T(8,128)(2,1)} %get-tuple-element.23), channel_id=1, source_target_pairs={{0,2},{1,3},{2,0},{3,1},{4,6},{5,7},{6,4},{7,5},{8,10},{9,11},{10,... | collective-permute-start | bytes 1572872 | tf_op jit(solution)/shard_map/ppermute | solution.py:21
  25.7 0.4 collective-permute-start.9
  26.1 0.9 %collective-permute-done.3 = bf16[128,256]{1,0:T(8,128)(2,1)S(1)} collective-permute-done((bf16[128,256]{1,0:T(8,128)(2,1)S(1)}, bf16[128,256]{1,0:T(8,128)(2,1)S(1)}, u32[]{:S(2)}, u32[]{:S(2)}) %collective-permute-start.3) | collective-permute-done | bytes 65568 | tf_op jit(solution)/shard_map/ppermute | solution.py:21
  27.0 1.6 %collective-permute-start.6 = (bf16[256,256]{1,0:T(8,128)(2,1)S(1)}, bf16[256,256]{1,0:T(8,128)(2,1)S(1)}, u32[]{:S(2)}, u32[]{:S(2)}) collective-permute-start(bf16[256,256]{1,0:T(8,128)(2,1)S(1)} %pad_maximum_fusion.refs_0_), channel_id=1, source_target_pairs={{0,2},{1,3},{2,0},{3,1},{4,6},{5,7},{6,4},{7,5},{8,10},{9,11},{10,... | collective-permute-start | bytes 393224 | tf_op jit(solution)/shard_map/ppermute | solution.py:21
  28.6 24.3 %collective-permute-done.6.refs_0_ = bf16[256,256]{1,0:T(8,128)(2,1)S(1)} collective-permute-done((bf16[256,256]{1,0:T(8,128)(2,1)S(1)}, bf16[256,256]{1,0:T(8,128)(2,1)S(1)}, u32[]{:S(2)}, u32[]{:S(2)}) %collective-permute-start.6) | collective-permute-done | bytes 131104 | tf_op jit(solution)/shard_map/ppermute | solution.py:21
  52.9 1.6 %shard_map.50 = (f32[256,1024]{1,0:T(8,128)S(1)}, f32[256,256]{1,0:T(8,128)}) custom-call(s32[2]{0:T(128)S(1)} %pad_add_fusion.place_ref, bf16[256,256]{1,0:T(8,128)(2,1)S(1)} %pad_maximum_fusion.refs_0_, bf16[256,256]{1,0:T(8,128)(2,1)S(1)} %collective-permute-done.4.refs_1_, bf16[1024,256]{1,0:T(8,128)(2,1)S(1)} %get-tuple-element.20.refs_2_, ...), custom_call_target="tpu_custom_call" | custom-call | flops 268435456 | bytes 2621440 | tf_op jit(solution)/shard_map/pallas_call | solution.py:274
  54.5 2.1 %shard_map.51 = (bf16[256,1024]{1,0:T(8,128)(2,1)S(1)}, bf16[256,1024]{1,0:T(8,128)(2,1)S(1)}, f32[136,128]{1,0:T(8,128)S(1)}, f32[136,128]{1,0:T(8,128)S(1)}) custom-call(s32[2]{0:T(128)S(1)} %pad_add_fusion.place_ref, bf16[256,256]{1,0:T(8,128)(2,1)S(1)} %collective-permute-done.6.refs_0_, bf16[256,256]{1,0:T(8,128)(2,1)S(1)} %collective-permute-done.7.refs_1_, ...), custom_call_target="tpu_custom_call" | custom-call | flops 671088640 | bytes 4071424 | tf_op jit(solution)/shard_map/pallas_call | solution.py:274
  56.6 0.6 collective-permute-start.10
  57.2 0.9 %collective-permute-done.10 = f32[136,128]{1,0:T(8,128)S(1)} collective-permute-done((f32[136,128]{1,0:T(8,128)S(1)}, f32[136,128]{1,0:T(8,128)S(1)}, u32[]{:S(2)}, u32[]{:S(2)}) %collective-permute-start.10) | collective-permute-done | bytes 69664 | tf_op jit(solution)/shard_map/ppermute | solution.py:21
  58.1 0.6 collective-permute-start.12
  58.6 2.4 %collective-permute-start.13 = (f32[136,128]{1,0:T(8,128)S(1)}, f32[136,128]{1,0:T(8,128)S(1)}, u32[]{:S(2)}, u32[]{:S(2)}) collective-permute-start(f32[136,128]{1,0:T(8,128)S(1)} %add.47), channel_id=1, source_target_pairs={{0,6},{1,25},{2,4},{3,27},{4,2},{5,29},{6,0},{7,31},{8,14},{9,17},... | collective-permute-start | bytes 208904 | tf_op jit(solution)/shard_map/ppermute | solution.py:21
  61.1 0.5 collective-permute-start.11
  61.6 0.8 collective-permute-done.12
  62.5 1.4 %collective-permute-done.13 = f32[136,128]{1,0:T(8,128)S(1)} collective-permute-done((f32[136,128]{1,0:T(8,128)S(1)}, f32[136,128]{1,0:T(8,128)S(1)}, u32[]{:S(2)}, u32[]{:S(2)}) %collective-permute-start.13) | collective-permute-done | bytes 69664 | tf_op jit(solution)/shard_map/ppermute | solution.py:21
  63.9 1.5 %collective-permute-done.11 = f32[136,128]{1,0:T(8,128)S(1)} collective-permute-done((f32[136,128]{1,0:T(8,128)S(1)}, f32[136,128]{1,0:T(8,128)S(1)}, u32[]{:S(2)}, u32[]{:S(2)}) %collective-permute-start.11) | collective-permute-done | bytes 69664 | tf_op jit(solution)/shard_map/ppermute | solution.py:21
  65.4 3.3 %collective-permute-start.15 = (f32[136,128]{1,0:T(8,128)S(1)}, f32[136,128]{1,0:T(8,128)S(1)}, u32[]{:S(2)}, u32[]{:S(2)}) collective-permute-start(f32[136,128]{1,0:T(8,128)S(1)} %add_add_fusion.1), channel_id=1, source_target_pairs={{0,16},{1,5},{2,18},{3,7},{4,20},{5,1},{6,22},{7,3},{8,24},{9,13},... | collective-permute-start | bytes 208904 | tf_op jit(solution)/shard_map/ppermute | solution.py:21
  68.8 2.1 %collective-permute-start.16 = (f32[136,128]{1,0:T(8,128)S(1)}, f32[136,128]{1,0:T(8,128)S(1)}, u32[]{:S(2)}, u32[]{:S(2)}) collective-permute-start(f32[136,128]{1,0:T(8,128)S(1)} %add_add_fusion.1), channel_id=1, source_target_pairs={{0,24},{1,7},{2,26},{3,5},{4,28},{5,3},{6,30},{7,1},{8,16},{9,15},... | collective-permute-start | bytes 208904 | tf_op jit(solution)/shard_map/ppermute | solution.py:21
  70.9 0.5 collective-permute-start.14
  71.4 3.5 %collective-permute-done.16 = f32[136,128]{1,0:T(8,128)S(1)} collective-permute-done((f32[136,128]{1,0:T(8,128)S(1)}, f32[136,128]{1,0:T(8,128)S(1)}, u32[]{:S(2)}, u32[]{:S(2)}) %collective-permute-start.16) | collective-permute-done | bytes 69664 | tf_op jit(solution)/shard_map/ppermute | solution.py:21
  74.9 0.7 collective-permute-done.14
  75.6 0.1 collective-permute-start.17
  75.7 1.2 %collective-permute-done.17.other_ref = f32[136,128]{1,0:T(8,128)S(1)} collective-permute-done((f32[136,128]{1,0:T(8,128)S(1)}, f32[136,128]{1,0:T(8,128)S(1)}, u32[]{:S(2)}, u32[]{:S(2)}) %collective-permute-start.17) | collective-permute-done | bytes 69664 | tf_op jit(solution)/shard_map/ppermute | solution.py:21
  77.0 8.6 %shard_map.52 = (f32[256,256]{1,0:T(8,128)}, bf16[256,1024]{1,0:T(8,128)(2,1)}) custom-call(s32[2]{0:T(128)S(1)} %pad_add_fusion.place_ref, f32[136,128]{1,0:T(8,128)S(1)} %add_add_fusion.mine_ref, f32[136,128]{1,0:T(8,128)S(1)} %collective-permute-done.17.other_ref, bf16[256,1024]{1,0:T(8,128)(2,1)S(1)} %get-tuple-element.29.high_ref, ...), custom_call_target="tpu_custom_call" | custom-call | flops 402653184 | bytes 1974272 | tf_op jit(solution)/shard_map/pallas_call | solution.py:274
  (17 shorter events, 0.1 us)
Async XLA Ops:
  5.1 6.0 %collective-permute-start = (f32[128,256]{1,0:T(8,128)S(1)}, f32[128,256]{1,0:T(8,128)S(1)}, u32[]{:S(2)}, u32[]{:S(2)}) collective-permute-start(f32[128,256]{1,0:T(8,128)S(1)} %get-tuple-element.19), channel_id=1, source_target_pairs={{0,4},{1,9},{2,6},{3,11},{4,0},{5,13},{6,2},{7,15},{8,12},{9,1},{1... | collective-permute-start | bytes 393224 | tf_op jit(solution)/shard_map/ppermute | solution.py:21
  11.1 5.6 %collective-permute-start.1 = (f32[128,256]{1,0:T(8,128)S(1)}, f32[128,256]{1,0:T(8,128)S(1)}, u32[]{:S(2)}, u32[]{:S(2)}) collective-permute-start(f32[128,256]{1,0:T(8,128)S(1)} %add.44), channel_id=1, source_target_pairs={{0,8},{1,17},{2,10},{3,19},{4,12},{5,21},{6,14},{7,23},{8,0},{9,25... | collective-permute-start | bytes 393224 | tf_op jit(solution)/shard_map/ppermute | solution.py:21
  16.7 6.0 %collective-permute-start.2 = (f32[128,256]{1,0:T(8,128)S(1)}, f32[128,256]{1,0:T(8,128)S(1)}, u32[]{:S(2)}, u32[]{:S(2)}) collective-permute-start(f32[128,256]{1,0:T(8,128)S(1)} %add.45), channel_id=1, source_target_pairs={{0,16},{1,5},{2,18},{3,7},{4,20},{5,1},{6,22},{7,3},{8,24},{9,13},... | collective-permute-start | bytes 393224 | tf_op jit(solution)/shard_map/ppermute | solution.py:21
  22.7 4.3 %collective-permute-start.3 = (bf16[128,256]{1,0:T(8,128)(2,1)S(1)}, bf16[128,256]{1,0:T(8,128)(2,1)S(1)}, u32[]{:S(2)}, u32[]{:S(2)}) collective-permute-start(bf16[128,256]{1,0:T(8,128)(2,1)S(1)} %multiply_convert_fusion), channel_id=1, source_target_pairs={{0,4},{1,9},{2,6},{3,11},{4,0},{5,13},{6,2},{7,15},{8,12},{9,1},{1... | collective-permute-start | bytes 196616 | tf_op jit(solution)/shard_map/ppermute | solution.py:21
  24.3 28.6 %collective-permute-start.5 = (bf16[1024,256]{1,0:T(8,128)(2,1)}, bf16[1024,256]{1,0:T(8,128)(2,1)S(1)}, u32[]{:S(2)}, u32[]{:S(2)}) collective-permute-start(bf16[1024,256]{1,0:T(8,128)(2,1)} %get-tuple-element.21), channel_id=1, source_target_pairs={{0,1},{1,0},{2,3},{3,2},{4,5},{5,4},{6,7},{7,6},{8,9},{9,8},{10,11... | collective-permute-start | bytes 1572872 | tf_op jit(solution)/shard_map/ppermute | solution.py:21
  24.3 30.2 %collective-permute-start.8 = (bf16[1024,256]{1,0:T(8,128)(2,1)}, bf16[1024,256]{1,0:T(8,128)(2,1)S(1)}, u32[]{:S(2)}, u32[]{:S(2)}) collective-permute-start(bf16[1024,256]{1,0:T(8,128)(2,1)} %get-tuple-element.23), channel_id=1, source_target_pairs={{0,2},{1,3},{2,0},{3,1},{4,6},{5,7},{6,4},{7,5},{8,10},{9,11},{10,... | collective-permute-start | bytes 1572872 | tf_op jit(solution)/shard_map/ppermute | solution.py:21
  25.7 28.7 %collective-permute-start.9 = (bf16[1024,256]{1,0:T(8,128)(2,1)S(1)}, bf16[1024,256]{1,0:T(8,128)(2,1)S(1)}, u32[]{:S(2)}, u32[]{:S(2)}) collective-permute-start(bf16[1024,256]{1,0:T(8,128)(2,1)S(1)} %get-tuple-element.24), channel_id=1, source_target_pairs={{0,3},{1,2},{2,1},{3,0},{4,7},{5,6},{6,5},{7,4},{8,11},{9,10},{10,... | collective-permute-start | bytes 1572872 | tf_op jit(solution)/shard_map/ppermute | solution.py:21
  27.0 25.8 %collective-permute-start.6 = (bf16[256,256]{1,0:T(8,128)(2,1)S(1)}, bf16[256,256]{1,0:T(8,128)(2,1)S(1)}, u32[]{:S(2)}, u32[]{:S(2)}) collective-permute-start(bf16[256,256]{1,0:T(8,128)(2,1)S(1)} %pad_maximum_fusion.refs_0_), channel_id=1, source_target_pairs={{0,2},{1,3},{2,0},{3,1},{4,6},{5,7},{6,4},{7,5},{8,10},{9,11},{10,... | collective-permute-start | bytes 393224 | tf_op jit(solution)/shard_map/ppermute | solution.py:21
  28.6 24.3 %collective-permute-start.4 = (bf16[256,256]{1,0:T(8,128)(2,1)S(1)}, bf16[256,256]{1,0:T(8,128)(2,1)S(1)}, u32[]{:S(2)}, u32[]{:S(2)}) collective-permute-start(bf16[256,256]{1,0:T(8,128)(2,1)S(1)} %pad_maximum_fusion.refs_0_), channel_id=1, source_target_pairs={{0,1},{1,0},{2,3},{3,2},{4,5},{5,4},{6,7},{7,6},{8,9},{9,8},{10,11... | collective-permute-start | bytes 393224 | tf_op jit(solution)/shard_map/ppermute | solution.py:21
  52.8 1.7 %collective-permute-start.7 = (bf16[256,256]{1,0:T(8,128)(2,1)S(1)}, bf16[256,256]{1,0:T(8,128)(2,1)S(1)}, u32[]{:S(2)}, u32[]{:S(2)}) collective-permute-start(bf16[256,256]{1,0:T(8,128)(2,1)S(1)} %collective-permute-done.6.refs_0_), channel_id=1, source_target_pairs={{0,1},{1,0},{2,3},{3,2},{4,5},{5,4},{6,7},{7,6},{8,9},{9,8},{10,11... | collective-permute-start | bytes 393224 | tf_op jit(solution)/shard_map/ppermute | solution.py:21
  56.6 1.5 %collective-permute-start.10 = (f32[136,128]{1,0:T(8,128)S(1)}, f32[136,128]{1,0:T(8,128)S(1)}, u32[]{:S(2)}, u32[]{:S(2)}) collective-permute-start(f32[136,128]{1,0:T(8,128)S(1)} %get-tuple-element.28), channel_id=1, source_target_pairs={{0,1},{1,0},{2,3},{3,2},{4,5},{5,4},{6,7},{7,6},{8,9},{9,8},{10,11... | collective-permute-start | bytes 208904 | tf_op jit(solution)/shard_map/ppermute | solution.py:21
  58.1 4.4 %collective-permute-start.12 = (f32[136,128]{1,0:T(8,128)S(1)}, f32[136,128]{1,0:T(8,128)S(1)}, u32[]{:S(2)}, u32[]{:S(2)}) collective-permute-start(f32[136,128]{1,0:T(8,128)S(1)} %add.47), channel_id=1, source_target_pairs={{0,4},{1,17},{2,6},{3,19},{4,0},{5,21},{6,2},{7,23},{8,12},{9,25},... | collective-permute-start | bytes 208904 | tf_op jit(solution)/shard_map/ppermute | solution.py:21
  58.6 5.2 %collective-permute-start.13 = (f32[136,128]{1,0:T(8,128)S(1)}, f32[136,128]{1,0:T(8,128)S(1)}, u32[]{:S(2)}, u32[]{:S(2)}) collective-permute-start(f32[136,128]{1,0:T(8,128)S(1)} %add.47), channel_id=1, source_target_pairs={{0,6},{1,25},{2,4},{3,27},{4,2},{5,29},{6,0},{7,31},{8,14},{9,17},... | collective-permute-start | bytes 208904 | tf_op jit(solution)/shard_map/ppermute | solution.py:21
  61.1 4.3 %collective-permute-start.11 = (f32[136,128]{1,0:T(8,128)S(1)}, f32[136,128]{1,0:T(8,128)S(1)}, u32[]{:S(2)}, u32[]{:S(2)}) collective-permute-start(f32[136,128]{1,0:T(8,128)S(1)} %add.47), channel_id=1, source_target_pairs={{0,2},{1,9},{2,0},{3,11},{4,6},{5,13},{6,4},{7,15},{8,10},{9,1},{1... | collective-permute-start | bytes 208904 | tf_op jit(solution)/shard_map/ppermute | solution.py:21
  65.4 6.0 %collective-permute-start.15 = (f32[136,128]{1,0:T(8,128)S(1)}, f32[136,128]{1,0:T(8,128)S(1)}, u32[]{:S(2)}, u32[]{:S(2)}) collective-permute-start(f32[136,128]{1,0:T(8,128)S(1)} %add_add_fusion.1), channel_id=1, source_target_pairs={{0,16},{1,5},{2,18},{3,7},{4,20},{5,1},{6,22},{7,3},{8,24},{9,13},... | collective-permute-start | bytes 208904 | tf_op jit(solution)/shard_map/ppermute | solution.py:21
  68.8 6.2 %collective-permute-start.16 = (f32[136,128]{1,0:T(8,128)S(1)}, f32[136,128]{1,0:T(8,128)S(1)}, u32[]{:S(2)}, u32[]{:S(2)}) collective-permute-start(f32[136,128]{1,0:T(8,128)S(1)} %add_add_fusion.1), channel_id=1, source_target_pairs={{0,24},{1,7},{2,26},{3,5},{4,28},{5,3},{6,30},{7,1},{8,16},{9,15},... | collective-permute-start | bytes 208904 | tf_op jit(solution)/shard_map/ppermute | solution.py:21
  70.9 4.7 %collective-permute-start.14 = (f32[136,128]{1,0:T(8,128)S(1)}, f32[136,128]{1,0:T(8,128)S(1)}, u32[]{:S(2)}, u32[]{:S(2)}) collective-permute-start(f32[136,128]{1,0:T(8,128)S(1)} %add_add_fusion.1), channel_id=1, source_target_pairs={{0,8},{1,3},{2,10},{3,1},{4,12},{5,7},{6,14},{7,5},{8,0},{9,11},{1... | collective-permute-start | bytes 208904 | tf_op jit(solution)/shard_map/ppermute | solution.py:21
  75.6 1.3 %collective-permute-start.17 = (f32[136,128]{1,0:T(8,128)S(1)}, f32[136,128]{1,0:T(8,128)S(1)}, u32[]{:S(2)}, u32[]{:S(2)}) collective-permute-start(f32[136,128]{1,0:T(8,128)S(1)} %add_add_fusion.mine_ref), channel_id=1, source_target_pairs={{0,1},{1,0},{2,3},{3,2},{4,5},{5,4},{6,7},{7,6},{8,9},{9,8},{10,11... | collective-permute-start | bytes 208904 | tf_op jit(solution)/shard_map/ppermute | solution.py:21

commit v3 on v1

--- a/solution.py
+++ b/solution.py
@@ -27,6 +27,13 @@
         found.append(step)
         step, count = 2 * step, count // 2
     return found
+
+
+def exchange_rounds(masks):
+    rounds = [(masks[at], masks[at + 1] if at + 1 < len(masks) else 0) for at in range(0, len(masks), 2)]
+    paired = [pair for pair in rounds if pair[1]]
+    single = [pair for pair in rounds if not pair[1]]
+    return paired + single, paired[::-1] + single
 
 
 def wide_split(value):
@@ -61,9 +68,9 @@
 
 
 def project_kernel(place_ref, basis_ref, snaps_ref, *refs):
-    count = (len(refs) - 3) // 2
+    count = (len(refs) - 4) // 2
     far_refs = refs[: count - 2]
-    keep_ref, send_ref, own_ref, near_ref = refs[count - 2 : count + 2]
+    keep_ref, send_ref, near_ref, own_ref = refs[count - 2 : count + 2]
     part_refs, basis_sem, snaps_sem = refs[count + 2 : -2], refs[-2], refs[-1]
     basis_copies = slab_copies(place_ref, basis_ref, (own_ref, near_ref), basis_sem, 0, True)
     snaps_copies = slab_copies(place_ref, snaps_ref, part_refs, snaps_sem, 0, False)
@@ -85,13 +92,15 @@
     send_ref[...] = jnp.where(odd, first, second)
 
 
-def recon_kernel(place_ref, *refs):
-    recon_ref, coefficients_ref = refs[-2:]
-    coefficients_ref[...] = refs[0][...].astype(jnp.float32).T
+def recon_kernel(place_ref, basis_ref, low_ref, near_low_ref, near_ref, recon_ref, coefficients_ref, own_ref, sem_ref):
+    (copy,) = slab_copies(place_ref, basis_ref, (own_ref,), sem_ref, 0, True)
+    copy.start()
+    coefficients_ref[...] = low_ref[...].astype(jnp.float32).T
+    copy.wait()
     chunk = 256
     for start in range(0, recon_ref.shape[1], chunk):
         cols = slice(start, start + chunk)
-        recon_ref[:, cols] = nt_dot(refs[0][...], refs[2][cols, :]) + nt_dot(refs[1][...], refs[3][cols, :])
+        recon_ref[:, cols] = nt_dot(low_ref[...], own_ref[cols, :]) + nt_dot(near_low_ref[...], near_ref[cols, :])
 
 
 def packed_rows(tiles):
@@ -114,10 +123,12 @@
     return lax.broadcasted_iota(jnp.int32, (LANES, LANES), dim)
 
 
-def residual_kernel(total_points, place_ref, *refs):
-    count = (len(refs) - 7) // 2
+def residual_kernel(total_points, place_ref, whole_ref, *refs):
+    count = (len(refs) - 8) // 2
     low_refs, basis_refs = refs[:count], refs[count : 2 * count]
-    begun_ref, snaps_ref, high_ref, rest_ref, keep_ref, send_ref, pack_ref = refs[2 * count :]
+    begun_ref, high_ref, rest_ref, keep_ref, send_ref, pack_ref, snaps_ref, sem_ref = refs[2 * count :]
+    (copy,) = slab_copies(place_ref, whole_ref, (snaps_ref,), sem_ref, 0, False)
+    copy.start()
     snaps, points = snaps_ref.shape
     chunk = 256
     for start in range(0, points, chunk):
@@ -125,6 +136,8 @@
         recon = begun_ref[:, cols]
         for low_ref, basis_ref in zip(low_refs, basis_refs):
             recon += nt_dot(low_ref[...], basis_ref[cols, :])
+        if start == 0:
+            copy.wait()
         residual = snaps_ref[:, cols].astype(jnp.float32) - recon * (1.0 / math.sqrt(RANK))
         high, rest = wide_split(residual)
         high_ref[:, cols] = high
@@ -310,15 +323,15 @@
     odd = (flat // jnp.where(column_index % 2 == 0, sum_steps[0][0], sum_steps[0][1])) % 2
     place = jnp.stack([column_index, odd]).astype(jnp.int32)
 
-    slab = shape(bf16, points, modes)
+    slab, part = shape(bf16, points, modes), shape(f32, half, modes)
+    slab_scratch, span_scratch = pltpu.VMEM((points, modes), bf16), pltpu.VMEM((snaps, points), bf16)
     semaphores = pltpu.SemaphoreType.DMA((columns,))
-    far_slabs = call(slab_kernel, (slab,) * (columns - 2), [semaphores], 0, 8, 1)(place, basis_cols)
+    far_slabs = call(slab_kernel, (slab,) * (columns - 2), [semaphores], 0, 4, 1)(place, basis_cols)
     arrived_slabs = [swap(far_slabs[at], (2 + at,) * 2) for at in range(columns - 2)]
-    part = shape(f32, half, modes)
-    kept, sent, own_slab, near_slab, own_snaps = call(
+    kept, sent, near_slab = call(
         project_kernel,
-        (part, part, slab, slab, shape(bf16, snaps, points)),
-        [pltpu.VMEM((snaps, points), bf16)] * (columns - 1) + [semaphores, semaphores],
+        (part, part, slab),
+        [slab_scratch] + [span_scratch] * columns + [semaphores, semaphores],
         2 * snaps * row_points * modes,
         12,
         2,
@@ -329,34 +342,41 @@
     for step in sum_steps[1:]:
         kept = kept + swap(kept, step)
     low = (kept * (math.sqrt(RANK) / total_points)).astype(bf16)
-    lows = {}
+    other = swap(low, sum_steps[0])
+    low = jnp.concatenate([jnp.where(odd == 1, other, low), jnp.where(odd == 1, low, other)], 0)
+    lows = {0: low}
+    for offset in range(2, columns, 2):
+        lows[offset] = swap(low, (offset, offset))
     for offset in range(0, columns, 2):
-        own = swap(low, (offset, offset)) if offset else low
-        other = swap(low, tuple(mask ^ offset for mask in sum_steps[0]))
-        lows[offset] = jnp.concatenate([jnp.where(odd == 1, other, own), jnp.where(odd == 1, own, other)], 0)
         lows[offset + 1] = swap(lows[offset], (1, 1))
 
     begun, coefficients = call(
-        recon_kernel, (shape(f32, snaps, points), shape(f32, modes, snaps)), [], 4 * snaps * points * modes, 8
-    )(place, lows[0], lows[1], own_slab, near_slab)
+        recon_kernel,
+        (shape(f32, snaps, points), shape(f32, modes, snaps)),
+        [slab_scratch, semaphores],
+        4 * snaps * points * modes,
+        8,
+        1,
+    )(place, basis_cols, lows[0], lows[1], near_slab)
     packed = packed_rows(snaps // LANES)
     part = shape(f32, packed // 2, LANES)
     wide = shape(bf16, snaps, points)
     high, rest, keep, send = call(
         functools.partial(residual_kernel, total_points),
         (wide, wide, part, part),
-        [pltpu.VMEM((packed, LANES), f32)],
+        [pltpu.VMEM((packed, LANES), f32), span_scratch, semaphores],
         2 * snaps * points * (modes * (columns - 2) + 3 * snaps),
         16,
-    )(place, *[lows[offset] for offset in range(2, columns)], *arrived_slabs, begun, own_snaps)
+        1,
+    )(place, snapshots, *[lows[offset] for offset in range(2, columns)], *arrived_slabs, begun)
     keep = keep + swap(send, (1, 1))
-    rest_bits = bits(columns // 2, 2) + row_bits
-    first_order = rest_bits[-1:] + rest_bits[:-1]
-    second_order = list(first_order)
-    for at in range(0, len(first_order) - 1, 2):
-        second_order[at : at + 2] = reversed(first_order[at : at + 2])
-    for step in zip(first_order, second_order):
-        keep = keep + swap(keep, step)
+    for masks in zip(*exchange_rounds(bits(columns // 2, 2) + row_bits)):
+        if masks[0][1] == 0:
+            keep = keep + swap(keep, [mask[0] for mask in masks])
+            continue
+        far = swap(keep, [mask[1] for mask in masks])
+        diagonal = swap(keep, [mask[0] ^ mask[1] for mask in masks])
+        keep = (keep + swap(keep, [mask[0] for mask in masks])) + (far + diagonal)
     rest_of_gram = swap(keep, (1, 1))
     factor, directions = call(
         factor_kernel,

time: 88.6 us -> 83.9 us (0.947)
  waiting for transfers between devices: 48 us -> 41.9 us
  starting transfers between devices: 20.4 us -> 21.8 us
    ppermute x17 -> x18, waiting for transfers between devices: 48 us -> 41.9 us  [swap(): lax.ppermute(value, ('rows', 'cols'), [(i, i ^ masks[i % 2]) for i in ran...]
    ppermute x17 -> x18, starting transfers between devices: 20.4 us -> 21.8 us  [swap(): lax.ppermute(value, ('rows', 'cols'), [(i, i ^ masks[i % 2]) for i in ran...]
  transfers between devices with their start and end apart: 17 -> 18, of which waited for: 11 -> 12; matrix products, arithmetic and copies ran while one was open for 0% -> 0% of each run, Pallas kernels for 2% -> 3%
where the time goes in v3:
time: 83.9 us; the launch traced here: 83.6 us
  waiting for transfers between devices  41.9 us (50%)
  starting transfers between devices  21.8 us (26%)
  Pallas kernels  19 us (23%)
    ppermute x18, waiting for transfers between devices, swap(): lax.ppermute(value, ('rows', 'cols'), [(i, i ^ masks[i % 2]) for i in ran...  41.9 us
    ppermute x18, starting transfers between devices, swap(): lax.ppermute(value, ('rows', 'cols'), [(i, i ^ masks[i % 2]) for i in ran...  21.8 us
    pallas_call x5, Pallas kernels, run(): pl.pallas_call(kernel, out_shape=outs, in_specs=[smem] + [hbm] * whole +...  19 us
  transfers between devices with their start and end apart: 18, of which 12 were waited for; matrix products, arithmetic and copies ran while one was open for 0% of the time, Pallas kernels for 3%

profile of v3, /device:TPU:0, one launch (start us, length us, event | category | flops | bytes accessed | tf_op | source)
XLA Modules:
  0.0 83.6 jit_solution(12133268690759628259)
XLA Ops:
  0.7 0.1 pad_add_fusion.place_ref
  0.8 1.8 %shard_map.49 = (bf16[1024,256]{1,0:T(8,128)(2,1)S(1)}, bf16[1024,256]{1,0:T(8,128)(2,1)S(1)}) custom-call(s32[2]{0:T(128)S(1)} %pad_add_fusion.place_ref, bf16[4096,256]{1,0:T(8,128)(2,1)} %basis_ref.5), custom_call_target="tpu_custom_call" | custom-call | bytes 3145728 | tf_op jit(solution)/shard_map/pallas_call | solution.py:293
  2.5 3.2 %shard_map.50 = (f32[128,256]{1,0:T(8,128)S(1)}, f32[128,256]{1,0:T(8,128)S(1)}, bf16[1024,256]{1,0:T(8,128)(2,1)S(1)}) custom-call(s32[2]{0:T(128)S(1)} %pad_add_fusion.place_ref, bf16[4096,256]{1,0:T(8,128)(2,1)} %basis_ref.5, bf16[256,4096]{1,0:T(8,128)(2,1)} %whole_ref.1, bf16[1024,256]{1,0:T(8,128)(2,1)S(1)} %get-tuple-element.16.refs_0_, ...), custom_call_target="tpu_custom_call" | custom-call | flops 536870912 | bytes 6029312 | tf_op jit(solution)/shard_map/pallas_call | solution.py:293
  5.8 3.1 %collective-permute-start = (f32[128,256]{1,0:T(8,128)S(1)}, f32[128,256]{1,0:T(8,128)S(1)}, u32[]{:S(2)}, u32[]{:S(2)}) collective-permute-start(f32[128,256]{1,0:T(8,128)S(1)} %get-tuple-element.19), channel_id=1, source_target_pairs={{0,4},{1,9},{2,6},{3,11},{4,0},{5,13},{6,2},{7,15},{8,12},{9,1},{1... | collective-permute-start | bytes 393224 | tf_op jit(solution)/shard_map/ppermute | solution.py:21
  8.9 2.9 %collective-permute-done = f32[128,256]{1,0:T(8,128)S(1)} collective-permute-done((f32[128,256]{1,0:T(8,128)S(1)}, f32[128,256]{1,0:T(8,128)S(1)}, u32[]{:S(2)}, u32[]{:S(2)}) %collective-permute-start) | collective-permute-done | bytes 131104 | tf_op jit(solution)/shard_map/ppermute | solution.py:21
  11.8 2.1 %collective-permute-start.1 = (f32[128,256]{1,0:T(8,128)S(1)}, f32[128,256]{1,0:T(8,128)S(1)}, u32[]{:S(2)}, u32[]{:S(2)}) collective-permute-start(f32[128,256]{1,0:T(8,128)S(1)} %add.44), channel_id=1, source_target_pairs={{0,8},{1,17},{2,10},{3,19},{4,12},{5,21},{6,14},{7,23},{8,0},{9,25... | collective-permute-start | bytes 393224 | tf_op jit(solution)/shard_map/ppermute | solution.py:21
  14.0 3.4 %collective-permute-done.1 = f32[128,256]{1,0:T(8,128)S(1)} collective-permute-done((f32[128,256]{1,0:T(8,128)S(1)}, f32[128,256]{1,0:T(8,128)S(1)}, u32[]{:S(2)}, u32[]{:S(2)}) %collective-permute-start.1) | collective-permute-done | bytes 131104 | tf_op jit(solution)/shard_map/ppermute | solution.py:21
  17.4 3.0 %collective-permute-start.2 = (f32[128,256]{1,0:T(8,128)S(1)}, f32[128,256]{1,0:T(8,128)S(1)}, u32[]{:S(2)}, u32[]{:S(2)}) collective-permute-start(f32[128,256]{1,0:T(8,128)S(1)} %add.45), channel_id=1, source_target_pairs={{0,16},{1,5},{2,18},{3,7},{4,20},{5,1},{6,22},{7,3},{8,24},{9,13},... | collective-permute-start | bytes 393224 | tf_op jit(solution)/shard_map/ppermute | solution.py:21
  20.4 2.9 %collective-permute-done.2 = f32[128,256]{1,0:T(8,128)S(1)} collective-permute-done((f32[128,256]{1,0:T(8,128)S(1)}, f32[128,256]{1,0:T(8,128)S(1)}, u32[]{:S(2)}, u32[]{:S(2)}) %collective-permute-start.2) | collective-permute-done | bytes 131104 | tf_op jit(solution)/shard_map/ppermute | solution.py:21
  23.4 1.6 %collective-permute-start.3 = (bf16[128,256]{1,0:T(8,128)(2,1)S(1)}, bf16[128,256]{1,0:T(8,128)(2,1)S(1)}, u32[]{:S(2)}, u32[]{:S(2)}) collective-permute-start(bf16[128,256]{1,0:T(8,128)(2,1)S(1)} %multiply_convert_fusion), channel_id=1, source_target_pairs={{0,4},{1,9},{2,6},{3,11},{4,0},{5,13},{6,2},{7,15},{8,12},{9,1},{1... | collective-permute-start | bytes 196616 | tf_op jit(solution)/shard_map/ppermute | solution.py:21
  25.0 1.5 %collective-permute-start.8 = (bf16[1024,256]{1,0:T(8,128)(2,1)S(1)}, bf16[1024,256]{1,0:T(8,128)(2,1)S(1)}, u32[]{:S(2)}, u32[]{:S(2)}) collective-permute-start(bf16[1024,256]{1,0:T(8,128)(2,1)S(1)} %get-tuple-element.16.refs_0_), channel_id=1, source_target_pairs={{0,2},{1,3},{2,0},{3,1},{4,6},{5,7},{6,4},{7,5},{8,10},{9,11},{10,... | collective-permute-start | bytes 1572872 | tf_op jit(solution)/shard_map/ppermute | solution.py:21
  26.5 0.6 collective-permute-start.5
  27.1 0.6 collective-permute-done.3
  27.8 1.6 %collective-permute-start.6 = (bf16[256,256]{1,0:T(8,128)(2,1)S(1)}, bf16[256,256]{1,0:T(8,128)(2,1)S(1)}, u32[]{:S(2)}, u32[]{:S(2)}) collective-permute-start(bf16[256,256]{1,0:T(8,128)(2,1)S(1)} %pad_maximum_fusion.low_ref), channel_id=1, source_target_pairs={{0,2},{1,3},{2,0},{3,1},{4,6},{5,7},{6,4},{7,5},{8,10},{9,11},{10,... | collective-permute-start | bytes 393224 | tf_op jit(solution)/shard_map/ppermute | solution.py:21
  29.3 20.7 %collective-permute-done.6.refs_0_ = bf16[256,256]{1,0:T(8,128)(2,1)S(1)} collective-permute-done((bf16[256,256]{1,0:T(8,128)(2,1)S(1)}, bf16[256,256]{1,0:T(8,128)(2,1)S(1)}, u32[]{:S(2)}, u32[]{:S(2)}) %collective-permute-start.6) | collective-permute-done | bytes 131104 | tf_op jit(solution)/shard_map/ppermute | solution.py:21
  50.1 2.3 %shard_map.51 = (f32[256,1024]{1,0:T(8,128)S(1)}, f32[256,256]{1,0:T(8,128)}) custom-call(s32[2]{0:T(128)S(1)} %pad_add_fusion.place_ref, bf16[4096,256]{1,0:T(8,128)(2,1)} %basis_ref.5, bf16[256,256]{1,0:T(8,128)(2,1)S(1)} %pad_maximum_fusion.low_ref, bf16[256,256]{1,0:T(8,128)(2,1)S(1)} %collective-permute-done.4.near_low_ref, ...), custom_call_target="tpu_custom_call" | custom-call | flops 268435456 | bytes 4194304 | tf_op jit(solution)/shard_map/pallas_call | solution.py:293
  52.4 3.0 %shard_map.52 = (bf16[256,1024]{1,0:T(8,128)(2,1)S(1)}, bf16[256,1024]{1,0:T(8,128)(2,1)S(1)}, f32[136,128]{1,0:T(8,128)S(1)}, f32[136,128]{1,0:T(8,128)S(1)}) custom-call(s32[2]{0:T(128)S(1)} %pad_add_fusion.place_ref, bf16[256,4096]{1,0:T(8,128)(2,1)} %whole_ref.1, bf16[256,256]{1,0:T(8,128)(2,1)S(1)} %collective-permute-done.6.refs_0_, ...), custom_call_target="tpu_custom_call" | custom-call | flops 671088640 | bytes 5644288 | tf_op jit(solution)/shard_map/pallas_call | solution.py:293
  55.5 0.6 collective-permute-start.10
  56.0 0.9 %collective-permute-done.10 = f32[136,128]{1,0:T(8,128)S(1)} collective-permute-done((f32[136,128]{1,0:T(8,128)S(1)}, f32[136,128]{1,0:T(8,128)S(1)}, u32[]{:S(2)}, u32[]{:S(2)}) %collective-permute-start.10) | collective-permute-done | bytes 69664 | tf_op jit(solution)/shard_map/ppermute | solution.py:21
  57.0 1.6 %collective-permute-start.12 = (f32[136,128]{1,0:T(8,128)S(1)}, f32[136,128]{1,0:T(8,128)S(1)}, u32[]{:S(2)}, u32[]{:S(2)}) collective-permute-start(f32[136,128]{1,0:T(8,128)S(1)} %add.47), channel_id=1, source_target_pairs={{0,4},{1,17},{2,6},{3,19},{4,0},{5,21},{6,2},{7,23},{8,12},{9,25},... | collective-permute-start | bytes 208904 | tf_op jit(solution)/shard_map/ppermute | solution.py:21
  58.5 1.4 %collective-permute-start.13 = (f32[136,128]{1,0:T(8,128)S(1)}, f32[136,128]{1,0:T(8,128)S(1)}, u32[]{:S(2)}, u32[]{:S(2)}) collective-permute-start(f32[136,128]{1,0:T(8,128)S(1)} %add.47), channel_id=1, source_target_pairs={{0,6},{1,25},{2,4},{3,27},{4,2},{5,29},{6,0},{7,31},{8,14},{9,17},... | collective-permute-start | bytes 208904 | tf_op jit(solution)/shard_map/ppermute | solution.py:21
  60.0 0.5 collective-permute-start.11
  60.5 0.8 collective-permute-done.12
  61.3 2.4 %collective-permute-done.13 = f32[136,128]{1,0:T(8,128)S(1)} collective-permute-done((f32[136,128]{1,0:T(8,128)S(1)}, f32[136,128]{1,0:T(8,128)S(1)}, u32[]{:S(2)}, u32[]{:S(2)}) %collective-permute-start.13) | collective-permute-done | bytes 69664 | tf_op jit(solution)/shard_map/ppermute | solution.py:21
  63.7 0.5 collective-permute-done.11
  64.3 3.2 %collective-permute-start.15 = (f32[136,128]{1,0:T(8,128)S(1)}, f32[136,128]{1,0:T(8,128)S(1)}, u32[]{:S(2)}, u32[]{:S(2)}) collective-permute-start(f32[136,128]{1,0:T(8,128)S(1)} %add_add_fusion.1), channel_id=1, source_target_pairs={{0,16},{1,5},{2,18},{3,7},{4,20},{5,1},{6,22},{7,3},{8,24},{9,13},... | collective-permute-start | bytes 208904 | tf_op jit(solution)/shard_map/ppermute | solution.py:21
  67.5 0.3 collective-permute-start.16
  67.9 0.5 collective-permute-start.14
  68.4 2.2 %collective-permute-done.15 = f32[136,128]{1,0:T(8,128)S(1)} collective-permute-done((f32[136,128]{1,0:T(8,128)S(1)}, f32[136,128]{1,0:T(8,128)S(1)}, u32[]{:S(2)}, u32[]{:S(2)}) %collective-permute-start.15) | collective-permute-done | bytes 69664 | tf_op jit(solution)/shard_map/ppermute | solution.py:21
  70.6 3.1 %collective-permute-done.16 = f32[136,128]{1,0:T(8,128)S(1)} collective-permute-done((f32[136,128]{1,0:T(8,128)S(1)}, f32[136,128]{1,0:T(8,128)S(1)}, u32[]{:S(2)}, u32[]{:S(2)}) %collective-permute-start.16) | collective-permute-done | bytes 69664 | tf_op jit(solution)/shard_map/ppermute | solution.py:21
  73.8 1.2 %collective-permute-done.17.other_ref = f32[136,128]{1,0:T(8,128)S(1)} collective-permute-done((f32[136,128]{1,0:T(8,128)S(1)}, f32[136,128]{1,0:T(8,128)S(1)}, u32[]{:S(2)}, u32[]{:S(2)}) %collective-permute-start.17) | collective-permute-done | bytes 69664 | tf_op jit(solution)/shard_map/ppermute | solution.py:21
  75.0 8.6 %shard_map.53 = (f32[256,256]{1,0:T(8,128)}, bf16[256,1024]{1,0:T(8,128)(2,1)}) custom-call(s32[2]{0:T(128)S(1)} %pad_add_fusion.place_ref, f32[136,128]{1,0:T(8,128)S(1)} %add_add_fusion.mine_ref, f32[136,128]{1,0:T(8,128)S(1)} %collective-permute-done.17.other_ref, bf16[256,1024]{1,0:T(8,128)(2,1)S(1)} %get-tuple-element.25.high_ref, ...), custom_call_target="tpu_custom_call" | custom-call | flops 402653184 | bytes 1974272 | tf_op jit(solution)/shard_map/pallas_call | solution.py:293
  (18 shorter events, 0.2 us)
Async XLA Ops:
  5.8 6.0 %collective-permute-start = (f32[128,256]{1,0:T(8,128)S(1)}, f32[128,256]{1,0:T(8,128)S(1)}, u32[]{:S(2)}, u32[]{:S(2)}) collective-permute-start(f32[128,256]{1,0:T(8,128)S(1)} %get-tuple-element.19), channel_id=1, source_target_pairs={{0,4},{1,9},{2,6},{3,11},{4,0},{5,13},{6,2},{7,15},{8,12},{9,1},{1... | collective-permute-start | bytes 393224 | tf_op jit(solution)/shard_map/ppermute | solution.py:21
  11.8 5.6 %collective-permute-start.1 = (f32[128,256]{1,0:T(8,128)S(1)}, f32[128,256]{1,0:T(8,128)S(1)}, u32[]{:S(2)}, u32[]{:S(2)}) collective-permute-start(f32[128,256]{1,0:T(8,128)S(1)} %add.44), channel_id=1, source_target_pairs={{0,8},{1,17},{2,10},{3,19},{4,12},{5,21},{6,14},{7,23},{8,0},{9,25... | collective-permute-start | bytes 393224 | tf_op jit(solution)/shard_map/ppermute | solution.py:21
  17.4 6.0 %collective-permute-start.2 = (f32[128,256]{1,0:T(8,128)S(1)}, f32[128,256]{1,0:T(8,128)S(1)}, u32[]{:S(2)}, u32[]{:S(2)}) collective-permute-start(f32[128,256]{1,0:T(8,128)S(1)} %add.45), channel_id=1, source_target_pairs={{0,16},{1,5},{2,18},{3,7},{4,20},{5,1},{6,22},{7,3},{8,24},{9,13},... | collective-permute-start | bytes 393224 | tf_op jit(solution)/shard_map/ppermute | solution.py:21
  23.4 4.3 %collective-permute-start.3 = (bf16[128,256]{1,0:T(8,128)(2,1)S(1)}, bf16[128,256]{1,0:T(8,128)(2,1)S(1)}, u32[]{:S(2)}, u32[]{:S(2)}) collective-permute-start(bf16[128,256]{1,0:T(8,128)(2,1)S(1)} %multiply_convert_fusion), channel_id=1, source_target_pairs={{0,4},{1,9},{2,6},{3,11},{4,0},{5,13},{6,2},{7,15},{8,12},{9,1},{1... | collective-permute-start | bytes 196616 | tf_op jit(solution)/shard_map/ppermute | solution.py:21
  25.0 27.4 %collective-permute-start.8 = (bf16[1024,256]{1,0:T(8,128)(2,1)S(1)}, bf16[1024,256]{1,0:T(8,128)(2,1)S(1)}, u32[]{:S(2)}, u32[]{:S(2)}) collective-permute-start(bf16[1024,256]{1,0:T(8,128)(2,1)S(1)} %get-tuple-element.16.refs_0_), channel_id=1, source_target_pairs={{0,2},{1,3},{2,0},{3,1},{4,6},{5,7},{6,4},{7,5},{8,10},{9,11},{10,... | collective-permute-start | bytes 1572872 | tf_op jit(solution)/shard_map/ppermute | solution.py:21
  26.5 26.0 %collective-permute-start.9 = (bf16[1024,256]{1,0:T(8,128)(2,1)S(1)}, bf16[1024,256]{1,0:T(8,128)(2,1)S(1)}, u32[]{:S(2)}, u32[]{:S(2)}) collective-permute-start(bf16[1024,256]{1,0:T(8,128)(2,1)S(1)} %get-tuple-element.17.refs_1_), channel_id=1, source_target_pairs={{0,3},{1,2},{2,1},{3,0},{4,7},{5,6},{6,5},{7,4},{8,11},{9,10},{10,... | collective-permute-start | bytes 1572872 | tf_op jit(solution)/shard_map/ppermute | solution.py:21
  26.5 23.6 %collective-permute-start.5 = (bf16[1024,256]{1,0:T(8,128)(2,1)S(1)}, bf16[1024,256]{1,0:T(8,128)(2,1)S(1)}, u32[]{:S(2)}, u32[]{:S(2)}) collective-permute-start(bf16[1024,256]{1,0:T(8,128)(2,1)S(1)} %get-tuple-element.20), channel_id=1, source_target_pairs={{0,1},{1,0},{2,3},{3,2},{4,5},{5,4},{6,7},{7,6},{8,9},{9,8},{10,11... | collective-permute-start | bytes 1572872 | tf_op jit(solution)/shard_map/ppermute | solution.py:21
  27.8 22.3 %collective-permute-start.6 = (bf16[256,256]{1,0:T(8,128)(2,1)S(1)}, bf16[256,256]{1,0:T(8,128)(2,1)S(1)}, u32[]{:S(2)}, u32[]{:S(2)}) collective-permute-start(bf16[256,256]{1,0:T(8,128)(2,1)S(1)} %pad_maximum_fusion.low_ref), channel_id=1, source_target_pairs={{0,2},{1,3},{2,0},{3,1},{4,6},{5,7},{6,4},{7,5},{8,10},{9,11},{10,... | collective-permute-start | bytes 393224 | tf_op jit(solution)/shard_map/ppermute | solution.py:21
  29.3 20.7 %collective-permute-start.4 = (bf16[256,256]{1,0:T(8,128)(2,1)S(1)}, bf16[256,256]{1,0:T(8,128)(2,1)S(1)}, u32[]{:S(2)}, u32[]{:S(2)}) collective-permute-start(bf16[256,256]{1,0:T(8,128)(2,1)S(1)} %pad_maximum_fusion.low_ref), channel_id=1, source_target_pairs={{0,1},{1,0},{2,3},{3,2},{4,5},{5,4},{6,7},{7,6},{8,9},{9,8},{10,11... | collective-permute-start | bytes 393224 | tf_op jit(solution)/shard_map/ppermute | solution.py:21
  50.0 2.4 %collective-permute-start.7 = (bf16[256,256]{1,0:T(8,128)(2,1)S(1)}, bf16[256,256]{1,0:T(8,128)(2,1)S(1)}, u32[]{:S(2)}, u32[]{:S(2)}) collective-permute-start(bf16[256,256]{1,0:T(8,128)(2,1)S(1)} %collective-permute-done.6.refs_0_), channel_id=1, source_target_pairs={{0,1},{1,0},{2,3},{3,2},{4,5},{5,4},{6,7},{7,6},{8,9},{9,8},{10,11... | collective-permute-start | bytes 393224 | tf_op jit(solution)/shard_map/ppermute | solution.py:21
  55.5 1.5 %collective-permute-start.10 = (f32[136,128]{1,0:T(8,128)S(1)}, f32[136,128]{1,0:T(8,128)S(1)}, u32[]{:S(2)}, u32[]{:S(2)}) collective-permute-start(f32[136,128]{1,0:T(8,128)S(1)} %get-tuple-element.24), channel_id=1, source_target_pairs={{0,1},{1,0},{2,3},{3,2},{4,5},{5,4},{6,7},{7,6},{8,9},{9,8},{10,11... | collective-permute-start | bytes 208904 | tf_op jit(solution)/shard_map/ppermute | solution.py:21
  57.0 4.4 %collective-permute-start.12 = (f32[136,128]{1,0:T(8,128)S(1)}, f32[136,128]{1,0:T(8,128)S(1)}, u32[]{:S(2)}, u32[]{:S(2)}) collective-permute-start(f32[136,128]{1,0:T(8,128)S(1)} %add.47), channel_id=1, source_target_pairs={{0,4},{1,17},{2,6},{3,19},{4,0},{5,21},{6,2},{7,23},{8,12},{9,25},... | collective-permute-start | bytes 208904 | tf_op jit(solution)/shard_map/ppermute | solution.py:21
  58.5 5.2 %collective-permute-start.13 = (f32[136,128]{1,0:T(8,128)S(1)}, f32[136,128]{1,0:T(8,128)S(1)}, u32[]{:S(2)}, u32[]{:S(2)}) collective-permute-start(f32[136,128]{1,0:T(8,128)S(1)} %add.47), channel_id=1, source_target_pairs={{0,6},{1,25},{2,4},{3,27},{4,2},{5,29},{6,0},{7,31},{8,14},{9,17},... | collective-permute-start | bytes 208904 | tf_op jit(solution)/shard_map/ppermute | solution.py:21
  60.0 4.3 %collective-permute-start.11 = (f32[136,128]{1,0:T(8,128)S(1)}, f32[136,128]{1,0:T(8,128)S(1)}, u32[]{:S(2)}, u32[]{:S(2)}) collective-permute-start(f32[136,128]{1,0:T(8,128)S(1)} %add.47), channel_id=1, source_target_pairs={{0,2},{1,9},{2,0},{3,11},{4,6},{5,13},{6,4},{7,15},{8,10},{9,1},{1... | collective-permute-start | bytes 208904 | tf_op jit(solution)/shard_map/ppermute | solution.py:21
  64.3 6.3 %collective-permute-start.15 = (f32[136,128]{1,0:T(8,128)S(1)}, f32[136,128]{1,0:T(8,128)S(1)}, u32[]{:S(2)}, u32[]{:S(2)}) collective-permute-start(f32[136,128]{1,0:T(8,128)S(1)} %add_add_fusion.1), channel_id=1, source_target_pairs={{0,16},{1,5},{2,18},{3,7},{4,20},{5,1},{6,22},{7,3},{8,24},{9,13},... | collective-permute-start | bytes 208904 | tf_op jit(solution)/shard_map/ppermute | solution.py:21
  67.5 6.1 %collective-permute-start.16 = (f32[136,128]{1,0:T(8,128)S(1)}, f32[136,128]{1,0:T(8,128)S(1)}, u32[]{:S(2)}, u32[]{:S(2)}) collective-permute-start(f32[136,128]{1,0:T(8,128)S(1)} %add_add_fusion.1), channel_id=1, source_target_pairs={{0,24},{1,7},{2,26},{3,5},{4,28},{5,3},{6,30},{7,1},{8,16},{9,15},... | collective-permute-start | bytes 208904 | tf_op jit(solution)/shard_map/ppermute | solution.py:21
  67.9 5.8 %collective-permute-start.14 = (f32[136,128]{1,0:T(8,128)S(1)}, f32[136,128]{1,0:T(8,128)S(1)}, u32[]{:S(2)}, u32[]{:S(2)}) collective-permute-start(f32[136,128]{1,0:T(8,128)S(1)} %add_add_fusion.1), channel_id=1, source_target_pairs={{0,8},{1,3},{2,10},{3,1},{4,12},{5,7},{6,14},{7,5},{8,0},{9,11},{1... | collective-permute-start | bytes 208904 | tf_op jit(solution)/shard_map/ppermute | solution.py:21
  73.7 1.3 %collective-permute-start.17 = (f32[136,128]{1,0:T(8,128)S(1)}, f32[136,128]{1,0:T(8,128)S(1)}, u32[]{:S(2)}, u32[]{:S(2)}) collective-permute-start(f32[136,128]{1,0:T(8,128)S(1)} %add_add_fusion.mine_ref), channel_id=1, source_target_pairs={{0,1},{1,0},{2,3},{3,2},{4,5},{5,4},{6,7},{7,6},{8,9},{9,8},{10,11... | collective-permute-start | bytes 208904 | tf_op jit(solution)/shard_map/ppermute | solution.py:21

commit v4 on v2

--- a/solution.py
+++ b/solution.py
@@ -49,43 +49,52 @@
     return lax.dot_general(left, right, (((0,), (0,)), ((), ())), preferred_element_type=jnp.float32)
 
 
-def project_kernel(place_ref, basis_ref, snaps_ref, keep_ref, send_ref, *refs):
-    count = (len(refs) - 2) // 2
-    slab_refs, part_refs, basis_sem, snaps_sem = refs[:count], refs[count : 2 * count], refs[-2], refs[-1]
-    points = slab_refs[0].shape[0]
+def slab_copies(place_ref, whole_ref, into_refs, sem_ref, first, by_rows):
     copies = []
-    for offset in range(count):
-        start = pl.multiple_of((place_ref[0] ^ offset) * points, points)
-        span = pl.ds(start, points)
-        copies.append(
-            (
-                pltpu.make_async_copy(basis_ref.at[span, :], slab_refs[offset], basis_sem.at[offset]),
-                pltpu.make_async_copy(snaps_ref.at[:, span], part_refs[offset], snaps_sem.at[offset]),
-            )
-        )
-    for pair in copies:
+    for index, into_ref in enumerate(into_refs):
+        size = into_ref.shape[0 if by_rows else 1]
+        start = pl.multiple_of((place_ref[0] ^ (first + index)) * size, size)
+        span = whole_ref.at[pl.ds(start, size), :] if by_rows else whole_ref.at[:, pl.ds(start, size)]
+        copies.append(pltpu.make_async_copy(span, into_ref, sem_ref.at[index]))
+    return copies
+
+
+def project_kernel(place_ref, basis_ref, snaps_ref, *refs):
+    count = (len(refs) - 7) // 2
+    piece_refs, slab_refs = refs[:4], (refs[3 + count],) + refs[4 : 3 + count]
+    part_refs, total_ref, basis_sem, snaps_sem = refs[4 + count : 4 + 2 * count], refs[-3], refs[-2], refs[-1]
+    basis_copies = slab_copies(place_ref, basis_ref, slab_refs, basis_sem, 0, True)
+    snaps_copies = slab_copies(place_ref, snaps_ref, part_refs, snaps_sem, 0, False)
+    for pair in zip(basis_copies, snaps_copies):
         for copy in pair:
             copy.start()
     total = None
     for offset in range(count):
-        for copy in copies[offset]:
-            copy.wait()
+        basis_copies[offset].wait()
+        snaps_copies[offset].wait()
         value = jnp.dot(part_refs[offset][...], slab_refs[offset][...], preferred_element_type=jnp.float32)
         total = value if total is None else total + value
-    half = total.shape[0] // 2
-    odd = place_ref[1] == 1
-    first, second = total[:half, :], total[half:, :]
-    keep_ref[...] = jnp.where(odd, second, first)
-    send_ref[...] = jnp.where(odd, first, second)
-
-
-def recon_kernel(place_ref, *refs):
-    recon_ref, coefficients_ref = refs[-2:]
-    coefficients_ref[...] = refs[0][...].astype(jnp.float32).T
+    total_ref[...] = total
+    rows = piece_refs[0].shape[0]
+    for offset, piece_ref in enumerate(piece_refs):
+        start = pl.multiple_of((place_ref[1] ^ offset) * rows, rows)
+        piece_ref[...] = total_ref[pl.ds(start, rows), :]
+
+
+def recon_kernel(place_ref, basis_ref, snaps_ref, low_ref, near_low_ref, near_ref, base_ref, coefficients_ref, *scratch):
+    own_ref, span_ref, basis_sem, snaps_sem = scratch
+    (basis_copy,) = slab_copies(place_ref, basis_ref, (own_ref,), basis_sem, 0, True)
+    (snaps_copy,) = slab_copies(place_ref, snaps_ref, (span_ref,), snaps_sem, 0, False)
+    basis_copy.start()
+    snaps_copy.start()
+    coefficients_ref[...] = low_ref[...].astype(jnp.float32).T
+    basis_copy.wait()
+    snaps_copy.wait()
     chunk = 256
-    for start in range(0, recon_ref.shape[1], chunk):
+    for start in range(0, base_ref.shape[1], chunk):
         cols = slice(start, start + chunk)
-        recon_ref[:, cols] = nt_dot(refs[0][...], refs[2][cols, :]) + nt_dot(refs[1][...], refs[3][cols, :])
+        recon = nt_dot(low_ref[...], own_ref[cols, :]) + nt_dot(near_low_ref[...], near_ref[cols, :])
+        base_ref[:, cols] = span_ref[:, cols].astype(jnp.float32) - recon * (1.0 / math.sqrt(RANK))
 
 
 def packed_rows(tiles):
@@ -109,18 +118,17 @@
 
 
 def residual_kernel(total_points, place_ref, *refs):
-    count = (len(refs) - 7) // 2
+    count = (len(refs) - 6) // 2
     low_refs, basis_refs = refs[:count], refs[count : 2 * count]
-    begun_ref, snaps_ref, high_ref, rest_ref, keep_ref, send_ref, pack_ref = refs[2 * count :]
-    snaps, points = snaps_ref.shape
+    base_ref, high_ref, rest_ref, keep_ref, send_ref, pack_ref = refs[2 * count :]
+    snaps, points = base_ref.shape
     chunk = 256
     for start in range(0, points, chunk):
         cols = slice(start, start + chunk)
-        recon = begun_ref[:, cols]
-        for low_ref, basis_ref in zip(low_refs, basis_refs):
+        recon = nt_dot(low_refs[0][...], basis_refs[0][cols, :])
+        for low_ref, basis_ref in zip(low_refs[1:], basis_refs[1:]):
             recon += nt_dot(low_ref[...], basis_ref[cols, :])
-        residual = snaps_ref[:, cols].astype(jnp.float32) - recon * (1.0 / math.sqrt(RANK))
-        high, rest = wide_split(residual)
+        high, rest = wide_split(base_ref[:, cols] - recon * (1.0 / math.sqrt(RANK)))
         high_ref[:, cols] = high
         rest_ref[:, cols] = rest
     scale = 1.0 / total_points
@@ -295,35 +303,39 @@
     row_count, columns = lax.axis_size("rows"), lax.axis_size("cols")
     total_points = row_points * row_count
     points = row_points // columns
-    half = snaps // 2
+    quarter = snaps // 4
     bf16, f32 = jnp.bfloat16, jnp.float32
 
     row_bits = bits(row_count, columns)
-    sum_steps = list(zip(row_bits, row_bits[1:] + row_bits[:1]))
+    orders = list(zip(row_bits, row_bits[1:] + row_bits[:1]))
+    first, second = orders[0], orders[1]
+    both = tuple(a ^ b for a, b in zip(first, second))
     flat = row_index * columns + column_index
-    odd = (flat // jnp.where(column_index % 2 == 0, sum_steps[0][0], sum_steps[0][1])) % 2
-    place = jnp.stack([column_index, odd]).astype(jnp.int32)
-
-    slab, part = shape(bf16, points, modes), shape(f32, half, modes)
+    even = column_index % 2 == 0
+    low_bit, high_bit = ((flat // jnp.where(even, *masks)) % 2 for masks in (first, second))
+    quad = (low_bit + 2 * high_bit).astype(jnp.int32)
+    place = jnp.stack([column_index.astype(jnp.int32), quad])
+
+    slab, piece = shape(bf16, points, modes), shape(f32, quarter, modes)
+    slab_scratch, span_scratch = pltpu.VMEM((points, modes), bf16), pltpu.VMEM((snaps, points), bf16)
     semaphores = pltpu.SemaphoreType.DMA((columns,))
-    kept, sent, *slabs, own_snaps = call(
+    kept, one, two, three, *slabs = call(
         project_kernel,
-        (part, part) + (slab,) * columns + (shape(bf16, snaps, points),),
-        [pltpu.VMEM((snaps, points), bf16)] * (columns - 1) + [semaphores, semaphores],
+        (piece,) * 4 + (slab,) * (columns - 1),
+        [slab_scratch] + [span_scratch] * columns + [pltpu.VMEM((snaps, modes), f32), semaphores, semaphores],
         2 * snaps * row_points * modes,
         12,
         2,
     )(place, basis_cols, snapshots)
-    arrived_slabs = [swap(slabs[offset], (offset,) * 2) for offset in range(2, columns)]
-    own_slab, near_slab = slabs[:2]
-    arrived = swap(sent, sum_steps[0])
-    near_slab = swap(near_slab, (1, 1))
-    kept = kept + arrived
-    for step in sum_steps[1:]:
+    arrived_slabs = [swap(slabs[offset - 1], (offset,) * 2) for offset in range(2, columns)]
+    one, two, three = swap(one, first), swap(two, second), swap(three, both)
+    near_slab = swap(slabs[0], (1, 1))
+    kept = (kept + one) + (two + three)
+    for step in orders[2:]:
         kept = kept + swap(kept, step)
     low = (kept * (math.sqrt(RANK) / total_points)).astype(bf16)
-    other = swap(low, sum_steps[0])
-    low = jnp.concatenate([jnp.where(odd == 1, other, low), jnp.where(odd == 1, low, other)], 0)
+    found = (low, swap(low, first), swap(low, second), swap(low, both))
+    low = jnp.concatenate([lax.select_n(quad ^ at, *found) for at in range(4)], 0)
     lows = {0: low}
     for offset in range(2, columns, 2):
         lows[offset] = swap(low, (offset, offset))
@@ -331,8 +343,13 @@
         lows[offset + 1] = swap(lows[offset], (1, 1))
 
     begun, coefficients = call(
-        recon_kernel, (shape(f32, snaps, points), shape(f32, modes, snaps)), [], 4 * snaps * points * modes, 8
-    )(place, lows[0], lows[1], own_slab, near_slab)
+        recon_kernel,
+        (shape(f32, snaps, points), shape(f32, modes, snaps)),
+        [slab_scratch, span_scratch, semaphores, semaphores],
+        4 * snaps * points * modes,
+        8,
+        2,
+    )(place, basis_cols, snapshots, lows[0], lows[1], near_slab)
     packed = packed_rows(snaps // LANES)
     part = shape(f32, packed // 2, LANES)
     wide = shape(bf16, snaps, points)
@@ -342,7 +359,7 @@
         [pltpu.VMEM((packed, LANES), f32)],
         2 * snaps * points * (modes * (columns - 2) + 3 * snaps),
         16,
-    )(place, *[lows[offset] for offset in range(2, columns)], *arrived_slabs, begun, own_snaps)
+    )(place, *[lows[offset] for offset in range(2, columns)], *arrived_slabs, begun)
     keep = keep + swap(send, (1, 1))
     for masks in zip(*exchange_rounds(bits(columns // 2, 2) + row_bits)):
         if masks[0][1] == 0:

time: 85.7 us -> 84.3 us (0.984)
  waiting for transfers between devices: 44.6 us -> 43.2 us
    ppermute x18 -> x21, waiting for transfers between devices: 44.6 us -> 43.2 us  [swap(): lax.ppermute(value, ('rows', 'cols'), [(i, i ^ masks[i % 2]) for i in ran...]
    ppermute x18 -> x21, starting transfers between devices: 23.4 us -> 22.9 us  [swap(): lax.ppermute(value, ('rows', 'cols'), [(i, i ^ masks[i % 2]) for i in ran...]
  transfers between devices with their start and end apart: 18 -> 21, of which waited for: 12 -> 12; matrix products, arithmetic and copies ran while one was open for 0% -> 0% of each run, Pallas kernels for 2% -> 3%
where the time goes in v4:
time: 84.3 us; the launch traced here: 84.2 us
  waiting for transfers between devices  43.2 us (51%)
  starting transfers between devices  22.9 us (27%)
  Pallas kernels  17.1 us (20%)
    ppermute x21, waiting for transfers between devices, swap(): lax.ppermute(value, ('rows', 'cols'), [(i, i ^ masks[i % 2]) for i in ran...  43.2 us
    ppermute x21, starting transfers between devices, swap(): lax.ppermute(value, ('rows', 'cols'), [(i, i ^ masks[i % 2]) for i in ran...  22.9 us
    pallas_call x4, Pallas kernels, run(): pl.pallas_call(kernel, out_shape=outs, in_specs=[smem] + [hbm] * whole +...  17.1 us
  transfers between devices with their start and end apart: 21, of which 12 were waited for; matrix products, arithmetic and copies ran while one was open for 0% of the time, Pallas kernels for 3%

profile of v4, /device:TPU:0, one launch (start us, length us, event | category | flops | bytes accessed | tf_op | source)
XLA Modules:
  0.0 84.2 jit_solution(2658949376908414149)
XLA Ops:
  0.7 0.1 pad_add_fusion.place_ref
  0.8 3.6 %shard_map.49 = (f32[64,256]{1,0:T(8,128)S(1)}, f32[64,256]{1,0:T(8,128)S(1)}, f32[64,256]{1,0:T(8,128)S(1)}, f32[64,256]{1,0:T(8,128)S(1)}, bf16[1024,256]{1,0:...) custom-call(s32[2]{0:T(128)S(1)} %pad_add_fusion.place_ref, bf16[4096,256]{1,0:T(8,128)(2,1)} %basis_ref.3, ...), custom_call_target="tpu_custom_call" | custom-call | flops 536870912 | bytes 6029312 | tf_op jit(solution)/shard_map/pallas_call | solution.py:282
  4.4 3.1 %collective-permute-start = (f32[64,256]{1,0:T(8,128)S(1)}, f32[64,256]{1,0:T(8,128)S(1)}, u32[]{:S(2)}, u32[]{:S(2)}) collective-permute-start(f32[64,256]{1,0:T(8,128)S(1)} %get-tuple-element.19), channel_id=1, source_target_pairs={{0,4},{1,9},{2,6},{3,11},{4,0},{5,13},{6,2},{7,15},{8,12},{9,1},{1... | collective-permute-start | bytes 196616 | tf_op jit(solution)/shard_map/ppermute | solution.py:21
  7.4 1.6 %collective-permute-start.1 = (f32[64,256]{1,0:T(8,128)S(1)}, f32[64,256]{1,0:T(8,128)S(1)}, u32[]{:S(2)}, u32[]{:S(2)}) collective-permute-start(f32[64,256]{1,0:T(8,128)S(1)} %get-tuple-element.20), channel_id=1, source_target_pairs={{0,8},{1,17},{2,10},{3,19},{4,12},{5,21},{6,14},{7,23},{8,0},{9,25... | collective-permute-start | bytes 196616 | tf_op jit(solution)/shard_map/ppermute | solution.py:21
  9.0 0.7 collective-permute-done
  9.7 2.2 %collective-permute-done.1 = f32[64,256]{1,0:T(8,128)S(1)} collective-permute-done((f32[64,256]{1,0:T(8,128)S(1)}, f32[64,256]{1,0:T(8,128)S(1)}, u32[]{:S(2)}, u32[]{:S(2)}) %collective-permute-start.1) | collective-permute-done | bytes 65568 | tf_op jit(solution)/shard_map/ppermute | solution.py:21
  11.9 2.3 %collective-permute-done.2 = f32[64,256]{1,0:T(8,128)S(1)} collective-permute-done((f32[64,256]{1,0:T(8,128)S(1)}, f32[64,256]{1,0:T(8,128)S(1)}, u32[]{:S(2)}, u32[]{:S(2)}) %collective-permute-start.2) | collective-permute-done | bytes 65568 | tf_op jit(solution)/shard_map/ppermute | solution.py:21
  14.2 2.7 %collective-permute-start.3 = (f32[64,256]{1,0:T(8,128)S(1)}, f32[64,256]{1,0:T(8,128)S(1)}, u32[]{:S(2)}, u32[]{:S(2)}) collective-permute-start(f32[64,256]{1,0:T(8,128)S(1)} %add_add_fusion.2), channel_id=1, source_target_pairs={{0,16},{1,5},{2,18},{3,7},{4,20},{5,1},{6,22},{7,3},{8,24},{9,13},... | collective-permute-start | bytes 196616 | tf_op jit(solution)/shard_map/ppermute | solution.py:21
  16.9 3.5 %collective-permute-done.3 = f32[64,256]{1,0:T(8,128)S(1)} collective-permute-done((f32[64,256]{1,0:T(8,128)S(1)}, f32[64,256]{1,0:T(8,128)S(1)}, u32[]{:S(2)}, u32[]{:S(2)}) %collective-permute-start.3) | collective-permute-done | bytes 65568 | tf_op jit(solution)/shard_map/ppermute | solution.py:21
  20.4 0.9 %collective-permute-start.6 = (bf16[64,256]{1,0:T(8,128)(2,1)S(1)}, bf16[64,256]{1,0:T(8,128)(2,1)S(1)}, u32[]{:S(2)}, u32[]{:S(2)}) collective-permute-start(bf16[64,256]{1,0:T(8,128)(2,1)S(1)} %multiply_convert_fusion), channel_id=1, source_target_pairs={{0,12},{1,25},{2,14},{3,27},{4,8},{5,29},{6,10},{7,31},{8,4},{9,17... | collective-permute-start | bytes 98312 | tf_op jit(solution)/shard_map/ppermute | solution.py:21
  21.3 0.2 collective-permute-start.5
  21.5 2.5 %collective-permute-start.4 = (bf16[64,256]{1,0:T(8,128)(2,1)S(1)}, bf16[64,256]{1,0:T(8,128)(2,1)S(1)}, u32[]{:S(2)}, u32[]{:S(2)}) collective-permute-start(bf16[64,256]{1,0:T(8,128)(2,1)S(1)} %multiply_convert_fusion), channel_id=1, source_target_pairs={{0,4},{1,9},{2,6},{3,11},{4,0},{5,13},{6,2},{7,15},{8,12},{9,1},{1... | collective-permute-start | bytes 98312 | tf_op jit(solution)/shard_map/ppermute | solution.py:21
  24.0 1.5 %collective-permute-start.11 = (bf16[1024,256]{1,0:T(8,128)(2,1)S(1)}, bf16[1024,256]{1,0:T(8,128)(2,1)S(1)}, u32[]{:S(2)}, u32[]{:S(2)}) collective-permute-start(bf16[1024,256]{1,0:T(8,128)(2,1)S(1)} %get-tuple-element.24), channel_id=1, source_target_pairs={{0,2},{1,3},{2,0},{3,1},{4,6},{5,7},{6,4},{7,5},{8,10},{9,11},{10,... | collective-permute-start | bytes 1572872 | tf_op jit(solution)/shard_map/ppermute | solution.py:21
  25.5 0.4 collective-permute-start.12
  25.9 1.6 %collective-permute-start.9 = (bf16[256,256]{1,0:T(8,128)(2,1)S(1)}, bf16[256,256]{1,0:T(8,128)(2,1)S(1)}, u32[]{:S(2)}, u32[]{:S(2)}) collective-permute-start(bf16[256,256]{1,0:T(8,128)(2,1)S(1)} %pad_maximum_fusion.low_ref), channel_id=1, source_target_pairs={{0,2},{1,3},{2,0},{3,1},{4,6},{5,7},{6,4},{7,5},{8,10},{9,11},{10,... | collective-permute-start | bytes 393224 | tf_op jit(solution)/shard_map/ppermute | solution.py:21
  27.5 24.9 %collective-permute-done.9.refs_0_ = bf16[256,256]{1,0:T(8,128)(2,1)S(1)} collective-permute-done((bf16[256,256]{1,0:T(8,128)(2,1)S(1)}, bf16[256,256]{1,0:T(8,128)(2,1)S(1)}, u32[]{:S(2)}, u32[]{:S(2)}) %collective-permute-start.9) | collective-permute-done | bytes 131104 | tf_op jit(solution)/shard_map/ppermute | solution.py:21
  52.4 2.8 %shard_map.50 = (f32[256,1024]{1,0:T(8,128)S(1)}, f32[256,256]{1,0:T(8,128)}) custom-call(s32[2]{0:T(128)S(1)} %pad_add_fusion.place_ref, bf16[4096,256]{1,0:T(8,128)(2,1)} %basis_ref.3, bf16[256,4096]{1,0:T(8,128)(2,1)} %snaps_ref.3, bf16[256,256]{1,0:T(8,128)(2,1)S(1)} %pad_maximum_fusion.low_ref, ...), custom_call_target="tpu_custom_call" | custom-call | flops 268435456 | bytes 6291456 | tf_op jit(solution)/shard_map/pallas_call | solution.py:282
  55.2 2.0 %shard_map.51 = (bf16[256,1024]{1,0:T(8,128)(2,1)S(1)}, bf16[256,1024]{1,0:T(8,128)(2,1)S(1)}, f32[136,128]{1,0:T(8,128)S(1)}, f32[136,128]{1,0:T(8,128)S(1)}) custom-call(s32[2]{0:T(128)S(1)} %pad_add_fusion.place_ref, bf16[256,256]{1,0:T(8,128)(2,1)S(1)} %collective-permute-done.9.refs_0_, bf16[256,256]{1,0:T(8,128)(2,1)S(1)} %collective-permute-done.10.refs_1_, ...), custom_call_target="tpu_custom_call" | custom-call | flops 671088640 | bytes 3547136 | tf_op jit(solution)/shard_map/pallas_call | solution.py:282
  57.3 0.6 collective-permute-start.13
  57.9 0.9 %collective-permute-done.13 = f32[136,128]{1,0:T(8,128)S(1)} collective-permute-done((f32[136,128]{1,0:T(8,128)S(1)}, f32[136,128]{1,0:T(8,128)S(1)}, u32[]{:S(2)}, u32[]{:S(2)}) %collective-permute-start.13) | collective-permute-done | bytes 69664 | tf_op jit(solution)/shard_map/ppermute | solution.py:21
  58.8 1.0 %collective-permute-start.16 = (f32[136,128]{1,0:T(8,128)S(1)}, f32[136,128]{1,0:T(8,128)S(1)}, u32[]{:S(2)}, u32[]{:S(2)}) collective-permute-start(f32[136,128]{1,0:T(8,128)S(1)} %add.60), channel_id=1, source_target_pairs={{0,6},{1,25},{2,4},{3,27},{4,2},{5,29},{6,0},{7,31},{8,14},{9,17},... | collective-permute-start | bytes 208904 | tf_op jit(solution)/shard_map/ppermute | solution.py:21
  59.8 2.0 %collective-permute-start.15 = (f32[136,128]{1,0:T(8,128)S(1)}, f32[136,128]{1,0:T(8,128)S(1)}, u32[]{:S(2)}, u32[]{:S(2)}) collective-permute-start(f32[136,128]{1,0:T(8,128)S(1)} %add.60), channel_id=1, source_target_pairs={{0,4},{1,17},{2,6},{3,19},{4,0},{5,21},{6,2},{7,23},{8,12},{9,25},... | collective-permute-start | bytes 208904 | tf_op jit(solution)/shard_map/ppermute | solution.py:21
  61.8 0.5 collective-permute-start.14
  62.3 1.8 %collective-permute-done.16 = f32[136,128]{1,0:T(8,128)S(1)} collective-permute-done((f32[136,128]{1,0:T(8,128)S(1)}, f32[136,128]{1,0:T(8,128)S(1)}, u32[]{:S(2)}, u32[]{:S(2)}) %collective-permute-start.16) | collective-permute-done | bytes 69664 | tf_op jit(solution)/shard_map/ppermute | solution.py:21
  64.1 0.7 collective-permute-done.15
  64.8 1.3 %collective-permute-done.14 = f32[136,128]{1,0:T(8,128)S(1)} collective-permute-done((f32[136,128]{1,0:T(8,128)S(1)}, f32[136,128]{1,0:T(8,128)S(1)}, u32[]{:S(2)}, u32[]{:S(2)}) %collective-permute-start.14) | collective-permute-done | bytes 69664 | tf_op jit(solution)/shard_map/ppermute | solution.py:21
  66.1 2.9 %collective-permute-start.19 = (f32[136,128]{1,0:T(8,128)S(1)}, f32[136,128]{1,0:T(8,128)S(1)}, u32[]{:S(2)}, u32[]{:S(2)}) collective-permute-start(f32[136,128]{1,0:T(8,128)S(1)} %add_add_fusion.1), channel_id=1, source_target_pairs={{0,24},{1,7},{2,26},{3,5},{4,28},{5,3},{6,30},{7,1},{8,16},{9,15},... | collective-permute-start | bytes 208904 | tf_op jit(solution)/shard_map/ppermute | solution.py:21
  69.0 1.6 %collective-permute-start.17 = (f32[136,128]{1,0:T(8,128)S(1)}, f32[136,128]{1,0:T(8,128)S(1)}, u32[]{:S(2)}, u32[]{:S(2)}) collective-permute-start(f32[136,128]{1,0:T(8,128)S(1)} %add_add_fusion.1), channel_id=1, source_target_pairs={{0,8},{1,3},{2,10},{3,1},{4,12},{5,7},{6,14},{7,5},{8,0},{9,11},{1... | collective-permute-start | bytes 208904 | tf_op jit(solution)/shard_map/ppermute | solution.py:21
  70.6 1.7 %collective-permute-done.19 = f32[136,128]{1,0:T(8,128)S(1)} collective-permute-done((f32[136,128]{1,0:T(8,128)S(1)}, f32[136,128]{1,0:T(8,128)S(1)}, u32[]{:S(2)}, u32[]{:S(2)}) %collective-permute-start.19) | collective-permute-done | bytes 69664 | tf_op jit(solution)/shard_map/ppermute | solution.py:21
  72.3 1.9 %collective-permute-done.18 = f32[136,128]{1,0:T(8,128)S(1)} collective-permute-done((f32[136,128]{1,0:T(8,128)S(1)}, f32[136,128]{1,0:T(8,128)S(1)}, u32[]{:S(2)}, u32[]{:S(2)}) %collective-permute-start.18) | collective-permute-done | bytes 69664 | tf_op jit(solution)/shard_map/ppermute | solution.py:21
  74.3 1.2 %collective-permute-done.20.other_ref = f32[136,128]{1,0:T(8,128)S(1)} collective-permute-done((f32[136,128]{1,0:T(8,128)S(1)}, f32[136,128]{1,0:T(8,128)S(1)}, u32[]{:S(2)}, u32[]{:S(2)}) %collective-permute-start.20) | collective-permute-done | bytes 69664 | tf_op jit(solution)/shard_map/ppermute | solution.py:21
  75.6 8.6 %shard_map.52 = (f32[256,256]{1,0:T(8,128)}, bf16[256,1024]{1,0:T(8,128)(2,1)}) custom-call(s32[2]{0:T(128)S(1)} %pad_add_fusion.place_ref, f32[136,128]{1,0:T(8,128)S(1)} %add_add_fusion.mine_ref, f32[136,128]{1,0:T(8,128)S(1)} %collective-permute-done.20.other_ref, bf16[256,1024]{1,0:T(8,128)(2,1)S(1)} %get-tuple-element.29.high_ref, ...), custom_call_target="tpu_custom_call" | custom-call | flops 402653184 | bytes 1974272 | tf_op jit(solution)/shard_map/pallas_call | solution.py:282
  (22 shorter events, 0.2 us)
Async XLA Ops:
  4.4 5.3 %collective-permute-start = (f32[64,256]{1,0:T(8,128)S(1)}, f32[64,256]{1,0:T(8,128)S(1)}, u32[]{:S(2)}, u32[]{:S(2)}) collective-permute-start(f32[64,256]{1,0:T(8,128)S(1)} %get-tuple-element.19), channel_id=1, source_target_pairs={{0,4},{1,9},{2,6},{3,11},{4,0},{5,13},{6,2},{7,15},{8,12},{9,1},{1... | collective-permute-start | bytes 196616 | tf_op jit(solution)/shard_map/ppermute | solution.py:21
  7.4 4.4 %collective-permute-start.1 = (f32[64,256]{1,0:T(8,128)S(1)}, f32[64,256]{1,0:T(8,128)S(1)}, u32[]{:S(2)}, u32[]{:S(2)}) collective-permute-start(f32[64,256]{1,0:T(8,128)S(1)} %get-tuple-element.20), channel_id=1, source_target_pairs={{0,8},{1,17},{2,10},{3,19},{4,12},{5,21},{6,14},{7,23},{8,0},{9,25... | collective-permute-start | bytes 196616 | tf_op jit(solution)/shard_map/ppermute | solution.py:21
  9.0 5.2 %collective-permute-start.2 = (f32[64,256]{1,0:T(8,128)S(1)}, f32[64,256]{1,0:T(8,128)S(1)}, u32[]{:S(2)}, u32[]{:S(2)}) collective-permute-start(f32[64,256]{1,0:T(8,128)S(1)} %get-tuple-element.21), channel_id=1, source_target_pairs={{0,12},{1,25},{2,14},{3,27},{4,8},{5,29},{6,10},{7,31},{8,4},{9,17... | collective-permute-start | bytes 196616 | tf_op jit(solution)/shard_map/ppermute | solution.py:21
  14.2 6.2 %collective-permute-start.3 = (f32[64,256]{1,0:T(8,128)S(1)}, f32[64,256]{1,0:T(8,128)S(1)}, u32[]{:S(2)}, u32[]{:S(2)}) collective-permute-start(f32[64,256]{1,0:T(8,128)S(1)} %add_add_fusion.2), channel_id=1, source_target_pairs={{0,16},{1,5},{2,18},{3,7},{4,20},{5,1},{6,22},{7,3},{8,24},{9,13},... | collective-permute-start | bytes 196616 | tf_op jit(solution)/shard_map/ppermute | solution.py:21
  20.4 5.1 %collective-permute-start.6 = (bf16[64,256]{1,0:T(8,128)(2,1)S(1)}, bf16[64,256]{1,0:T(8,128)(2,1)S(1)}, u32[]{:S(2)}, u32[]{:S(2)}) collective-permute-start(bf16[64,256]{1,0:T(8,128)(2,1)S(1)} %multiply_convert_fusion), channel_id=1, source_target_pairs={{0,12},{1,25},{2,14},{3,27},{4,8},{5,29},{6,10},{7,31},{8,4},{9,17... | collective-permute-start | bytes 98312 | tf_op jit(solution)/shard_map/ppermute | solution.py:21
  21.3 4.6 %collective-permute-start.5 = (bf16[64,256]{1,0:T(8,128)(2,1)S(1)}, bf16[64,256]{1,0:T(8,128)(2,1)S(1)}, u32[]{:S(2)}, u32[]{:S(2)}) collective-permute-start(bf16[64,256]{1,0:T(8,128)(2,1)S(1)} %multiply_convert_fusion), channel_id=1, source_target_pairs={{0,8},{1,17},{2,10},{3,19},{4,12},{5,21},{6,14},{7,23},{8,0},{9,25... | collective-permute-start | bytes 98312 | tf_op jit(solution)/shard_map/ppermute | solution.py:21
  21.5 4.4 %collective-permute-start.4 = (bf16[64,256]{1,0:T(8,128)(2,1)S(1)}, bf16[64,256]{1,0:T(8,128)(2,1)S(1)}, u32[]{:S(2)}, u32[]{:S(2)}) collective-permute-start(bf16[64,256]{1,0:T(8,128)(2,1)S(1)} %multiply_convert_fusion), channel_id=1, source_target_pairs={{0,4},{1,9},{2,6},{3,11},{4,0},{5,13},{6,2},{7,15},{8,12},{9,1},{1... | collective-permute-start | bytes 98312 | tf_op jit(solution)/shard_map/ppermute | solution.py:21
  24.0 28.4 %collective-permute-start.8 = (bf16[1024,256]{1,0:T(8,128)(2,1)S(1)}, bf16[1024,256]{1,0:T(8,128)(2,1)S(1)}, u32[]{:S(2)}, u32[]{:S(2)}) collective-permute-start(bf16[1024,256]{1,0:T(8,128)(2,1)S(1)} %get-tuple-element.22), channel_id=1, source_target_pairs={{0,1},{1,0},{2,3},{3,2},{4,5},{5,4},{6,7},{7,6},{8,9},{9,8},{10,11... | collective-permute-start | bytes 1572872 | tf_op jit(solution)/shard_map/ppermute | solution.py:21
  24.0 31.3 %collective-permute-start.11 = (bf16[1024,256]{1,0:T(8,128)(2,1)S(1)}, bf16[1024,256]{1,0:T(8,128)(2,1)S(1)}, u32[]{:S(2)}, u32[]{:S(2)}) collective-permute-start(bf16[1024,256]{1,0:T(8,128)(2,1)S(1)} %get-tuple-element.24), channel_id=1, source_target_pairs={{0,2},{1,3},{2,0},{3,1},{4,6},{5,7},{6,4},{7,5},{8,10},{9,11},{10,... | collective-permute-start | bytes 1572872 | tf_op jit(solution)/shard_map/ppermute | solution.py:21
  25.5 29.8 %collective-permute-start.12 = (bf16[1024,256]{1,0:T(8,128)(2,1)S(1)}, bf16[1024,256]{1,0:T(8,128)(2,1)S(1)}, u32[]{:S(2)}, u32[]{:S(2)}) collective-permute-start(bf16[1024,256]{1,0:T(8,128)(2,1)S(1)} %get-tuple-element.25), channel_id=1, source_target_pairs={{0,3},{1,2},{2,1},{3,0},{4,7},{5,6},{6,5},{7,4},{8,11},{9,10},{10,... | collective-permute-start | bytes 1572872 | tf_op jit(solution)/shard_map/ppermute | solution.py:21
  25.9 26.4 %collective-permute-start.9 = (bf16[256,256]{1,0:T(8,128)(2,1)S(1)}, bf16[256,256]{1,0:T(8,128)(2,1)S(1)}, u32[]{:S(2)}, u32[]{:S(2)}) collective-permute-start(bf16[256,256]{1,0:T(8,128)(2,1)S(1)} %pad_maximum_fusion.low_ref), channel_id=1, source_target_pairs={{0,2},{1,3},{2,0},{3,1},{4,6},{5,7},{6,4},{7,5},{8,10},{9,11},{10,... | collective-permute-start | bytes 393224 | tf_op jit(solution)/shard_map/ppermute | solution.py:21
  27.5 24.9 %collective-permute-start.7 = (bf16[256,256]{1,0:T(8,128)(2,1)S(1)}, bf16[256,256]{1,0:T(8,128)(2,1)S(1)}, u32[]{:S(2)}, u32[]{:S(2)}) collective-permute-start(bf16[256,256]{1,0:T(8,128)(2,1)S(1)} %pad_maximum_fusion.low_ref), channel_id=1, source_target_pairs={{0,1},{1,0},{2,3},{3,2},{4,5},{5,4},{6,7},{7,6},{8,9},{9,8},{10,11... | collective-permute-start | bytes 393224 | tf_op jit(solution)/shard_map/ppermute | solution.py:21
  52.3 2.9 %collective-permute-start.10 = (bf16[256,256]{1,0:T(8,128)(2,1)S(1)}, bf16[256,256]{1,0:T(8,128)(2,1)S(1)}, u32[]{:S(2)}, u32[]{:S(2)}) collective-permute-start(bf16[256,256]{1,0:T(8,128)(2,1)S(1)} %collective-permute-done.9.refs_0_), channel_id=1, source_target_pairs={{0,1},{1,0},{2,3},{3,2},{4,5},{5,4},{6,7},{7,6},{8,9},{9,8},{10,11... | collective-permute-start | bytes 393224 | tf_op jit(solution)/shard_map/ppermute | solution.py:21
  57.3 1.5 %collective-permute-start.13 = (f32[136,128]{1,0:T(8,128)S(1)}, f32[136,128]{1,0:T(8,128)S(1)}, u32[]{:S(2)}, u32[]{:S(2)}) collective-permute-start(f32[136,128]{1,0:T(8,128)S(1)} %get-tuple-element.28), channel_id=1, source_target_pairs={{0,1},{1,0},{2,3},{3,2},{4,5},{5,4},{6,7},{7,6},{8,9},{9,8},{10,11... | collective-permute-start | bytes 208904 | tf_op jit(solution)/shard_map/ppermute | solution.py:21
  58.8 5.4 %collective-permute-start.16 = (f32[136,128]{1,0:T(8,128)S(1)}, f32[136,128]{1,0:T(8,128)S(1)}, u32[]{:S(2)}, u32[]{:S(2)}) collective-permute-start(f32[136,128]{1,0:T(8,128)S(1)} %add.60), channel_id=1, source_target_pairs={{0,6},{1,25},{2,4},{3,27},{4,2},{5,29},{6,0},{7,31},{8,14},{9,17},... | collective-permute-start | bytes 208904 | tf_op jit(solution)/shard_map/ppermute | solution.py:21
  59.8 5.0 %collective-permute-start.15 = (f32[136,128]{1,0:T(8,128)S(1)}, f32[136,128]{1,0:T(8,128)S(1)}, u32[]{:S(2)}, u32[]{:S(2)}) collective-permute-start(f32[136,128]{1,0:T(8,128)S(1)} %add.60), channel_id=1, source_target_pairs={{0,4},{1,17},{2,6},{3,19},{4,0},{5,21},{6,2},{7,23},{8,12},{9,25},... | collective-permute-start | bytes 208904 | tf_op jit(solution)/shard_map/ppermute | solution.py:21
  61.8 4.3 %collective-permute-start.14 = (f32[136,128]{1,0:T(8,128)S(1)}, f32[136,128]{1,0:T(8,128)S(1)}, u32[]{:S(2)}, u32[]{:S(2)}) collective-permute-start(f32[136,128]{1,0:T(8,128)S(1)} %add.60), channel_id=1, source_target_pairs={{0,2},{1,9},{2,0},{3,11},{4,6},{5,13},{6,4},{7,15},{8,10},{9,1},{1... | collective-permute-start | bytes 208904 | tf_op jit(solution)/shard_map/ppermute | solution.py:21
  66.1 6.2 %collective-permute-start.19 = (f32[136,128]{1,0:T(8,128)S(1)}, f32[136,128]{1,0:T(8,128)S(1)}, u32[]{:S(2)}, u32[]{:S(2)}) collective-permute-start(f32[136,128]{1,0:T(8,128)S(1)} %add_add_fusion.1), channel_id=1, source_target_pairs={{0,24},{1,7},{2,26},{3,5},{4,28},{5,3},{6,30},{7,1},{8,16},{9,15},... | collective-permute-start | bytes 208904 | tf_op jit(solution)/shard_map/ppermute | solution.py:21
  69.0 5.2 %collective-permute-start.18 = (f32[136,128]{1,0:T(8,128)S(1)}, f32[136,128]{1,0:T(8,128)S(1)}, u32[]{:S(2)}, u32[]{:S(2)}) collective-permute-start(f32[136,128]{1,0:T(8,128)S(1)} %add_add_fusion.1), channel_id=1, source_target_pairs={{0,16},{1,5},{2,18},{3,7},{4,20},{5,1},{6,22},{7,3},{8,24},{9,13},... | collective-permute-start | bytes 208904 | tf_op jit(solution)/shard_map/ppermute | solution.py:21
  69.0 5.2 %collective-permute-start.17 = (f32[136,128]{1,0:T(8,128)S(1)}, f32[136,128]{1,0:T(8,128)S(1)}, u32[]{:S(2)}, u32[]{:S(2)}) collective-permute-start(f32[136,128]{1,0:T(8,128)S(1)} %add_add_fusion.1), channel_id=1, source_target_pairs={{0,8},{1,3},{2,10},{3,1},{4,12},{5,7},{6,14},{7,5},{8,0},{9,11},{1... | collective-permute-start | bytes 208904 | tf_op jit(solution)/shard_map/ppermute | solution.py:21
  74.2 1.3 %collective-permute-start.20 = (f32[136,128]{1,0:T(8,128)S(1)}, f32[136,128]{1,0:T(8,128)S(1)}, u32[]{:S(2)}, u32[]{:S(2)}) collective-permute-start(f32[136,128]{1,0:T(8,128)S(1)} %add_add_fusion.mine_ref), channel_id=1, source_target_pairs={{0,1},{1,0},{2,3},{3,2},{4,5},{5,4},{6,7},{7,6},{8,9},{9,8},{10,11... | collective-permute-start | bytes 208904 | tf_op jit(solution)/shard_map/ppermute | solution.py:21

commit v5 on v4

--- a/solution.py
+++ b/solution.py
@@ -11,7 +11,7 @@
 
 RANK = 1024
 LANES = 128
-BLOCK = 64
+BLOCK = 32
 STEP = 16
 SUB = 8
 
@@ -49,22 +49,29 @@
     return lax.dot_general(left, right, (((0,), (0,)), ((), ())), preferred_element_type=jnp.float32)
 
 
-def slab_copies(place_ref, whole_ref, into_refs, sem_ref, first, by_rows):
+def slab_copies(whole_ref, into_refs, sem_ref, first, by_rows):
     copies = []
     for index, into_ref in enumerate(into_refs):
         size = into_ref.shape[0 if by_rows else 1]
-        start = pl.multiple_of((place_ref[0] ^ (first + index)) * size, size)
+        start = pl.multiple_of((lax.axis_index("cols") ^ (first + index)) * size, size)
         span = whole_ref.at[pl.ds(start, size), :] if by_rows else whole_ref.at[:, pl.ds(start, size)]
         copies.append(pltpu.make_async_copy(span, into_ref, sem_ref.at[index]))
     return copies
 
 
-def project_kernel(place_ref, basis_ref, snaps_ref, *refs):
+def quad_index(first, second):
+    column = lax.axis_index("cols")
+    flat = lax.axis_index("rows") * lax.axis_size("cols") + column
+    low, high = (flat // jnp.where(column % 2 == 0, *masks) % 2 for masks in (first, second))
+    return (low + 2 * high).astype(jnp.int32)
+
+
+def project_kernel(first, second, basis_ref, snaps_ref, *refs):
     count = (len(refs) - 7) // 2
     piece_refs, slab_refs = refs[:4], (refs[3 + count],) + refs[4 : 3 + count]
     part_refs, total_ref, basis_sem, snaps_sem = refs[4 + count : 4 + 2 * count], refs[-3], refs[-2], refs[-1]
-    basis_copies = slab_copies(place_ref, basis_ref, slab_refs, basis_sem, 0, True)
-    snaps_copies = slab_copies(place_ref, snaps_ref, part_refs, snaps_sem, 0, False)
+    basis_copies = slab_copies(basis_ref, slab_refs, basis_sem, 0, True)
+    snaps_copies = slab_copies(snaps_ref, part_refs, snaps_sem, 0, False)
     for pair in zip(basis_copies, snaps_copies):
         for copy in pair:
             copy.start()
@@ -76,15 +83,16 @@
         total = value if total is None else total + value
     total_ref[...] = total
     rows = piece_refs[0].shape[0]
+    quad = quad_index(first, second)
     for offset, piece_ref in enumerate(piece_refs):
-        start = pl.multiple_of((place_ref[1] ^ offset) * rows, rows)
+        start = pl.multiple_of((quad ^ offset) * rows, rows)
         piece_ref[...] = total_ref[pl.ds(start, rows), :]
 
 
-def recon_kernel(place_ref, basis_ref, snaps_ref, low_ref, near_low_ref, near_ref, base_ref, coefficients_ref, *scratch):
+def recon_kernel(basis_ref, snaps_ref, low_ref, near_low_ref, near_ref, base_ref, coefficients_ref, *scratch):
     own_ref, span_ref, basis_sem, snaps_sem = scratch
-    (basis_copy,) = slab_copies(place_ref, basis_ref, (own_ref,), basis_sem, 0, True)
-    (snaps_copy,) = slab_copies(place_ref, snaps_ref, (span_ref,), snaps_sem, 0, False)
+    (basis_copy,) = slab_copies(basis_ref, (own_ref,), basis_sem, 0, True)
+    (snaps_copy,) = slab_copies(snaps_ref, (span_ref,), snaps_sem, 0, False)
     basis_copy.start()
     snaps_copy.start()
     coefficients_ref[...] = low_ref[...].astype(jnp.float32).T
@@ -117,7 +125,7 @@
     return lax.broadcasted_iota(jnp.int32, (LANES, LANES), dim)
 
 
-def residual_kernel(total_points, place_ref, *refs):
+def residual_kernel(total_points, *refs):
     count = (len(refs) - 6) // 2
     low_refs, basis_refs = refs[:count], refs[count : 2 * count]
     base_ref, high_ref, rest_ref, keep_ref, send_ref, pack_ref = refs[2 * count :]
@@ -133,11 +141,11 @@
         rest_ref[:, cols] = rest
     scale = 1.0 / total_points
 
+    high, rest = high_ref[...], rest_ref[...]
+    gram = (nt_dot(high, high) + (nt_dot(high, rest) + nt_dot(rest, high))) * scale
+
     def block(row, col):
-        rows, cols = pl.ds(row * LANES, LANES), pl.ds(col * LANES, LANES)
-        value = nt_dot(high_ref[rows, :], high_ref[cols, :])
-        value += nt_dot(high_ref[rows, :], rest_ref[cols, :]) + nt_dot(rest_ref[rows, :], high_ref[cols, :])
-        return value * scale
+        return gram[row * LANES : (row + 1) * LANES, col * LANES : (col + 1) * LANES]
 
     pairs, blocks = pack_layout(snaps // LANES)
     down, across = square_iota(0), square_iota(1)
@@ -149,7 +157,7 @@
     for row, col, at in blocks:
         pack_ref[pl.ds(at, LANES), :] = block(row, col)
     half = pack_ref.shape[0] // 2
-    odd = place_ref[0] % 2 == 1
+    odd = lax.axis_index("cols") % 2 == 1
     first, second = pack_ref[pl.ds(0, half), :], pack_ref[pl.ds(half, half), :]
     keep_ref[...] = jnp.where(odd, second, first)
     send_ref[...] = jnp.where(odd, first, second)
@@ -179,26 +187,27 @@
             pivot = row_of(column[home], line)
             inverse = 1.0 / pivot
             scales[home] = jnp.where(sub_iota == line, lax.rsqrt(pivot), scales[home])
-            factors = {}
-            for g in range(home, groups):
-                value = column[g] * inverse
-                if g == home:
-                    if line == SUB - 1:
-                        continue
-                    value = jnp.where(sub_iota > line, value, 0.0)
-                factors[g] = value
-            for lanes in columns[p - begin + 1 :] + panel:
-                lead = row_of(lanes[home], line)
-                for g, value in factors.items():
-                    lanes[g] = lanes[g] - value * lead
+            below = list(column)
+            below[home] = jnp.where(sub_iota > line, column[home], 0.0)
+            last = home + 1 if line == SUB - 1 else home
+            for j in range(p + 1, begin + STEP):
+                lanes, first = columns[j - begin], j // SUB
+                lead = row_of(column[first], j % SUB) * inverse
+                for g in range(max(first, last), groups):
+                    lanes[g] = lanes[g] - below[g] * lead
+            for lanes in panel:
+                lead = row_of(lanes[home], line) * inverse
+                for g in range(last, groups):
+                    lanes[g] = lanes[g] - below[g] * lead
     return [[tile * scale for tile, scale in zip(lanes, scales)] for lanes in panel]
 
 
-def factor_kernel(place_ref, mine_ref, other_ref, high_ref, rest_ref, factor_ref, out_ref, a_ref, w_ref, pack_ref):
+def factor_kernel(mine_ref, other_ref, high_ref, rest_ref, factor_out_ref, directions_ref, *scratch):
+    factor_ref, out_ref, a_ref, w_ref, pack_ref, factor_sem, out_sem = scratch
     size = factor_ref.shape[0]
     tiles = size // LANES
     half = mine_ref.shape[0]
-    odd = place_ref[0] % 2 == 1
+    odd = lax.axis_index("cols") % 2 == 1
     pack_ref[pl.ds(0, half), :] = jnp.where(odd, other_ref[...], mine_ref[...])
     pack_ref[pl.ds(half, half), :] = jnp.where(odd, mine_ref[...], other_ref[...])
     pairs, blocks = pack_layout(tiles)
@@ -220,6 +229,49 @@
     cols_iota = lax.broadcasted_iota(jnp.int32, (size, size), 1)
     w_ref[...] = jnp.where(rows_iota == cols_iota, 1.0, 0.0)
 
+    def row_copies(row):
+        rows = pl.ds(row * LANES, LANES)
+        return (
+            pltpu.make_async_copy(factor_ref.at[rows, :], factor_out_ref.at[rows, :], factor_sem.at[row]),
+            pltpu.make_async_copy(out_ref.at[rows, :], directions_ref.at[rows, :], out_sem.at[row]),
+        )
+
+    def update_rest(places, panel, a_tiles, after):
+        parts = [wide_split(value) for value in panel]
+        left = [jnp.concatenate([a, a, b], axis=0) for a, b in parts[: len(a_tiles)]]
+        right = [jnp.concatenate([a, b, a], axis=0) for a, b in parts]
+        for row_tile in a_tiles:
+            skip = max(after - row_tile * LANES, 0)
+            if skip == LANES:
+                continue
+            rows = pl.ds(row_tile * LANES + skip, LANES - skip)
+            for (ref, t), value in zip(places, right):
+                if ref is a_ref and t < row_tile:
+                    continue
+                update = tn_dot(left[row_tile - a_tiles[0]], value)
+                lanes = pl.ds(t * LANES, LANES)
+                ref[rows, lanes] = ref[rows, lanes] - update[skip:, :]
+
+    def emit(row):
+        rows = pl.ds(row * LANES, LANES)
+        for col in range(tiles):
+            into = (rows, pl.ds(col * LANES, LANES))
+            if row < col:
+                factor_ref[into] = jnp.zeros((LANES, LANES), jnp.float32)
+                continue
+            block = a_ref[pl.ds(col * LANES, LANES), rows].T
+            factor_ref[into] = jnp.where(down >= across, block, 0.0) if row == col else block
+        depth, chunk = (row + 1) * LANES, 256
+        high, rest = wide_split(w_ref[rows, pl.ds(0, depth)])
+        for start in range(0, out_ref.shape[1], chunk):
+            cols = pl.ds(start, chunk)
+            right_high, right_rest = high_ref[pl.ds(0, depth), cols], rest_ref[pl.ds(0, depth), cols]
+            value = jnp.dot(high, right_high, preferred_element_type=jnp.float32)
+            value += jnp.dot(high, right_rest, preferred_element_type=jnp.float32)
+            value += jnp.dot(rest, right_high, preferred_element_type=jnp.float32)
+            out_ref[rows, cols] = value.astype(jnp.bfloat16)
+
+    done_tiles, started = [], 0
     for base in range(0, size, BLOCK):
         tile, offset = divmod(base, LANES)
         a_tiles, w_tiles = range(tile, tiles), range(tile + 1)
@@ -231,63 +283,38 @@
         for (ref, t), value in zip(places, panel):
             ref[pl.ds(base, BLOCK), pl.ds(t * LANES, LANES)] = value
         after = base + BLOCK
-        if after == size:
-            break
-        parts = [wide_split(value) for value in panel]
-        left = [jnp.concatenate([a, a, b], axis=0) for a, b in parts[: len(a_tiles)]]
-        right = [jnp.concatenate([a, b, a], axis=0) for a, b in parts]
-        for row_tile in a_tiles:
-            skip = after - row_tile * LANES if after > row_tile * LANES else 0
-            if skip == LANES:
-                continue
-            rows = pl.ds(row_tile * LANES + skip, LANES - skip)
-            for (ref, t), value in zip(places, right):
-                if ref is a_ref and t < row_tile:
-                    continue
-                update = tn_dot(left[row_tile - tile], value)
-                lanes = pl.ds(t * LANES, LANES)
-                ref[rows, lanes] = ref[rows, lanes] - update[skip:, :]
-
-    lower = rows_iota[:LANES, :LANES] >= cols_iota[:LANES, :LANES]
-    for row in range(tiles):
-        for col in range(tiles):
-            into = (pl.ds(row * LANES, LANES), pl.ds(col * LANES, LANES))
-            if row < col:
-                factor_ref[into] = jnp.zeros((LANES, LANES), jnp.float32)
-                continue
-            block = a_ref[pl.ds(col * LANES, LANES), pl.ds(row * LANES, LANES)].T
-            factor_ref[into] = jnp.where(lower, block, 0.0) if row == col else block
-    chunk = 256
-    for row in range(tiles):
-        depth = (row + 1) * LANES
-        rows = pl.ds(row * LANES, LANES)
-        high, rest = wide_split(w_ref[rows, pl.ds(0, depth)])
-        for start in range(0, out_ref.shape[1], chunk):
-            cols = pl.ds(start, chunk)
-            right_high, right_rest = high_ref[pl.ds(0, depth), cols], rest_ref[pl.ds(0, depth), cols]
-            value = jnp.dot(high, right_high, preferred_element_type=jnp.float32)
-            value += jnp.dot(high, right_rest, preferred_element_type=jnp.float32)
-            value += jnp.dot(rest, right_high, preferred_element_type=jnp.float32)
-            out_ref[rows, cols] = value.astype(jnp.bfloat16)
-
-
-def call(kernel, outs, scratch, flops, grant, whole=0):
+        update_rest(places, panel, a_tiles, after)
+        if started < len(done_tiles):
+            for copy in row_copies(done_tiles[started]):
+                copy.start()
+            started += 1
+        if after % LANES == 0:
+            emit(tile)
+            done_tiles.append(tile)
+    for row in done_tiles[started:]:
+        for copy in row_copies(row):
+            copy.start()
+    for row in done_tiles:
+        for copy in row_copies(row):
+            copy.wait()
+
+
+def call(kernel, outs, scratch, flops, grant, whole=0, stay=False):
     vmem = pl.BlockSpec(memory_space=pltpu.VMEM)
-    smem = pl.BlockSpec(memory_space=pltpu.SMEM)
     hbm = pl.BlockSpec(memory_space=pltpu.HBM)
 
-    def run(scalar, *args):
+    def run(*args):
         size = sum(math.prod(x.shape) * x.dtype.itemsize for x in (*args, *outs))
         args = [pltpu.with_memory_space_constraint(x, pltpu.HBM) for x in args[:whole]] + list(args[whole:])
         return pl.pallas_call(
             kernel,
             out_shape=outs,
-            in_specs=[smem] + [hbm] * whole + [vmem] * (len(args) - whole),
-            out_specs=[vmem] * len(outs),
+            in_specs=[hbm] * whole + [vmem] * (len(args) - whole),
+            out_specs=[hbm if stay else vmem] * len(outs),
             scratch_shapes=scratch,
             compiler_params=pltpu.CompilerParams(vmem_limit_bytes=grant << 20),
             cost_estimate=pl.CostEstimate(flops=flops, bytes_accessed=size, transcendentals=0),
-        )(scalar, *args)
+        )(*args)
 
     return run
 
@@ -299,7 +326,6 @@
 def compute(basis_cols, snapshots):
     snaps, row_points = snapshots.shape
     modes = basis_cols.shape[1]
-    row_index, column_index = lax.axis_index("rows"), lax.axis_index("cols")
     row_count, columns = lax.axis_size("rows"), lax.axis_size("cols")
     total_points = row_points * row_count
     points = row_points // columns
@@ -310,23 +336,19 @@
     orders = list(zip(row_bits, row_bits[1:] + row_bits[:1]))
     first, second = orders[0], orders[1]
     both = tuple(a ^ b for a, b in zip(first, second))
-    flat = row_index * columns + column_index
-    even = column_index % 2 == 0
-    low_bit, high_bit = ((flat // jnp.where(even, *masks)) % 2 for masks in (first, second))
-    quad = (low_bit + 2 * high_bit).astype(jnp.int32)
-    place = jnp.stack([column_index.astype(jnp.int32), quad])
+    quad = quad_index(first, second)
 
     slab, piece = shape(bf16, points, modes), shape(f32, quarter, modes)
     slab_scratch, span_scratch = pltpu.VMEM((points, modes), bf16), pltpu.VMEM((snaps, points), bf16)
     semaphores = pltpu.SemaphoreType.DMA((columns,))
     kept, one, two, three, *slabs = call(
-        project_kernel,
+        functools.partial(project_kernel, first, second),
         (piece,) * 4 + (slab,) * (columns - 1),
         [slab_scratch] + [span_scratch] * columns + [pltpu.VMEM((snaps, modes), f32), semaphores, semaphores],
         2 * snaps * row_points * modes,
         12,
         2,
-    )(place, basis_cols, snapshots)
+    )(basis_cols, snapshots)
     arrived_slabs = [swap(slabs[offset - 1], (offset,) * 2) for offset in range(2, columns)]
     one, two, three = swap(one, first), swap(two, second), swap(three, both)
     near_slab = swap(slabs[0], (1, 1))
@@ -349,7 +371,7 @@
         4 * snaps * points * modes,
         8,
         2,
-    )(place, basis_cols, snapshots, lows[0], lows[1], near_slab)
+    )(basis_cols, snapshots, lows[0], lows[1], near_slab)
     packed = packed_rows(snaps // LANES)
     part = shape(f32, packed // 2, LANES)
     wide = shape(bf16, snaps, points)
@@ -359,7 +381,7 @@
         [pltpu.VMEM((packed, LANES), f32)],
         2 * snaps * points * (modes * (columns - 2) + 3 * snaps),
         16,
-    )(place, *[lows[offset] for offset in range(2, columns)], *arrived_slabs, begun)
+    )(*[lows[offset] for offset in range(2, columns)], *arrived_slabs, begun)
     keep = keep + swap(send, (1, 1))
     for masks in zip(*exchange_rounds(bits(columns // 2, 2) + row_bits)):
         if masks[0][1] == 0:
@@ -372,10 +394,14 @@
     factor, directions = call(
         factor_kernel,
         (shape(f32, snaps, snaps), wide),
-        [pltpu.VMEM((snaps, snaps), f32)] * 2 + [pltpu.VMEM((packed, LANES), f32)],
+        [pltpu.VMEM((snaps, snaps), f32), span_scratch]
+        + [pltpu.VMEM((snaps, snaps), f32)] * 2
+        + [pltpu.VMEM((packed, LANES), f32)]
+        + [pltpu.SemaphoreType.DMA((snaps // LANES,))] * 2,
         6 * snaps * snaps * points,
         16,
-    )(place, keep, rest_of_gram, high, rest)
+        stay=True,
+    )(keep, rest_of_gram, high, rest)
     return (coefficients, factor, directions)
 
 

time: 84.3 us -> 81.2 us (0.963)
  Pallas kernels: 17.1 us -> 14.1 us
    pallas_call x4, Pallas kernels: 17.1 us -> 14.1 us  [run(): pl.pallas_call(kernel, out_shape=outs, in_specs=[hbm] * whole + [vmem] *...]
where the time goes in v5:
time: 81.2 us; the launch traced here: 81.1 us
  waiting for transfers between devices  43.2 us (53%)
  starting transfers between devices  22.9 us (28%)
  Pallas kernels  14.1 us (17%)
    ppermute x21, waiting for transfers between devices, swap(): lax.ppermute(value, ('rows', 'cols'), [(i, i ^ masks[i % 2]) for i in ran...  43.2 us
    ppermute x21, starting transfers between devices, swap(): lax.ppermute(value, ('rows', 'cols'), [(i, i ^ masks[i % 2]) for i in ran...  22.9 us
    pallas_call x4, Pallas kernels, run(): pl.pallas_call(kernel, out_shape=outs, in_specs=[hbm] * whole + [vmem] *...  14.1 us
  transfers between devices with their start and end apart: 21, of which 12 were waited for; matrix products, arithmetic and copies ran while one was open for 0% of the time, Pallas kernels for 3%

profile of v5, /device:TPU:0, one launch (start us, length us, event | category | flops | bytes accessed | tf_op | source)
XLA Modules:
  0.0 81.1 jit_solution(8627932619135463099)
XLA Ops:
  0.6 3.0 %shard_map.49 = (f32[64,256]{1,0:T(8,128)S(1)}, f32[64,256]{1,0:T(8,128)S(1)}, f32[64,256]{1,0:T(8,128)S(1)}, f32[64,256]{1,0:T(8,128)S(1)}, bf16[1024,256]{1,0:...) custom-call(bf16[4096,256]{1,0:T(8,128)(2,1)} %basis_ref.3, bf16[256,4096]{1,0:T(8,128)(2,1)} %snaps_ref.3), custom_call_target="tpu_custom_call" | custom-call | flops 536870912 | bytes 6029312 | tf_op jit(solution)/shard_map/pallas_call | solution.py:309
  3.7 3.1 %collective-permute-start = (f32[64,256]{1,0:T(8,128)S(1)}, f32[64,256]{1,0:T(8,128)S(1)}, u32[]{:S(2)}, u32[]{:S(2)}) collective-permute-start(f32[64,256]{1,0:T(8,128)S(1)} %get-tuple-element.19), channel_id=1, source_target_pairs={{0,4},{1,9},{2,6},{3,11},{4,0},{5,13},{6,2},{7,15},{8,12},{9,1},{1... | collective-permute-start | bytes 196616 | tf_op jit(solution)/shard_map/ppermute | solution.py:21
  6.7 1.6 %collective-permute-start.1 = (f32[64,256]{1,0:T(8,128)S(1)}, f32[64,256]{1,0:T(8,128)S(1)}, u32[]{:S(2)}, u32[]{:S(2)}) collective-permute-start(f32[64,256]{1,0:T(8,128)S(1)} %get-tuple-element.20), channel_id=1, source_target_pairs={{0,8},{1,17},{2,10},{3,19},{4,12},{5,21},{6,14},{7,23},{8,0},{9,25... | collective-permute-start | bytes 196616 | tf_op jit(solution)/shard_map/ppermute | solution.py:21
  8.3 0.7 collective-permute-done
  9.0 2.2 %collective-permute-done.1 = f32[64,256]{1,0:T(8,128)S(1)} collective-permute-done((f32[64,256]{1,0:T(8,128)S(1)}, f32[64,256]{1,0:T(8,128)S(1)}, u32[]{:S(2)}, u32[]{:S(2)}) %collective-permute-start.1) | collective-permute-done | bytes 65568 | tf_op jit(solution)/shard_map/ppermute | solution.py:21
  11.2 2.3 %collective-permute-done.2 = f32[64,256]{1,0:T(8,128)S(1)} collective-permute-done((f32[64,256]{1,0:T(8,128)S(1)}, f32[64,256]{1,0:T(8,128)S(1)}, u32[]{:S(2)}, u32[]{:S(2)}) %collective-permute-start.2) | collective-permute-done | bytes 65568 | tf_op jit(solution)/shard_map/ppermute | solution.py:21
  13.5 2.7 %collective-permute-start.3 = (f32[64,256]{1,0:T(8,128)S(1)}, f32[64,256]{1,0:T(8,128)S(1)}, u32[]{:S(2)}, u32[]{:S(2)}) collective-permute-start(f32[64,256]{1,0:T(8,128)S(1)} %add_add_fusion.2), channel_id=1, source_target_pairs={{0,16},{1,5},{2,18},{3,7},{4,20},{5,1},{6,22},{7,3},{8,24},{9,13},... | collective-permute-start | bytes 196616 | tf_op jit(solution)/shard_map/ppermute | solution.py:21
  16.1 3.5 %collective-permute-done.3 = f32[64,256]{1,0:T(8,128)S(1)} collective-permute-done((f32[64,256]{1,0:T(8,128)S(1)}, f32[64,256]{1,0:T(8,128)S(1)}, u32[]{:S(2)}, u32[]{:S(2)}) %collective-permute-start.3) | collective-permute-done | bytes 65568 | tf_op jit(solution)/shard_map/ppermute | solution.py:21
  19.7 0.9 %collective-permute-start.6 = (bf16[64,256]{1,0:T(8,128)(2,1)S(1)}, bf16[64,256]{1,0:T(8,128)(2,1)S(1)}, u32[]{:S(2)}, u32[]{:S(2)}) collective-permute-start(bf16[64,256]{1,0:T(8,128)(2,1)S(1)} %multiply_convert_fusion), channel_id=1, source_target_pairs={{0,12},{1,25},{2,14},{3,27},{4,8},{5,29},{6,10},{7,31},{8,4},{9,17... | collective-permute-start | bytes 98312 | tf_op jit(solution)/shard_map/ppermute | solution.py:21
  20.6 0.2 collective-permute-start.5
  20.8 2.5 %collective-permute-start.4 = (bf16[64,256]{1,0:T(8,128)(2,1)S(1)}, bf16[64,256]{1,0:T(8,128)(2,1)S(1)}, u32[]{:S(2)}, u32[]{:S(2)}) collective-permute-start(bf16[64,256]{1,0:T(8,128)(2,1)S(1)} %multiply_convert_fusion), channel_id=1, source_target_pairs={{0,4},{1,9},{2,6},{3,11},{4,0},{5,13},{6,2},{7,15},{8,12},{9,1},{1... | collective-permute-start | bytes 98312 | tf_op jit(solution)/shard_map/ppermute | solution.py:21
  23.3 1.5 %collective-permute-start.11 = (bf16[1024,256]{1,0:T(8,128)(2,1)S(1)}, bf16[1024,256]{1,0:T(8,128)(2,1)S(1)}, u32[]{:S(2)}, u32[]{:S(2)}) collective-permute-start(bf16[1024,256]{1,0:T(8,128)(2,1)S(1)} %get-tuple-element.24), channel_id=1, source_target_pairs={{0,2},{1,3},{2,0},{3,1},{4,6},{5,7},{6,4},{7,5},{8,10},{9,11},{10,... | collective-permute-start | bytes 1572872 | tf_op jit(solution)/shard_map/ppermute | solution.py:21
  24.8 0.4 collective-permute-start.12
  25.2 1.6 %collective-permute-start.9 = (bf16[256,256]{1,0:T(8,128)(2,1)S(1)}, bf16[256,256]{1,0:T(8,128)(2,1)S(1)}, u32[]{:S(2)}, u32[]{:S(2)}) collective-permute-start(bf16[256,256]{1,0:T(8,128)(2,1)S(1)} %pad_maximum_fusion.low_ref), channel_id=1, source_target_pairs={{0,2},{1,3},{2,0},{3,1},{4,6},{5,7},{6,4},{7,5},{8,10},{9,11},{10,... | collective-permute-start | bytes 393224 | tf_op jit(solution)/shard_map/ppermute | solution.py:21
  26.8 24.9 %collective-permute-done.9.refs_0_ = bf16[256,256]{1,0:T(8,128)(2,1)S(1)} collective-permute-done((bf16[256,256]{1,0:T(8,128)(2,1)S(1)}, bf16[256,256]{1,0:T(8,128)(2,1)S(1)}, u32[]{:S(2)}, u32[]{:S(2)}) %collective-permute-start.9) | collective-permute-done | bytes 131104 | tf_op jit(solution)/shard_map/ppermute | solution.py:21
  51.7 2.3 %shard_map.50 = (f32[256,1024]{1,0:T(8,128)S(1)}, f32[256,256]{1,0:T(8,128)}) custom-call(bf16[4096,256]{1,0:T(8,128)(2,1)} %basis_ref.3, bf16[256,4096]{1,0:T(8,128)(2,1)} %snaps_ref.3, bf16[256,256]{1,0:T(8,128)(2,1)S(1)} %pad_maximum_fusion.low_ref, bf16[256,256]{1,0:T(8,128)(2,1)S(1)} %collective-permute-done.7.near_low_ref, ...), custom_call_target="tpu_custom_call" | custom-call | flops 268435456 | bytes 6291456 | tf_op jit(solution)/shard_map/pallas_call | solution.py:309
  54.0 1.5 %shard_map.51 = (bf16[256,1024]{1,0:T(8,128)(2,1)S(1)}, bf16[256,1024]{1,0:T(8,128)(2,1)S(1)}, f32[136,128]{1,0:T(8,128)S(1)}, f32[136,128]{1,0:T(8,128)S(1)}) custom-call(bf16[256,256]{1,0:T(8,128)(2,1)S(1)} %collective-permute-done.9.refs_0_, bf16[256,256]{1,0:T(8,128)(2,1)S(1)} %collective-permute-done.10.refs_1_, ...), custom_call_target="tpu_custom_call" | custom-call | flops 671088640 | bytes 3547136 | tf_op jit(solution)/shard_map/pallas_call | solution.py:309
  55.5 0.6 collective-permute-start.13
  56.1 0.9 %collective-permute-done.13 = f32[136,128]{1,0:T(8,128)S(1)} collective-permute-done((f32[136,128]{1,0:T(8,128)S(1)}, f32[136,128]{1,0:T(8,128)S(1)}, u32[]{:S(2)}, u32[]{:S(2)}) %collective-permute-start.13) | collective-permute-done | bytes 69664 | tf_op jit(solution)/shard_map/ppermute | solution.py:21
  57.0 1.0 %collective-permute-start.16 = (f32[136,128]{1,0:T(8,128)S(1)}, f32[136,128]{1,0:T(8,128)S(1)}, u32[]{:S(2)}, u32[]{:S(2)}) collective-permute-start(f32[136,128]{1,0:T(8,128)S(1)} %add.61), channel_id=1, source_target_pairs={{0,6},{1,25},{2,4},{3,27},{4,2},{5,29},{6,0},{7,31},{8,14},{9,17},... | collective-permute-start | bytes 208904 | tf_op jit(solution)/shard_map/ppermute | solution.py:21
  58.0 2.0 %collective-permute-start.15 = (f32[136,128]{1,0:T(8,128)S(1)}, f32[136,128]{1,0:T(8,128)S(1)}, u32[]{:S(2)}, u32[]{:S(2)}) collective-permute-start(f32[136,128]{1,0:T(8,128)S(1)} %add.61), channel_id=1, source_target_pairs={{0,4},{1,17},{2,6},{3,19},{4,0},{5,21},{6,2},{7,23},{8,12},{9,25},... | collective-permute-start | bytes 208904 | tf_op jit(solution)/shard_map/ppermute | solution.py:21
  60.0 0.5 collective-permute-start.14
  60.5 1.8 %collective-permute-done.16 = f32[136,128]{1,0:T(8,128)S(1)} collective-permute-done((f32[136,128]{1,0:T(8,128)S(1)}, f32[136,128]{1,0:T(8,128)S(1)}, u32[]{:S(2)}, u32[]{:S(2)}) %collective-permute-start.16) | collective-permute-done | bytes 69664 | tf_op jit(solution)/shard_map/ppermute | solution.py:21
  62.3 0.7 collective-permute-done.15
  63.0 1.3 %collective-permute-done.14 = f32[136,128]{1,0:T(8,128)S(1)} collective-permute-done((f32[136,128]{1,0:T(8,128)S(1)}, f32[136,128]{1,0:T(8,128)S(1)}, u32[]{:S(2)}, u32[]{:S(2)}) %collective-permute-start.14) | collective-permute-done | bytes 69664 | tf_op jit(solution)/shard_map/ppermute | solution.py:21
  64.3 2.9 %collective-permute-start.19 = (f32[136,128]{1,0:T(8,128)S(1)}, f32[136,128]{1,0:T(8,128)S(1)}, u32[]{:S(2)}, u32[]{:S(2)}) collective-permute-start(f32[136,128]{1,0:T(8,128)S(1)} %add_add_fusion.1), channel_id=1, source_target_pairs={{0,24},{1,7},{2,26},{3,5},{4,28},{5,3},{6,30},{7,1},{8,16},{9,15},... | collective-permute-start | bytes 208904 | tf_op jit(solution)/shard_map/ppermute | solution.py:21
  67.2 1.6 %collective-permute-start.17 = (f32[136,128]{1,0:T(8,128)S(1)}, f32[136,128]{1,0:T(8,128)S(1)}, u32[]{:S(2)}, u32[]{:S(2)}) collective-permute-start(f32[136,128]{1,0:T(8,128)S(1)} %add_add_fusion.1), channel_id=1, source_target_pairs={{0,8},{1,3},{2,10},{3,1},{4,12},{5,7},{6,14},{7,5},{8,0},{9,11},{1... | collective-permute-start | bytes 208904 | tf_op jit(solution)/shard_map/ppermute | solution.py:21
  68.8 1.7 %collective-permute-done.19 = f32[136,128]{1,0:T(8,128)S(1)} collective-permute-done((f32[136,128]{1,0:T(8,128)S(1)}, f32[136,128]{1,0:T(8,128)S(1)}, u32[]{:S(2)}, u32[]{:S(2)}) %collective-permute-start.19) | collective-permute-done | bytes 69664 | tf_op jit(solution)/shard_map/ppermute | solution.py:21
  70.5 1.9 %collective-permute-done.18 = f32[136,128]{1,0:T(8,128)S(1)} collective-permute-done((f32[136,128]{1,0:T(8,128)S(1)}, f32[136,128]{1,0:T(8,128)S(1)}, u32[]{:S(2)}, u32[]{:S(2)}) %collective-permute-start.18) | collective-permute-done | bytes 69664 | tf_op jit(solution)/shard_map/ppermute | solution.py:21
  72.4 0.1 collective-permute-start.20
  72.5 1.2 %collective-permute-done.20.other_ref = f32[136,128]{1,0:T(8,128)S(1)} collective-permute-done((f32[136,128]{1,0:T(8,128)S(1)}, f32[136,128]{1,0:T(8,128)S(1)}, u32[]{:S(2)}, u32[]{:S(2)}) %collective-permute-start.20) | collective-permute-done | bytes 69664 | tf_op jit(solution)/shard_map/ppermute | solution.py:21
  73.7 7.3 %shard_map.52 = (f32[256,256]{1,0:T(8,128)}, bf16[256,1024]{1,0:T(8,128)(2,1)}) custom-call(f32[136,128]{1,0:T(8,128)S(1)} %add_add_fusion.mine_ref, f32[136,128]{1,0:T(8,128)S(1)} %collective-permute-done.20.other_ref, bf16[256,1024]{1,0:T(8,128)(2,1)S(1)} %get-tuple-element.29.high_ref, bf16[256,1024]{1,0:T(8,128)(2,1)S(1)} %get-tuple-element.30.rest_ref), custom_call_target="tpu_custom_call" | custom-call | flops 402653184 | bytes 1974272 | tf_op jit(solution)/shard_map/pallas_call | solution.py:309
  (21 shorter events, 0.2 us)
Async XLA Ops:
  3.7 5.3 %collective-permute-start = (f32[64,256]{1,0:T(8,128)S(1)}, f32[64,256]{1,0:T(8,128)S(1)}, u32[]{:S(2)}, u32[]{:S(2)}) collective-permute-start(f32[64,256]{1,0:T(8,128)S(1)} %get-tuple-element.19), channel_id=1, source_target_pairs={{0,4},{1,9},{2,6},{3,11},{4,0},{5,13},{6,2},{7,15},{8,12},{9,1},{1... | collective-permute-start | bytes 196616 | tf_op jit(solution)/shard_map/ppermute | solution.py:21
  6.7 4.4 %collective-permute-start.1 = (f32[64,256]{1,0:T(8,128)S(1)}, f32[64,256]{1,0:T(8,128)S(1)}, u32[]{:S(2)}, u32[]{:S(2)}) collective-permute-start(f32[64,256]{1,0:T(8,128)S(1)} %get-tuple-element.20), channel_id=1, source_target_pairs={{0,8},{1,17},{2,10},{3,19},{4,12},{5,21},{6,14},{7,23},{8,0},{9,25... | collective-permute-start | bytes 196616 | tf_op jit(solution)/shard_map/ppermute | solution.py:21
  8.3 5.2 %collective-permute-start.2 = (f32[64,256]{1,0:T(8,128)S(1)}, f32[64,256]{1,0:T(8,128)S(1)}, u32[]{:S(2)}, u32[]{:S(2)}) collective-permute-start(f32[64,256]{1,0:T(8,128)S(1)} %get-tuple-element.21), channel_id=1, source_target_pairs={{0,12},{1,25},{2,14},{3,27},{4,8},{5,29},{6,10},{7,31},{8,4},{9,17... | collective-permute-start | bytes 196616 | tf_op jit(solution)/shard_map/ppermute | solution.py:21
  13.5 6.2 %collective-permute-start.3 = (f32[64,256]{1,0:T(8,128)S(1)}, f32[64,256]{1,0:T(8,128)S(1)}, u32[]{:S(2)}, u32[]{:S(2)}) collective-permute-start(f32[64,256]{1,0:T(8,128)S(1)} %add_add_fusion.2), channel_id=1, source_target_pairs={{0,16},{1,5},{2,18},{3,7},{4,20},{5,1},{6,22},{7,3},{8,24},{9,13},... | collective-permute-start | bytes 196616 | tf_op jit(solution)/shard_map/ppermute | solution.py:21
  19.7 5.1 %collective-permute-start.6 = (bf16[64,256]{1,0:T(8,128)(2,1)S(1)}, bf16[64,256]{1,0:T(8,128)(2,1)S(1)}, u32[]{:S(2)}, u32[]{:S(2)}) collective-permute-start(bf16[64,256]{1,0:T(8,128)(2,1)S(1)} %multiply_convert_fusion), channel_id=1, source_target_pairs={{0,12},{1,25},{2,14},{3,27},{4,8},{5,29},{6,10},{7,31},{8,4},{9,17... | collective-permute-start | bytes 98312 | tf_op jit(solution)/shard_map/ppermute | solution.py:21
  20.6 4.6 %collective-permute-start.5 = (bf16[64,256]{1,0:T(8,128)(2,1)S(1)}, bf16[64,256]{1,0:T(8,128)(2,1)S(1)}, u32[]{:S(2)}, u32[]{:S(2)}) collective-permute-start(bf16[64,256]{1,0:T(8,128)(2,1)S(1)} %multiply_convert_fusion), channel_id=1, source_target_pairs={{0,8},{1,17},{2,10},{3,19},{4,12},{5,21},{6,14},{7,23},{8,0},{9,25... | collective-permute-start | bytes 98312 | tf_op jit(solution)/shard_map/ppermute | solution.py:21
  20.8 4.4 %collective-permute-start.4 = (bf16[64,256]{1,0:T(8,128)(2,1)S(1)}, bf16[64,256]{1,0:T(8,128)(2,1)S(1)}, u32[]{:S(2)}, u32[]{:S(2)}) collective-permute-start(bf16[64,256]{1,0:T(8,128)(2,1)S(1)} %multiply_convert_fusion), channel_id=1, source_target_pairs={{0,4},{1,9},{2,6},{3,11},{4,0},{5,13},{6,2},{7,15},{8,12},{9,1},{1... | collective-permute-start | bytes 98312 | tf_op jit(solution)/shard_map/ppermute | solution.py:21
  23.3 28.4 %collective-permute-start.8 = (bf16[1024,256]{1,0:T(8,128)(2,1)S(1)}, bf16[1024,256]{1,0:T(8,128)(2,1)S(1)}, u32[]{:S(2)}, u32[]{:S(2)}) collective-permute-start(bf16[1024,256]{1,0:T(8,128)(2,1)S(1)} %get-tuple-element.22), channel_id=1, source_target_pairs={{0,1},{1,0},{2,3},{3,2},{4,5},{5,4},{6,7},{7,6},{8,9},{9,8},{10,11... | collective-permute-start | bytes 1572872 | tf_op jit(solution)/shard_map/ppermute | solution.py:21
  23.3 30.7 %collective-permute-start.11 = (bf16[1024,256]{1,0:T(8,128)(2,1)S(1)}, bf16[1024,256]{1,0:T(8,128)(2,1)S(1)}, u32[]{:S(2)}, u32[]{:S(2)}) collective-permute-start(bf16[1024,256]{1,0:T(8,128)(2,1)S(1)} %get-tuple-element.24), channel_id=1, source_target_pairs={{0,2},{1,3},{2,0},{3,1},{4,6},{5,7},{6,4},{7,5},{8,10},{9,11},{10,... | collective-permute-start | bytes 1572872 | tf_op jit(solution)/shard_map/ppermute | solution.py:21
  24.8 29.2 %collective-permute-start.12 = (bf16[1024,256]{1,0:T(8,128)(2,1)S(1)}, bf16[1024,256]{1,0:T(8,128)(2,1)S(1)}, u32[]{:S(2)}, u32[]{:S(2)}) collective-permute-start(bf16[1024,256]{1,0:T(8,128)(2,1)S(1)} %get-tuple-element.25), channel_id=1, source_target_pairs={{0,3},{1,2},{2,1},{3,0},{4,7},{5,6},{6,5},{7,4},{8,11},{9,10},{10,... | collective-permute-start | bytes 1572872 | tf_op jit(solution)/shard_map/ppermute | solution.py:21
  25.2 26.4 %collective-permute-start.9 = (bf16[256,256]{1,0:T(8,128)(2,1)S(1)}, bf16[256,256]{1,0:T(8,128)(2,1)S(1)}, u32[]{:S(2)}, u32[]{:S(2)}) collective-permute-start(bf16[256,256]{1,0:T(8,128)(2,1)S(1)} %pad_maximum_fusion.low_ref), channel_id=1, source_target_pairs={{0,2},{1,3},{2,0},{3,1},{4,6},{5,7},{6,4},{7,5},{8,10},{9,11},{10,... | collective-permute-start | bytes 393224 | tf_op jit(solution)/shard_map/ppermute | solution.py:21
  26.7 24.9 %collective-permute-start.7 = (bf16[256,256]{1,0:T(8,128)(2,1)S(1)}, bf16[256,256]{1,0:T(8,128)(2,1)S(1)}, u32[]{:S(2)}, u32[]{:S(2)}) collective-permute-start(bf16[256,256]{1,0:T(8,128)(2,1)S(1)} %pad_maximum_fusion.low_ref), channel_id=1, source_target_pairs={{0,1},{1,0},{2,3},{3,2},{4,5},{5,4},{6,7},{7,6},{8,9},{9,8},{10,11... | collective-permute-start | bytes 393224 | tf_op jit(solution)/shard_map/ppermute | solution.py:21
  51.6 2.3 %collective-permute-start.10 = (bf16[256,256]{1,0:T(8,128)(2,1)S(1)}, bf16[256,256]{1,0:T(8,128)(2,1)S(1)}, u32[]{:S(2)}, u32[]{:S(2)}) collective-permute-start(bf16[256,256]{1,0:T(8,128)(2,1)S(1)} %collective-permute-done.9.refs_0_), channel_id=1, source_target_pairs={{0,1},{1,0},{2,3},{3,2},{4,5},{5,4},{6,7},{7,6},{8,9},{9,8},{10,11... | collective-permute-start | bytes 393224 | tf_op jit(solution)/shard_map/ppermute | solution.py:21
  55.5 1.5 %collective-permute-start.13 = (f32[136,128]{1,0:T(8,128)S(1)}, f32[136,128]{1,0:T(8,128)S(1)}, u32[]{:S(2)}, u32[]{:S(2)}) collective-permute-start(f32[136,128]{1,0:T(8,128)S(1)} %get-tuple-element.28), channel_id=1, source_target_pairs={{0,1},{1,0},{2,3},{3,2},{4,5},{5,4},{6,7},{7,6},{8,9},{9,8},{10,11... | collective-permute-start | bytes 208904 | tf_op jit(solution)/shard_map/ppermute | solution.py:21
  57.0 5.4 %collective-permute-start.16 = (f32[136,128]{1,0:T(8,128)S(1)}, f32[136,128]{1,0:T(8,128)S(1)}, u32[]{:S(2)}, u32[]{:S(2)}) collective-permute-start(f32[136,128]{1,0:T(8,128)S(1)} %add.61), channel_id=1, source_target_pairs={{0,6},{1,25},{2,4},{3,27},{4,2},{5,29},{6,0},{7,31},{8,14},{9,17},... | collective-permute-start | bytes 208904 | tf_op jit(solution)/shard_map/ppermute | solution.py:21
  58.0 5.0 %collective-permute-start.15 = (f32[136,128]{1,0:T(8,128)S(1)}, f32[136,128]{1,0:T(8,128)S(1)}, u32[]{:S(2)}, u32[]{:S(2)}) collective-permute-start(f32[136,128]{1,0:T(8,128)S(1)} %add.61), channel_id=1, source_target_pairs={{0,4},{1,17},{2,6},{3,19},{4,0},{5,21},{6,2},{7,23},{8,12},{9,25},... | collective-permute-start | bytes 208904 | tf_op jit(solution)/shard_map/ppermute | solution.py:21
  60.0 4.3 %collective-permute-start.14 = (f32[136,128]{1,0:T(8,128)S(1)}, f32[136,128]{1,0:T(8,128)S(1)}, u32[]{:S(2)}, u32[]{:S(2)}) collective-permute-start(f32[136,128]{1,0:T(8,128)S(1)} %add.61), channel_id=1, source_target_pairs={{0,2},{1,9},{2,0},{3,11},{4,6},{5,13},{6,4},{7,15},{8,10},{9,1},{1... | collective-permute-start | bytes 208904 | tf_op jit(solution)/shard_map/ppermute | solution.py:21
  64.3 6.2 %collective-permute-start.19 = (f32[136,128]{1,0:T(8,128)S(1)}, f32[136,128]{1,0:T(8,128)S(1)}, u32[]{:S(2)}, u32[]{:S(2)}) collective-permute-start(f32[136,128]{1,0:T(8,128)S(1)} %add_add_fusion.1), channel_id=1, source_target_pairs={{0,24},{1,7},{2,26},{3,5},{4,28},{5,3},{6,30},{7,1},{8,16},{9,15},... | collective-permute-start | bytes 208904 | tf_op jit(solution)/shard_map/ppermute | solution.py:21
  67.2 5.2 %collective-permute-start.18 = (f32[136,128]{1,0:T(8,128)S(1)}, f32[136,128]{1,0:T(8,128)S(1)}, u32[]{:S(2)}, u32[]{:S(2)}) collective-permute-start(f32[136,128]{1,0:T(8,128)S(1)} %add_add_fusion.1), channel_id=1, source_target_pairs={{0,16},{1,5},{2,18},{3,7},{4,20},{5,1},{6,22},{7,3},{8,24},{9,13},... | collective-permute-start | bytes 208904 | tf_op jit(solution)/shard_map/ppermute | solution.py:21
  67.2 5.2 %collective-permute-start.17 = (f32[136,128]{1,0:T(8,128)S(1)}, f32[136,128]{1,0:T(8,128)S(1)}, u32[]{:S(2)}, u32[]{:S(2)}) collective-permute-start(f32[136,128]{1,0:T(8,128)S(1)} %add_add_fusion.1), channel_id=1, source_target_pairs={{0,8},{1,3},{2,10},{3,1},{4,12},{5,7},{6,14},{7,5},{8,0},{9,11},{1... | collective-permute-start | bytes 208904 | tf_op jit(solution)/shard_map/ppermute | solution.py:21
  72.4 1.3 %collective-permute-start.20 = (f32[136,128]{1,0:T(8,128)S(1)}, f32[136,128]{1,0:T(8,128)S(1)}, u32[]{:S(2)}, u32[]{:S(2)}) collective-permute-start(f32[136,128]{1,0:T(8,128)S(1)} %add_add_fusion.mine_ref), channel_id=1, source_target_pairs={{0,1},{1,0},{2,3},{3,2},{4,5},{5,4},{6,7},{7,6},{8,9},{9,8},{10,11... | collective-permute-start | bytes 208904 | tf_op jit(solution)/shard_map/ppermute | solution.py:21
